TPU v7x, 32 devices: a whole 2x2x4 slice. The times are simulated.
32 devices in a mesh: row: 8 (over z, core), col: 4 (over y, x).
Axes of the slice: x: 2, y: 2, z: 4, core: 2. Of those that a mesh axis runs over, the one named last changes fastest.
Arguments:
- layer_input: bfloat16 [1024, 8192], P('col', 'row'), may hold values from -6 to 6
- clip_lengths: int32 [8], P('row'), may hold values from 768 to 1024, as said below
- first_gain: float32 [1024], P('col'), may hold values from 0.5 to 1.5
- first_up: bfloat16 [1024, 4096], P('row', 'col'), may hold values from -0.1875 to 0.1875
- first_down: bfloat16 [4096, 1024], P('col', 'row'), may hold values from -0.09375 to 0.09375
- attend_gain: float32 [1024], P('col'), may hold values from 0.5 to 1.5
- query_weight: bfloat16 [1024, 1024], P('row', 'col'), may hold values from -0.1875 to 0.1875
- key_weight: bfloat16 [1024, 1024], P('row', 'col'), may hold values from -0.1875 to 0.1875
- value_weight: bfloat16 [1024, 1024], P('row', 'col'), may hold values from -0.1875 to 0.1875
- output_weight: bfloat16 [1024, 1024], P('col', 'row'), may hold values from -0.75 to 0.75
- distance_table: bfloat16 [73, 64], replicated, may hold values from -6 to 6
- conv_gain: float32 [1024], P('col'), may hold values from 0.5 to 1.5
- pointwise_value: bfloat16 [1024, 1024], P('row', 'col'), may hold values from -0.1875 to 0.1875
- pointwise_gate: bfloat16 [1024, 1024], P('row', 'col'), may hold values from -0.1875 to 0.1875
- depthwise_kernel: bfloat16 [31, 1024], P(None, 'col'), may hold values from -1 to 1
- depthwise_gain: float32 [1024], P('col'), may hold values from 0.5 to 1.5
- pointwise_out: bfloat16 [1024, 1024], P('col', 'row'), may hold values from -0.1875 to 0.1875
- second_gain: float32 [1024], P('col'), may hold values from 0.5 to 1.5
- second_up: bfloat16 [1024, 4096], P('row', 'col'), may hold values from -0.1875 to 0.1875
- second_down: bfloat16 [4096, 1024], P('col', 'row'), may hold values from -0.09375 to 0.09375
- final_gain: float32 [1024], P('col'), may hold values from 0.5 to 1.5
- output_cotangent: bfloat16 [1024, 8192], P('col', 'row'), may hold values from -6 to 6
Outputs:
- layer_output: bfloat16 [1024, 8192], P('col', 'row')
- input_grad: float32 [1024, 8192], P('col', 'row')
- first_gain_grad: float32 [1024], P('col')
- first_up_grad: float32 [1024, 4096], P('row', 'col')
- first_down_grad: float32 [4096, 1024], P('col', 'row')
- attend_gain_grad: float32 [1024], P('col')
- query_weight_grad: float32 [1024, 1024], P('row', 'col')
- key_weight_grad: float32 [1024, 1024], P('row', 'col')
- value_weight_grad: float32 [1024, 1024], P('row', 'col')
- output_weight_grad: float32 [1024, 1024], P('col', 'row')
- distance_table_grad: float32 [73, 64], replicated
- conv_gain_grad: float32 [1024], P('col')
- pointwise_value_grad: float32 [1024, 1024], P('row', 'col')
- pointwise_gate_grad: float32 [1024, 1024], P('row', 'col')
- depthwise_kernel_grad: float32 [31, 1024], P(None, 'col')
- depthwise_gain_grad: float32 [1024], P('col')
- pointwise_out_grad: float32 [1024, 1024], P('col', 'row')
- second_gain_grad: float32 [1024], P('col')
- second_up_grad: float32 [1024, 4096], P('row', 'col')
- second_down_grad: float32 [4096, 1024], P('col', 'row')
- final_gain_grad: float32 [1024], P('col')
- masked_rms: float32 [8], replicated
Inputs may be any that keep to these rules, and one draw needn't show every extreme that they name: Each clip's valid tokens are its first clip_lengths slots; the rest of its 1024 slots are padding. Some clip is full in every draw.
All inputs are finite; a program needn't handle non-finite values.
Results may differ from a plain program's by a relative error of at most 0.015.
Values may be sent and summed in bfloat16 or wider, within the bound.
A program may use at most 192 MiB of HBM per device.

v0:
```python
import math

import jax
import jax.numpy as jnp
from jax import lax
from jax.sharding import PartitionSpec as P

HEAD_DIM = 64
LEFT = 64
RIGHT = 8
CLIP_TOKEN_SLOTS = 1024


EPSILON = 1e-05
NEG_FILL = -1e30
HIGH_ACCURACY = lax.Precision.HIGHEST


def matmul(left, right):
    return jnp.dot(left, right, preferred_element_type=jnp.float32)


def matmul_nt(left, right):
    return lax.dot_general(
        left, right, (((1,), (1,)), ((), ())), preferred_element_type=jnp.float32
    )


def matmul_tn(left, right):
    return lax.dot_general(
        left, right, (((0,), (0,)), ((), ())), preferred_element_type=jnp.float32
    )


def norm_forward(hidden):
    full_width = hidden.shape[1] * lax.axis_size("col")
    totals = lax.psum((jnp.sum(hidden, axis=1), jnp.sum(hidden * hidden, axis=1)), "col")
    average = totals[0] / full_width
    second = totals[1] / full_width - average * average
    inverse_dev = lax.rsqrt(second + EPSILON)
    return ((hidden - average[:, None]) * inverse_dev[:, None], inverse_dev)


def norm_backward(grad_in, normed, inverse_dev, gains):
    full_width = grad_in.shape[1] * lax.axis_size("col")
    scaled = grad_in * gains
    totals = lax.psum((jnp.sum(scaled, axis=1), jnp.sum(scaled * normed, axis=1)), "col")
    result = inverse_dev[:, None] * (
        scaled - totals[0][:, None] / full_width - normed * (totals[1][:, None] / full_width)
    )
    return (result, jnp.sum(grad_in * normed, axis=0))


def normed_rows(hidden, gains):
    normed, inverse_dev = norm_forward(hidden)
    rows_full = lax.all_gather((normed * gains).astype(jnp.bfloat16), "col", axis=1, tiled=True)
    return (rows_full, normed, inverse_dev)


def collect_in(stacked):
    return lax.all_gather(stacked, "row", axis=1, tiled=True)


def collect_out(shard):
    return lax.all_gather(shard, "row", axis=1, tiled=True)


def reduce_cols(activated, weight_full):
    return lax.psum_scatter(matmul(activated, weight_full), "col", scatter_dimension=1, tiled=True)


def input_partial(pairs):
    total = None
    for grad_part, weight_full in pairs:
        piece = matmul_nt(grad_part, weight_full)
        total = piece if total is None else total + piece
    return lax.psum_scatter(total, "col", scatter_dimension=1, tiled=True)


def spread_grad(grad_local):
    return lax.all_gather(grad_local, "col", axis=1, tiled=True)


def in_weight_grads(stacked):
    return lax.psum_scatter(stacked, "row", scatter_dimension=1, tiled=True)


def out_weight_grad(grad_full):
    return lax.psum_scatter(grad_full, "row", scatter_dimension=1, tiled=True)


def feed_forward(hidden, gains, up_shard, down_shard):
    rows_full, normed, inverse_dev = normed_rows(hidden, gains)
    up_full = collect_in(up_shard[None])[0]
    down_full = collect_out(down_shard)
    pre_act = matmul(rows_full, up_full)
    activated = jax.nn.silu(pre_act).astype(jnp.bfloat16)
    branch = reduce_cols(activated, down_full)
    return (branch, (rows_full, normed, inverse_dev, up_full, down_full, pre_act, activated))


def feed_forward_back(resid_grad, saved, gains, factor):
    rows_full, normed, inverse_dev, up_full, down_full, pre_act, activated = saved
    branch_grad = spread_grad((factor * resid_grad).astype(jnp.bfloat16))
    act_grad = matmul_nt(branch_grad, down_full)
    down_grad = out_weight_grad(matmul_tn(activated, branch_grad))
    sigmoid_val = jax.nn.sigmoid(pre_act)
    pre_grad = (act_grad * (sigmoid_val + pre_act * sigmoid_val * (1.0 - sigmoid_val))).astype(
        jnp.bfloat16
    )
    rows_grad = input_partial(((pre_grad, up_full),))
    up_grad = in_weight_grads(matmul_tn(rows_full, pre_grad)[None])[0]
    norm_grad, gain_grad = norm_backward(rows_grad, normed, inverse_dev, gains)
    return (resid_grad + norm_grad, gain_grad, up_grad, down_grad)


def relative_index(length, left, right):
    rows_iota = lax.broadcasted_iota(jnp.int32, (length, length), 0)
    cols_iota = lax.broadcasted_iota(jnp.int32, (length, length), 1)
    return jnp.clip(cols_iota - rows_iota, -left, right) + left


def place_terms(rel_terms, rel_index):
    row_count, table_rows = rel_terms.shape
    padded = jnp.pad(rel_terms, ((0, 0), (0, row_count)))
    skewed_width = row_count + table_rows - 1
    flattened = padded.reshape(-1)[LEFT : LEFT + row_count * skewed_width]
    banded = flattened.reshape(row_count, skewed_width)[:, :row_count]
    far_left = jnp.where(rel_index == 0, rel_terms[:, 0:1], banded)
    return jnp.where(
        rel_index == table_rows - 1, rel_terms[:, table_rows - 1 : table_rows], far_left
    )


def split_heads(flat, clip_count):
    head_count = flat.shape[1] // HEAD_DIM
    framed = flat.reshape(clip_count, CLIP_TOKEN_SLOTS, head_count, HEAD_DIM).transpose(0, 2, 1, 3)
    return framed.reshape(clip_count * head_count, CLIP_TOKEN_SLOTS, HEAD_DIM)


def merge_heads(split, clip_count):
    head_count = split.shape[0] // clip_count
    framed = split.reshape(clip_count, head_count, CLIP_TOKEN_SLOTS, HEAD_DIM).transpose(0, 2, 1, 3)
    return framed.reshape(clip_count * CLIP_TOKEN_SLOTS, head_count * HEAD_DIM)


def head_scores(head_query, head_key, positional, head_keep, score_scale):
    scores = (matmul_nt(head_query, head_key) + positional) * score_scale
    return jnp.where(head_keep[None, :], scores, NEG_FILL)


def attention(hidden, gains, query_shard, key_shard, value_shard, output_shard, table, keep_keys):
    rows_full, normed, inverse_dev = normed_rows(hidden, gains)
    proj_full = collect_in(jnp.stack([query_shard, key_shard, value_shard]))
    output_full = collect_out(output_shard)
    clip_count = hidden.shape[0] // CLIP_TOKEN_SLOTS
    query_heads = split_heads(matmul(rows_full, proj_full[0]).astype(jnp.bfloat16), clip_count)
    key_heads = split_heads(matmul(rows_full, proj_full[1]).astype(jnp.bfloat16), clip_count)
    value_heads = split_heads(matmul(rows_full, proj_full[2]).astype(jnp.bfloat16), clip_count)
    head_count = query_heads.shape[0] // clip_count
    keep_heads = jnp.repeat(keep_keys, head_count, axis=0)
    score_scale = 1.0 / math.sqrt(HEAD_DIM)
    rel_index = relative_index(CLIP_TOKEN_SLOTS, LEFT, RIGHT)

    def one_head(items):
        head_query, head_key, head_value, head_keep = items
        positional = place_terms(matmul_nt(head_query, table), rel_index)
        scores = head_scores(head_query, head_key, positional, head_keep, score_scale)
        row_peak = jnp.max(scores, axis=1)
        unnormed = jnp.exp(scores - row_peak[:, None])
        row_total = jnp.sum(unnormed, axis=1)
        attention_probability = (unnormed / row_total[:, None]).astype(jnp.bfloat16)
        context = matmul(attention_probability, head_value).astype(jnp.bfloat16)
        return (context, row_peak + jnp.log(row_total))

    context, log_total = lax.map(one_head, (query_heads, key_heads, value_heads, keep_heads))
    context_flat = merge_heads(context, clip_count)
    branch = reduce_cols(context_flat, output_full)
    return (
        branch,
        (
            rows_full,
            normed,
            inverse_dev,
            proj_full,
            output_full,
            query_heads,
            key_heads,
            value_heads,
            context_flat,
            log_total,
            keep_heads,
        ),
    )


def attention_back(resid_grad, saved, gains, table):
    (
        rows_full,
        normed,
        inverse_dev,
        proj_full,
        output_full,
        query_heads,
        key_heads,
        value_heads,
        context_flat,
        log_total,
        keep_heads,
    ) = saved
    clip_count = rows_full.shape[0] // CLIP_TOKEN_SLOTS
    branch_grad = spread_grad(resid_grad.astype(jnp.bfloat16))
    context_grad = split_heads(matmul_nt(branch_grad, output_full).astype(jnp.bfloat16), clip_count)
    output_grad = out_weight_grad(matmul_tn(context_flat, branch_grad))
    table_full = table.astype(jnp.float32)
    score_scale = 1.0 / math.sqrt(HEAD_DIM)
    rel_index = relative_index(CLIP_TOKEN_SLOTS, LEFT, RIGHT)

    def one_head(items):
        head_query, head_key, head_value, head_grad, head_total, head_keep = items
        rel_terms = matmul_nt(head_query, table)
        positional, take_back = jax.vjp(lambda terms: place_terms(terms, rel_index), rel_terms)
        scores = head_scores(head_query, head_key, positional, head_keep, score_scale)
        probs_full = jnp.exp(scores - head_total[:, None])
        attention_probability = probs_full.astype(jnp.bfloat16)
        prob_grad = matmul_nt(head_grad, head_value)
        row_dot = jnp.sum(probs_full * prob_grad, axis=1)
        score_grad = (probs_full * (prob_grad - row_dot[:, None])).astype(jnp.bfloat16)
        value_grad = matmul_tn(attention_probability, head_grad)
        key_grad = matmul_tn(score_grad, head_query) * score_scale
        (rel_grad,) = take_back(score_grad.astype(jnp.float32) * score_scale)
        query_grad = matmul(score_grad, head_key) * score_scale + jnp.dot(
            rel_grad, table_full, precision=HIGH_ACCURACY
        )
        table_term = jnp.dot(rel_grad.T, head_query.astype(jnp.float32), precision=HIGH_ACCURACY)
        return (query_grad, key_grad, value_grad, table_term)

    query_grad, key_grad, value_grad, table_terms = lax.map(
        one_head, (query_heads, key_heads, value_heads, context_grad, log_total, keep_heads)
    )
    query_flat = merge_heads(query_grad, clip_count).astype(jnp.bfloat16)
    key_flat = merge_heads(key_grad, clip_count).astype(jnp.bfloat16)
    value_flat = merge_heads(value_grad, clip_count).astype(jnp.bfloat16)
    rows_grad = input_partial(
        ((query_flat, proj_full[0]), (key_flat, proj_full[1]), (value_flat, proj_full[2]))
    )
    proj_grads = in_weight_grads(
        jnp.stack(
            [
                matmul_tn(rows_full, query_flat),
                matmul_tn(rows_full, key_flat),
                matmul_tn(rows_full, value_flat),
            ]
        )
    )
    norm_grad, gain_grad = norm_backward(rows_grad, normed, inverse_dev, gains)
    return (
        resid_grad + norm_grad,
        gain_grad,
        proj_grads,
        output_grad,
        jnp.sum(table_terms, axis=0),
    )


def depthwise(signal, kernel, clip_count):
    tap_count = kernel.shape[0]
    framed = signal.reshape(clip_count, -1, signal.shape[1])
    length = framed.shape[1]
    padded = jnp.pad(framed, ((0, 0), (tap_count - 1, 0), (0, 0)))
    result = padded[:, 0:length] * kernel[0]
    for tap_index in range(1, tap_count):
        result = result + padded[:, tap_index : tap_index + length] * kernel[tap_index]
    return result.reshape(signal.shape)


def convolution(hidden, gains, value_shard, gate_shard, out_shard, kernel, depth_gains, keep_rows):
    rows_full, normed, inverse_dev = normed_rows(hidden, gains)
    glu_full = collect_in(jnp.stack([value_shard, gate_shard]))
    out_full = collect_out(out_shard)
    clip_count = hidden.shape[0] // CLIP_TOKEN_SLOTS
    value_pre = matmul(rows_full, glu_full[0])
    gate_sig = jax.nn.sigmoid(matmul(rows_full, glu_full[1]))
    gated = value_pre * gate_sig * keep_rows[:, None]
    kernel_full = kernel.astype(jnp.float32)
    mixed = depthwise(gated, kernel_full, clip_count)
    mixed_normed, mixed_inverse = norm_forward(mixed)
    scaled = mixed_normed * depth_gains
    activated = jax.nn.silu(scaled).astype(jnp.bfloat16)
    branch = reduce_cols(activated, out_full)
    return (
        branch,
        (
            rows_full,
            normed,
            inverse_dev,
            glu_full,
            out_full,
            value_pre,
            gate_sig,
            gated,
            kernel_full,
            mixed_normed,
            mixed_inverse,
            scaled,
            activated,
        ),
    )


def convolution_back(resid_grad, saved, gains, depth_gains, keep_rows):
    (
        rows_full,
        normed,
        inverse_dev,
        glu_full,
        out_full,
        value_pre,
        gate_sig,
        gated,
        kernel_full,
        mixed_normed,
        mixed_inverse,
        scaled,
        activated,
    ) = saved
    clip_count = rows_full.shape[0] // CLIP_TOKEN_SLOTS
    branch_grad = spread_grad(resid_grad.astype(jnp.bfloat16))
    act_grad = matmul_nt(branch_grad, out_full)
    out_grad = out_weight_grad(matmul_tn(activated, branch_grad))
    sig_scaled = jax.nn.sigmoid(scaled)
    scaled_grad = act_grad * (sig_scaled + scaled * sig_scaled * (1.0 - sig_scaled))
    mixed_grad, depth_gain_grad = norm_backward(
        scaled_grad, mixed_normed, mixed_inverse, depth_gains
    )
    _, conv_back = jax.vjp(
        lambda signal, taps: depthwise(signal, taps, clip_count), gated, kernel_full
    )
    gated_grad, kernel_grad = conv_back(mixed_grad)
    gated_grad = gated_grad * keep_rows[:, None]
    value_grad = (gated_grad * gate_sig).astype(jnp.bfloat16)
    gate_grad = (gated_grad * value_pre * gate_sig * (1.0 - gate_sig)).astype(jnp.bfloat16)
    rows_grad = input_partial(((value_grad, glu_full[0]), (gate_grad, glu_full[1])))
    glu_grads = in_weight_grads(
        jnp.stack([matmul_tn(rows_full, value_grad), matmul_tn(rows_full, gate_grad)])
    )
    norm_grad, gain_grad = norm_backward(rows_grad, normed, inverse_dev, gains)
    return (resid_grad + norm_grad, gain_grad, glu_grads, kernel_grad, depth_gain_grad, out_grad)


def body(
    layer_input,
    clip_lengths,
    first_gain,
    first_up,
    first_down,
    attend_gain,
    query_weight,
    key_weight,
    value_weight,
    output_weight,
    distance_table,
    conv_gain,
    pointwise_value,
    pointwise_gate,
    depthwise_kernel,
    depthwise_gain,
    pointwise_out,
    second_gain,
    second_up,
    second_down,
    final_gain,
    output_cotangent,
):
    clip_count = clip_lengths.shape[0]
    positions = lax.broadcasted_iota(jnp.int32, (clip_count, CLIP_TOKEN_SLOTS), 1)
    keep_keys = positions < clip_lengths[:, None]
    keep_rows = keep_keys.reshape(-1).astype(jnp.float32)
    start = layer_input.astype(jnp.float32).T
    branch_first, first_saved = feed_forward(start, first_gain, first_up, first_down)
    after_first = start + 0.5 * branch_first
    branch_attend, attend_saved = attention(
        after_first,
        attend_gain,
        query_weight,
        key_weight,
        value_weight,
        output_weight,
        distance_table,
        keep_keys,
    )
    after_attend = after_first + branch_attend
    branch_conv, conv_saved = convolution(
        after_attend,
        conv_gain,
        pointwise_value,
        pointwise_gate,
        pointwise_out,
        depthwise_kernel,
        depthwise_gain,
        keep_rows,
    )
    after_conv = after_attend + branch_conv
    branch_second, second_saved = feed_forward(after_conv, second_gain, second_up, second_down)
    after_second = after_conv + 0.5 * branch_second
    streams = (
        branch_first,
        branch_attend,
        branch_conv,
        branch_second,
        after_first,
        after_attend,
        after_conv,
        after_second,
    )
    squares = jnp.stack(
        [jnp.sum(jnp.sum(stream * stream, axis=1) * keep_rows) for stream in streams]
    )
    final_normed, final_inverse = norm_forward(after_second)
    layer_output = (final_normed * final_gain).T.astype(jnp.bfloat16)
    grad_second, final_part = norm_backward(
        output_cotangent.astype(jnp.float32).T, final_normed, final_inverse, final_gain
    )
    grad_conv, second_part, second_up_grad, second_down_grad = feed_forward_back(
        grad_second, second_saved, second_gain, 0.5
    )
    grad_attend, conv_part, glu_grads, kernel_part, depth_part, pointwise_out_grad = (
        convolution_back(grad_conv, conv_saved, conv_gain, depthwise_gain, keep_rows)
    )
    grad_first, attend_part, proj_grads, output_weight_grad, table_part = attention_back(
        grad_attend, attend_saved, attend_gain, distance_table
    )
    input_rows, first_part, first_up_grad, first_down_grad = feed_forward_back(
        grad_first, first_saved, first_gain, 0.5
    )
    input_grad = input_rows.T
    gain_parts = jnp.stack(
        [first_part, attend_part, conv_part, depth_part, second_part, final_part]
    )
    gain_sums, kernel_sum, count_sum = lax.psum(
        (gain_parts, kernel_part, jnp.sum(clip_lengths).astype(jnp.float32)), "row"
    )
    square_sums, table_sum = lax.psum((squares, table_part), ("row", "col"))
    full_width = layer_input.shape[0] * lax.axis_size("col")
    masked_rms = jnp.sqrt(square_sums / (count_sum * full_width))
    return (
        layer_output,
        input_grad,
        gain_sums[0],
        first_up_grad,
        first_down_grad,
        gain_sums[1],
        proj_grads[0],
        proj_grads[1],
        proj_grads[2],
        output_weight_grad,
        table_sum,
        gain_sums[2],
        glu_grads[0],
        glu_grads[1],
        kernel_sum,
        gain_sums[3],
        pointwise_out_grad,
        gain_sums[4],
        second_up_grad,
        second_down_grad,
        gain_sums[5],
        masked_rms,
    )


def solution(mesh):
    in_specs = (
        P("col", "row"),
        P("row"),
        P("col"),
        P("row", "col"),
        P("col", "row"),
        P("col"),
        P("row", "col"),
        P("row", "col"),
        P("row", "col"),
        P("col", "row"),
        P(),
        P("col"),
        P("row", "col"),
        P("row", "col"),
        P(None, "col"),
        P("col"),
        P("col", "row"),
        P("col"),
        P("row", "col"),
        P("col", "row"),
        P("col"),
        P("col", "row"),
    )
    out_specs = (
        P("col", "row"),
        P("col", "row"),
        P("col"),
        P("row", "col"),
        P("col", "row"),
        P("col"),
        P("row", "col"),
        P("row", "col"),
        P("row", "col"),
        P("col", "row"),
        P(),
        P("col"),
        P("row", "col"),
        P("row", "col"),
        P(None, "col"),
        P("col"),
        P("col", "row"),
        P("col"),
        P("row", "col"),
        P("col", "row"),
        P("col"),
        P(),
    )
    return jax.shard_map(body, mesh=mesh, in_specs=in_specs, out_specs=out_specs, check_vma=False)
```

profile of v0, /device:TPU:0, one launch (start us, length us, event | category | flops | bytes accessed | tf_op | source)
XLA Modules:
  0.0 1946.4 jit_solution(11871315715032242766)
XLA Ops:
  8.9 11.5 all-reduce.82
  23.8 33.2 %all-gather.17.cloned.1.call-done = bf16[1024,1024]{1,0:T(8,128)(2,1)} async-done(((bf16[1024,256]{1,0:T(8,128)(2,1)}), bf16[1024,1024]{1,0:T(8,128)(2,1)}) %all-gather.17.cloned.1.call-update) | async-done | bytes 2097168 | tf_op jit(solution)/shard_map/all_gather | solution.py:56
  56.9 30.7 %all-gather.41.cloned.1.call-done = bf16[1024,1024]{1,0:T(8,128)(2,1)} async-done(((bf16[128,1024]{1,0:T(8,128)(2,1)}), bf16[1024,1024]{1,0:T(8,128)(2,1)}) %all-gather.41.cloned.1.call-update) | async-done | bytes 2097168 | tf_op jit(solution)/shard_map/all_gather | solution.py:61
  87.7 6.9 fusion.72
  94.6 25.0 %all-gather.19.cloned.1.call-done = bf16[1024,1024]{1,0:T(8,128)(2,1)} async-done(((bf16[1024,128]{1,0:T(8,128)(2,1)}), bf16[1024,1024]{1,0:T(8,128)(2,1)}) %all-gather.19.cloned.1.call-update) | async-done | bytes 2097168 | tf_op jit(solution)/shard_map/all_gather | solution.py:65
  127.2 50.2 %reduce-scatter.17.cloned.1.call-done = f32[1024,256]{1,0:T(8,128)} async-done(((f32[1024,1024]{1,0:T(8,128)}), f32[1024,256]{1,0:T(8,128)}) %reduce-scatter.17.cloned.1.call-update) | async-done | bytes 1048592 | tf_op jit(solution)/shard_map/reduce_scatter | solution.py:69
  179.7 9.1 all-reduce.81
  190.8 19.3 all_gather.53
  210.0 35.7 %all-gather.21.cloned.1.call-done = bf16[1024,1024]{1,0:T(8,128)(2,1)} async-done(((bf16[1024,256]{1,0:T(8,128)(2,1)}), bf16[1024,1024]{1,0:T(8,128)(2,1)}) %all-gather.21.cloned.1.call-update) | async-done | bytes 2097168 | tf_op jit(solution)/shard_map/all_gather | solution.py:56
  257.8 156.1 %while.36 = (s32[]{:T(128)}, bf16[4,1024,64]{1,2,0:T(8,128)(2,1)}, f32[4,1024]{1,0:T(4,128)S(1)}, pred[4,1024]{1,0:T(4,128)(4,1)S(1)}, bf16[4,1024,64]{2,1,0:T(8...) while((s32[]{:T(128)}, bf16[4,1024,64]{1,2,0:T(8,128)(2,1)}, ...), condition=%wide.region_12.13_spmd.clone.clone, body=%wide.region_9.12_spmd.clone.clone.sunk | while | flops 294845440 | bytes 67454080 | solution.py:176
  261.1 8.0 reshape.579
  300.1 8.0 reshape.579
  339.0 8.0 reshape.579
  351.4 6.9 reshape.580
  378.0 8.0 reshape.579
  419.4 51.2 %reduce-scatter.19.cloned.1.call-done = f32[1024,256]{1,0:T(8,128)} async-done(((f32[1024,1024]{1,0:T(8,128)}), f32[1024,256]{1,0:T(8,128)}) %reduce-scatter.19.cloned.1.call-update) | async-done | bytes 1048592 | tf_op jit(solution)/shard_map/reduce_scatter | solution.py:69
  473.0 9.1 all-reduce.80
  483.4 17.6 all_gather.56
  501.0 33.4 %all-gather.25.cloned.1.call-done = bf16[1024,1024]{1,0:T(8,128)(2,1)} async-done(((bf16[1024,256]{1,0:T(8,128)(2,1)}), bf16[1024,1024]{1,0:T(8,128)(2,1)}) %all-gather.25.cloned.1.call-update) | async-done | bytes 2097168 | tf_op jit(solution)/shard_map/all_gather | solution.py:56
  543.2 9.1 all-reduce.79
  557.1 52.0 %reduce-scatter.21.cloned.1.call-done = f32[1024,256]{1,0:T(8,128)} async-done(((f32[1024,1024]{1,0:T(8,128)}), f32[1024,256]{1,0:T(8,128)}) %reduce-scatter.21.cloned.1.call-update) | async-done | bytes 1048592 | tf_op jit(solution)/shard_map/reduce_scatter | solution.py:69
  612.2 9.0 all-reduce.78
  624.5 15.4 all-gather.43.cloned.1.call-done
  639.9 37.1 %all-gather.29.cloned.1.call-done = bf16[1024,1024]{1,0:T(8,128)(2,1)} async-done(((bf16[1024,256]{1,0:T(8,128)(2,1)}), bf16[1024,1024]{1,0:T(8,128)(2,1)}) %all-gather.29.cloned.1.call-update) | async-done | bytes 2097168 | tf_op jit(solution)/shard_map/all_gather | solution.py:56
  677.0 7.5 fusion.71
  684.5 25.0 %all-gather.31.cloned.1.call-done = bf16[1024,1024]{1,0:T(8,128)(2,1)} async-done(((bf16[1024,128]{1,0:T(8,128)(2,1)}), bf16[1024,1024]{1,0:T(8,128)(2,1)}) %all-gather.31.cloned.1.call-update) | async-done | bytes 2097168 | tf_op jit(solution)/shard_map/all_gather | solution.py:65
  718.2 49.8 %reduce-scatter.23.cloned.1.call-done = f32[1024,256]{1,0:T(8,128)} async-done(((f32[1024,1024]{1,0:T(8,128)}), f32[1024,256]{1,0:T(8,128)}) %reduce-scatter.23.cloned.1.call-update) | async-done | bytes 1048592 | tf_op jit(solution)/shard_map/reduce_scatter | solution.py:69
  771.5 9.0 all-reduce.77
  783.2 9.1 all-reduce.76
  795.0 35.3 %all-gather.33.cloned.1.call-done = bf16[1024,1024]{1,0:T(8,128)(2,1)} async-done(((bf16[1024,256]{1,0:T(8,128)(2,1)}), bf16[1024,1024]{1,0:T(8,128)(2,1)}) %all-gather.33.cloned.1.call-update) | async-done | bytes 2097168 | tf_op jit(solution)/shard_map/all_gather | solution.py:81
  842.9 52.8 %reduce-scatter.25.cloned.1.call-done = f32[1024,256]{1,0:T(8,128)} async-done(((f32[1024,1024]{1,0:T(8,128)}), f32[1024,256]{1,0:T(8,128)}) %reduce-scatter.25.cloned.1.call-update) | async-done | bytes 1048592 | tf_op jit(solution)/shard_map/reduce_scatter | solution.py:77
  898.4 9.0 all-reduce.75
  912.3 35.2 %all-gather.35.cloned.1.call-done = bf16[1024,1024]{1,0:T(8,128)(2,1)} async-done(((bf16[1024,256]{1,0:T(8,128)(2,1)}), bf16[1024,1024]{1,0:T(8,128)(2,1)}) %all-gather.35.cloned.1.call-update) | async-done | bytes 2097168 | tf_op jit(solution)/shard_map/all_gather | solution.py:81
  952.1 9.1 all-reduce.74
  972.4 8.0 pad_add_fusion
  986.4 52.7 %reduce-scatter.27.cloned.1.call-done = f32[1024,256]{1,0:T(8,128)} async-done(((f32[1024,1024]{1,0:T(8,128)}), f32[1024,256]{1,0:T(8,128)}) %reduce-scatter.27.cloned.1.call-update) | async-done | bytes 1048592 | tf_op jit(solution)/shard_map/reduce_scatter | solution.py:77
  1041.6 9.1 all-reduce.73
  1053.7 35.0 %all-gather.37.cloned.1.call-done = bf16[1024,1024]{1,0:T(8,128)(2,1)} async-done(((bf16[1024,256]{1,0:T(8,128)(2,1)}), bf16[1024,1024]{1,0:T(8,128)(2,1)}) %all-gather.37.cloned.1.call-update) | async-done | bytes 2097168 | tf_op jit(solution)/shard_map/all_gather | solution.py:81
  1091.7 331.3 %while.37 = (s32[]{:T(128)}, bf16[4,1024,64]{1,2,0:T(8,128)(2,1)}, bf16[4,1024,64]{1,2,0:T(8,128)(2,1)}, bf16[4,1024,64]{1,2,0:T(8,128)(2,1)}, f32[4,73,64]{1,2,...) while((s32[]{:T(128)}, bf16[4,1024,64]{1,2,0:T(8,128)(2,1)}, ...), condition=%wide.region_54.55_spmd.clone.clone, body=%wide.region_50.54_spmd.clone.clone.sunk | while | flops 835814400 | bytes 161982992 | solution.py:238
  1098.7 8.1 reshape.581
  1152.5 7.1 reshape.583
  1164.0 8.0 reshape.584
  1181.3 8.1 reshape.581
  1235.2 7.1 reshape.583
  1246.7 8.0 reshape.584
  1264.0 8.1 reshape.581
  1317.9 7.1 reshape.583
  1329.4 8.0 reshape.584
  1346.7 8.1 reshape.581
  1400.6 7.1 reshape.583
  1412.0 8.0 reshape.584
  1429.1 52.8 %reduce-scatter.29.cloned.1.call-done = f32[1024,256]{1,0:T(8,128)} async-done(((f32[1024,1024]{1,0:T(8,128)}), f32[1024,256]{1,0:T(8,128)}) %reduce-scatter.29.cloned.1.call-update) | async-done | bytes 1048592 | tf_op jit(solution)/shard_map/reduce_scatter | solution.py:77
  1483.8 9.1 all-reduce.72
  1506.4 23.5 %all-gather.39.cloned.1.call-done = bf16[1024,1024]{1,0:T(8,128)(2,1)} async-done(((bf16[1024,256]{1,0:T(8,128)(2,1)}), bf16[1024,1024]{1,0:T(8,128)(2,1)}) %all-gather.39.cloned.1.call-update) | async-done | bytes 2097168 | tf_op jit(solution)/shard_map/all_gather | solution.py:81
  1595.4 40.3 %all-reduce.69 = (f32[73,64]{0,1:T(8,128)}, f32[8]{0:T(128)S(1)}) all-reduce(f32[73,64]{0,1:T(8,128)S(1)} %reduce_sum.761, f32[8]{0:T(128)S(1)} %stack.119), channel_id=1, replica_groups=mesh['row'=8,'col'=4] {'row','col'}, use_global_device_ids=true, to_apply=%region_77.78 | all-reduce | flops 4680 | bytes 37440 | tf_op jit(solution)/shard_map/psum | solution.py:443
  1637.5 27.8 %reduce-scatter.31.cloned.1.call-done = f32[1024,256]{1,0:T(8,128)} async-done(((f32[1024,1024]{1,0:T(8,128)}), f32[1024,256]{1,0:T(8,128)}) %reduce-scatter.31.cloned.1.call-update) | async-done | bytes 1048592 | tf_op jit(solution)/shard_map/reduce_scatter | solution.py:77
  1667.3 9.1 all-reduce.71
  1679.7 30.4 %all-reduce.70 = (f32[6,256]{1,0:T(8,128)S(1)}, f32[31,256]{1,0:T(8,128)}, f32[]{:T(128)}) all-reduce(f32[6,256]{1,0:T(8,128)S(1)} %stack.103, f32[31,256]{1,0:T(8,128)S(1)} %pad_add_fusion.7, f32[]{:T(128)S(6)} %convert_element_type.208), channel_id=1, replica_groups=mesh['row'=8,'col'=4] {'row'}, use_global_device_ids=true, to_apply=%region_71.72 | all-reduce | flops 9473 | bytes 75784 | tf_op jit(solution)/shard_map/psum | solution.py:440
  1711.9 7.6 reduce-scatter.47.cloned.1.call-done
  1719.5 50.9 %reduce-scatter.45.cloned.1.call-done = f32[1,128,1024]{2,1,0:T(8,128)} async-done(((f32[1,1024,1024]{2,1,0:T(8,128)}), f32[1,128,1024]{2,1,0:T(8,128)}) %reduce-scatter.45.cloned.1.call-update) | async-done | bytes 524304 | tf_op jit(solution)/shard_map/reduce_scatter | solution.py:85
  1770.4 33.3 %reduce-scatter.43.cloned.1.call-done = f32[256,128]{1,0:T(8,128)} async-done(((f32[256,1024]{1,0:T(8,128)}), f32[256,128]{1,0:T(8,128)}) %reduce-scatter.43.cloned.1.call-update) | async-done | bytes 131088 | tf_op jit(solution)/shard_map/reduce_scatter | solution.py:89
  1803.7 33.5 %reduce-scatter.39.cloned.1.call-done = f32[256,128]{1,0:T(8,128)} async-done(((f32[256,1024]{1,0:T(8,128)}), f32[256,128]{1,0:T(8,128)}) %reduce-scatter.39.cloned.1.call-update) | async-done | bytes 131088 | tf_op jit(solution)/shard_map/reduce_scatter | solution.py:89
  1837.2 51.0 %reduce-scatter.35.cloned.1.call-done = f32[1024,128]{1,0:T(8,128)} async-done(((f32[1024,1024]{1,0:T(8,128)}), f32[1024,128]{1,0:T(8,128)}) %reduce-scatter.35.cloned.1.call-update) | async-done | bytes 524304 | tf_op jit(solution)/shard_map/reduce_scatter | solution.py:89
  1888.2 50.9 %reduce-scatter.33.cloned.1.call-done = f32[1,128,1024]{2,1,0:T(8,128)} async-done(((f32[1,1024,1024]{2,1,0:T(8,128)}), f32[1,128,1024]{2,1,0:T(8,128)}) %reduce-scatter.33.cloned.1.call-update) | async-done | bytes 524304 | tf_op jit(solution)/shard_map/reduce_scatter | solution.py:85
  (537 shorter events, 573.7 us)
Async XLA Ops:
  7.2 13.9 copy-start.75
  7.2 49.7 %all-gather.17.cloned.1.call-start = ((), (), s32[]{:S(2)}) async-start(), calls=%async_computation.16 | async-start | bytes 2621440 | tf_op jit(solution)/shard_map/all_gather | solution.py:56
  8.5 168.9 %copy-start.9 = (bf16[256,1024]{0,1:T(8,128)(2,1)}, bf16[256,1024]{0,1:T(8,128)(2,1)S(1)}, u32[]{:S(2)}) copy-start(bf16[256,1024]{0,1:T(8,128)(2,1)S(1)} %copy.59) | copy-start | bytes 1572868
  22.2 65.4 %all-gather.41.cloned.1.call-start = ((), (), s32[]{:S(2)}) async-start(), calls=%async_computation.44 | async-start | bytes 2359296 | tf_op jit(solution)/shard_map/all_gather | solution.py:61
  23.0 96.6 %all-gather.19.cloned.1.call-start = ((), (), s32[]{:S(2)}) async-start(), calls=%async_computation.17 | async-start | bytes 2359296 | tf_op jit(solution)/shard_map/all_gather | solution.py:65
  23.7 153.7 %reduce-scatter.17.cloned.1.call-start = ((), (), s32[]{:S(2)}) async-start(), calls=%async_computation.18 | async-start | bytes 5242880 | tf_op jit(solution)/shard_map/reduce_scatter | solution.py:69
  94.6 30.9 %copy-start.91 = (bf16[1024,1024]{1,0:T(8,128)(2,1)}, bf16[1024,1024]{1,0:T(8,128)(2,1)S(1)}, u32[]{:S(2)}) copy-start(bf16[1024,1024]{1,0:T(8,128)(2,1)S(1)} %get-tuple-element.728) | copy-start | bytes 6291460
  125.5 63.3 %copy-start.72 = (f32[256]{0:T(256)S(1)}, f32[256]{0:T(256)}, u32[]{:S(2)}) copy-start(f32[256]{0:T(256)} %param.31) | copy-start | bytes 3076
  125.5 84.5 %all-gather.23.cloned.1.call-start = ((), (), s32[]{:S(2)}) async-start(), calls=%async_computation.20 | async-start | bytes 1769472 | tf_op jit(solution)/shard_map/all_gather | solution.py:61
  127.1 63.6 %copy-start.38 = (bf16[256,128]{1,0:T(8,128)(2,1)S(1)}, bf16[256,128]{1,0:T(8,128)(2,1)}, u32[]{:S(2)}) copy-start(bf16[256,128]{1,0:T(8,128)(2,1)} %param.35) | copy-start | bytes 196612
  127.1 118.5 %all-gather.21.cloned.1.call-start = ((), (), s32[]{:S(2)}) async-start(), calls=%async_computation.19 | async-start | bytes 2621440 | tf_op jit(solution)/shard_map/all_gather | solution.py:56
  179.7 290.9 %copy-start.5 = (f32[1024,256]{1,0:T(8,128)}, f32[1024,256]{1,0:T(8,128)S(1)}, u32[]{:S(2)}) copy-start(f32[1024,256]{1,0:T(8,128)S(1)} %get-tuple-element.629) | copy-start | bytes 3145732
  188.8 21.2 %copy-start.49 = (f32[1024]{0:T(1024)}, f32[1024]{0:T(1024)S(1)}, u32[]{:S(2)}) copy-start(f32[1024]{0:T(1024)S(1)} %get-tuple-element.724) | copy-start | bytes 12292
  188.8 21.2 %copy-start.51 = (f32[1024]{0:T(1024)}, f32[1024]{0:T(1024)S(1)}, u32[]{:S(2)}) copy-start(f32[1024]{0:T(1024)S(1)} %get-tuple-element.725) | copy-start | bytes 12292
  190.0 280.7 %reduce-scatter.19.cloned.1.call-start = ((), (), s32[]{:S(2)}) async-start(), calls=%async_computation.21 | async-start | bytes 5242880 | tf_op jit(solution)/shard_map/reduce_scatter | solution.py:69
  210.0 39.4 %copy-start.30 = (bf16[3,1024,256]{2,1,0:T(8,128)(2,1)S(1)}, bf16[3,1024,256]{2,1,0:T(8,128)(2,1)}, u32[]{:S(2)}) copy-start(bf16[3,1024,256]{2,1,0:T(8,128)(2,1)} %all-gather.23.cloned.1.call-done) | copy-start | bytes 4718596
  417.8 64.3 %copy-start.71 = (f32[256]{0:T(256)S(1)}, f32[256]{0:T(256)}, u32[]{:S(2)}) copy-start(f32[256]{0:T(256)} %param.37) | copy-start | bytes 3076
  417.9 83.2 %all-gather.27.cloned.1.call-start = ((), (), s32[]{:S(2)}) async-start(), calls=%async_computation.23 | async-start | bytes 1179648 | tf_op jit(solution)/shard_map/all_gather | solution.py:61
  419.4 63.9 %copy-start.53 = (bf16[31,256]{1,0:T(8,128)(2,1)S(1)}, bf16[31,256]{1,0:T(8,128)(2,1)}, u32[]{:S(2)}) copy-start(bf16[31,256]{1,0:T(8,128)(2,1)} %param.40) | copy-start | bytes 47620
  419.4 64.0 %copy-start.39 = (bf16[256,128]{1,0:T(8,128)(2,1)S(1)}, bf16[256,128]{1,0:T(8,128)(2,1)}, u32[]{:S(2)}) copy-start(bf16[256,128]{1,0:T(8,128)(2,1)} %param.42) | copy-start | bytes 196612
  419.4 115.1 %all-gather.25.cloned.1.call-start = ((), (), s32[]{:S(2)}) async-start(), calls=%async_computation.22 | async-start | bytes 2621440 | tf_op jit(solution)/shard_map/all_gather | solution.py:56
  473.0 61.5 %copy-start.7 = (f32[1024,256]{1,0:T(8,128)}, f32[1024,256]{1,0:T(8,128)S(1)}, u32[]{:S(2)}) copy-start(f32[1024,256]{1,0:T(8,128)S(1)} %get-tuple-element.628) | copy-start | bytes 3145732
  483.3 125.8 %reduce-scatter.21.cloned.1.call-start = ((), (), s32[]{:S(2)}) async-start(), calls=%async_computation.24 | async-start | bytes 5242880 | tf_op jit(solution)/shard_map/reduce_scatter | solution.py:69
  501.0 36.0 %copy-start.21 = (bf16[2,1024,256]{2,1,0:T(8,128)(2,1)S(1)}, bf16[2,1024,256]{2,1,0:T(8,128)(2,1)}, u32[]{:S(2)}) copy-start(bf16[2,1024,256]{2,1,0:T(8,128)(2,1)} %all-gather.27.cloned.1.call-done) | copy-start | bytes 3145732
  538.7 422.4 %copy-start.1 = (f32[1024,256]{1,0:T(8,128)}, f32[1024,256]{1,0:T(8,128)S(1)}, u32[]{:S(2)}) copy-start(f32[1024,256]{1,0:T(8,128)S(1)} %get-tuple-element.730) | copy-start | bytes 3145732
  538.7 13.6 copy-start.82
  543.0 13.3 copy-start.13
  552.3 408.9 %copy-start.66 = (f32[1024]{0:T(1024)}, f32[1024]{0:T(1024)S(1)}, u32[]{:S(2)}) copy-start(f32[1024]{0:T(1024)S(1)} %get-tuple-element.720) | copy-start | bytes 12292
  552.3 408.9 %copy-start.68 = (f32[1024]{0:T(1024)}, f32[1024]{0:T(1024)S(1)}, u32[]{:S(2)}) copy-start(f32[1024]{0:T(1024)S(1)} %get-tuple-element.721) | copy-start | bytes 12292
  556.3 52.8 %copy-start.8 = (f32[1024,256]{1,0:T(8,128)S(1)}, f32[1024,256]{1,0:T(8,128)}, u32[]{:S(2)}) copy-start(f32[1024,256]{1,0:T(8,128)} %copy-done.7) | copy-start | bytes 3145732
  556.3 65.0 %copy-start.70 = (f32[256]{0:T(256)S(1)}, f32[256]{0:T(256)}, u32[]{:S(2)}) copy-start(f32[256]{0:T(256)} %param.43) | copy-start | bytes 3076
  556.3 83.6 %all-gather.43.cloned.1.call-start = ((), (), s32[]{:S(2)}) async-start(), calls=%async_computation.45 | async-start | bytes 2359296 | tf_op jit(solution)/shard_map/all_gather | solution.py:61
  557.0 119.9 %all-gather.29.cloned.1.call-start = ((), (), s32[]{:S(2)}) async-start(), calls=%async_computation.25 | async-start | bytes 2621440 | tf_op jit(solution)/shard_map/all_gather | solution.py:56
  623.7 85.8 %all-gather.31.cloned.1.call-start = ((), (), s32[]{:S(2)}) async-start(), calls=%async_computation.26 | async-start | bytes 2359296 | tf_op jit(solution)/shard_map/all_gather | solution.py:65
  624.5 143.6 %reduce-scatter.23.cloned.1.call-start = ((), (), s32[]{:S(2)}) async-start(), calls=%async_computation.27 | async-start | bytes 5242880 | tf_op jit(solution)/shard_map/reduce_scatter | solution.py:69
  716.1 64.4 %copy-start.74 = (f32[256]{0:T(256)S(1)}, f32[256]{0:T(256)}, u32[]{:S(2)}) copy-start(f32[256]{0:T(256)} %param.46) | copy-start | bytes 3076
  716.2 114.1 %all-gather.33.cloned.1.call-start = ((), (), s32[]{:S(2)}) async-start(), calls=%async_computation.28 | async-start | bytes 2621440 | tf_op jit(solution)/shard_map/all_gather | solution.py:81
  794.9 100.8 %reduce-scatter.25.cloned.1.call-start = ((), (), s32[]{:S(2)}) async-start(), calls=%async_computation.29 | async-start | bytes 5242880 | tf_op jit(solution)/shard_map/reduce_scatter | solution.py:77
  842.8 104.7 %all-gather.35.cloned.1.call-start = ((), (), s32[]{:S(2)}) async-start(), calls=%async_computation.30 | async-start | bytes 2621440 | tf_op jit(solution)/shard_map/all_gather | solution.py:81
  912.3 126.8 %reduce-scatter.27.cloned.1.call-start = ((), (), s32[]{:S(2)}) async-start(), calls=%async_computation.31 | async-start | bytes 5242880 | tf_op jit(solution)/shard_map/reduce_scatter | solution.py:77
  986.3 102.4 %all-gather.37.cloned.1.call-start = ((), (), s32[]{:S(2)}) async-start(), calls=%async_computation.32 | async-start | bytes 2621440 | tf_op jit(solution)/shard_map/all_gather | solution.py:81
  1039.1 11.6 copy-start.17
  1053.5 428.3 %reduce-scatter.29.cloned.1.call-start = ((), (), s32[]{:S(2)}) async-start(), calls=%async_computation.33 | async-start | bytes 5242880 | tf_op jit(solution)/shard_map/reduce_scatter | solution.py:77
  1429.0 52.9 %copy-start.6 = (f32[1024,256]{1,0:T(8,128)S(1)}, f32[1024,256]{1,0:T(8,128)}, u32[]{:S(2)}) copy-start(f32[1024,256]{1,0:T(8,128)} %copy-done.5) | copy-start | bytes 3145732
  1429.0 52.9 %copy-start.50 = (f32[1024]{0:T(1024)S(1)}, f32[1024]{0:T(1024)}, u32[]{:S(2)}) copy-start(f32[1024]{0:T(1024)} %copy-done.49) | copy-start | bytes 12292
  1429.0 52.9 %copy-start.52 = (f32[1024]{0:T(1024)S(1)}, f32[1024]{0:T(1024)}, u32[]{:S(2)}) copy-start(f32[1024]{0:T(1024)} %copy-done.51) | copy-start | bytes 12292
  1429.0 52.9 %copy-start.73 = (f32[256]{0:T(256)S(1)}, f32[256]{0:T(256)}, u32[]{:S(2)}) copy-start(f32[256]{0:T(256)} %param.31) | copy-start | bytes 3076
  1429.0 63.9 %copy-start.19 = (f32[1024,256]{1,0:T(8,128)S(1)}, f32[1024,256]{1,0:T(8,128)}, u32[]{:S(2)}) copy-start(f32[1024,256]{1,0:T(8,128)} %get-tuple-element.619) | copy-start | bytes 3145732
  1429.0 101.0 %all-gather.39.cloned.1.call-start = ((), (), s32[]{:S(2)}) async-start(), calls=%async_computation.34 | async-start | bytes 2621440 | tf_op jit(solution)/shard_map/all_gather | solution.py:81
  1481.9 11.1 copy-start.16
  1494.8 99.0 %reduce-scatter.41.cloned.1.call-start = ((), (), s32[]{:S(2)}) async-start(), calls=%async_computation.40 | async-start | bytes 2359296 | tf_op jit(solution)/shard_map/reduce_scatter | solution.py:85
  1499.7 136.1 %reduce-scatter.37.cloned.1.call-start = ((), (), s32[]{:S(2)}) async-start(), calls=%async_computation.38 | async-start | bytes 3538944 | tf_op jit(solution)/shard_map/reduce_scatter | solution.py:85
  1506.2 23.8 %copy-start.86 = (bf16[1024,1024]{1,0:T(8,128)(2,1)S(1)}, bf16[1024,1024]{1,0:T(8,128)(2,1)}, u32[]{:S(2)}) copy-start(bf16[1024,1024]{1,0:T(8,128)(2,1)} %all-gather.19.cloned.1.call-done) | copy-start | bytes 6291460
  1506.2 159.1 %reduce-scatter.31.cloned.1.call-start = ((), (), s32[]{:S(2)}) async-start(), calls=%async_computation.35 | async-start | bytes 5242880 | tf_op jit(solution)/shard_map/reduce_scatter | solution.py:77
  1541.9 177.6 %reduce-scatter.47.cloned.1.call-start = ((), (), s32[]{:S(2)}) async-start(), calls=%async_computation.43 | async-start | bytes 4718592 | tf_op jit(solution)/shard_map/reduce_scatter | solution.py:89
  1549.5 220.9 %reduce-scatter.45.cloned.1.call-start = ((), (), s32[]{:S(2)}) async-start(), calls=%async_computation.42 | async-start | bytes 4718592 | tf_op jit(solution)/shard_map/reduce_scatter | solution.py:85
  1557.1 246.6 %reduce-scatter.43.cloned.1.call-start = ((), (), s32[]{:S(2)}) async-start(), calls=%async_computation.41 | async-start | bytes 1179648 | tf_op jit(solution)/shard_map/reduce_scatter | solution.py:89
  1562.0 275.2 %reduce-scatter.39.cloned.1.call-start = ((), (), s32[]{:S(2)}) async-start(), calls=%async_computation.39 | async-start | bytes 1179648 | tf_op jit(solution)/shard_map/reduce_scatter | solution.py:89
  1565.4 322.8 %reduce-scatter.35.cloned.1.call-start = ((), (), s32[]{:S(2)}) async-start(), calls=%async_computation.37 | async-start | bytes 4718592 | tf_op jit(solution)/shard_map/reduce_scatter | solution.py:89
  1572.4 366.7 %reduce-scatter.33.cloned.1.call-start = ((), (), s32[]{:S(2)}) async-start(), calls=%async_computation.36 | async-start | bytes 4718592 | tf_op jit(solution)/shard_map/reduce_scatter | solution.py:85
  1592.4 73.0 %copy-start.10 = (bf16[256,1024]{0,1:T(8,128)(2,1)S(1)}, bf16[256,1024]{0,1:T(8,128)(2,1)}, u32[]{:S(2)}) copy-start(bf16[256,1024]{0,1:T(8,128)(2,1)} %copy-done.9) | copy-start | bytes 1572868
  1592.4 73.0 %copy-start.46 = (f32[1024]{0:T(1024)S(1)}, f32[1024]{0:T(1024)}, u32[]{:S(2)}) copy-start(f32[1024]{0:T(1024)} %copy-done.45) | copy-start | bytes 12292
  1592.4 73.0 %copy-start.48 = (f32[1024]{0:T(1024)S(1)}, f32[1024]{0:T(1024)}, u32[]{:S(2)}) copy-start(f32[1024]{0:T(1024)} %copy-done.47) | copy-start | bytes 12292
  1592.4 72.9 %copy-start.76 = (f32[256]{0:T(256)S(1)}, f32[256]{0:T(256)}, u32[]{:S(2)}) copy-start(f32[256]{0:T(256)} %param.28) | copy-start | bytes 3076
  (69 other events, 230.5 us)
Sparse Core Ops, SparseCore 0:
  22.4 34.5 all-gather.16
  58.5 29.0 all-gather.40
  89.3 30.3 all-gather.18
  125.7 51.7 reduce-scatter.16
  179.5 28.8 all-gather.22
  210.8 34.8 all-gather.20
  418.0 52.6 reduce-scatter.18
  472.9 24.0 all-gather.26
  499.3 35.0 all-gather.24
  556.4 52.5 reduce-scatter.20
  610.7 29.0 all-gather.42
  642.3 34.6 all-gather.28
  678.6 30.8 all-gather.30
  716.3 51.7 reduce-scatter.22
  795.0 35.1 all-gather.32
  843.0 52.6 reduce-scatter.24
  912.4 35.0 all-gather.34
  986.4 52.6 reduce-scatter.26
  1053.6 35.0 all-gather.36
  1429.1 52.6 reduce-scatter.28
  1494.9 35.0 all-gather.38
  1532.4 35.8 reduce-scatter.40
  1570.6 39.0 reduce-scatter.36
  1612.8 52.4 reduce-scatter.30
  1668.2 51.2 reduce-scatter.46
  1722.2 48.1 reduce-scatter.44
  1773.1 30.5 reduce-scatter.42
  1806.5 30.5 reduce-scatter.38
  1840.1 48.1 reduce-scatter.34
  1890.9 48.1 reduce-scatter.32
where the time goes:
time: 1960 us; the launch traced here: 1950 us
  waiting for transfers between devices  984 us (50%)
  local copies, waits for them, and re-layouts  414 us (21%)
  blocking collectives  219 us (11%)
  matrix products  206 us (11%)
  other arithmetic  103 us (5%)
    reduce_scatter x4, waiting for transfers between devices, reduce_cols(): lax.psum_scatter(matmul(activated, weight_full), 'col', scatter_dimension...  203 us
    reduce_scatter x4, waiting for transfers between devices, input_partial(): return lax.psum_scatter(total, 'col', scatter_dimension=1, tiled=True)  186 us
    all_gather x4, waiting for transfers between devices, normed_rows(): lax.all_gather((normed * gains).astype(jnp.bfloat16), 'col', axis=1, tile...  139 us
    all_gather x4, waiting for transfers between devices, spread_grad(): return lax.all_gather(grad_local, 'col', axis=1, tiled=True)  129 us
    reduce_scatter x4, waiting for transfers between devices, out_weight_grad(): return lax.psum_scatter(grad_full, 'row', scatter_dimension=1, tiled=True)  125 us
    reduce_scatter x4, waiting for transfers between devices, in_weight_grads(): return lax.psum_scatter(stacked, 'row', scatter_dimension=1, tiled=True)  102 us
    reshape x12, local copies, waits for them, and re-layouts, place_terms(): flattened = padded.reshape(-1)[LEFT:LEFT + row_count * skewed_width]  96.3 us
    dot_general x31, matrix products, matmul_nt(): lax.dot_general(left, right, (((1,), (1,)), ((), ())), preferred_element_...  88.9 us
  transfers between devices with their start and end apart: 30, of which 26 were waited for; matrix products, arithmetic and copies ran while one was open for 5% of the time, Pallas kernels for 0%

commit v1 on v0

v1 whole, which is shorter than its diff:
```python
import functools
import math

import jax
import jax.numpy as jnp
from jax import lax
from jax.experimental import pallas as pl
from jax.experimental.pallas import tpu as pltpu
from jax.sharding import PartitionSpec as P

HEAD_DIM = 64
LEFT = 64
RIGHT = 8
EPSILON = 1e-05
NEG_FILL = -1e30
BF16 = jnp.bfloat16
F32 = jnp.float32
MESH = pl.DeviceIdType.MESH
BLOCK = 128
WINDOW = 384
SPAN = 512
VMEM_LIMIT = 60 * 1024 * 1024


def matmul(left, right):
    return jnp.dot(left, right, preferred_element_type=F32)


def matmul_nt(left, right):
    return lax.dot_general(left, right, (((1,), (1,)), ((), ())), preferred_element_type=F32)


def matmul_tn(left, right):
    return lax.dot_general(left, right, (((0,), (0,)), ((), ())), preferred_element_type=F32)


def vmem():
    return pl.BlockSpec(memory_space=pltpu.VMEM)


def anywhere():
    return pl.BlockSpec(memory_space=pl.ANY)


def comm_params(collective_id):
    return pltpu.CompilerParams(
        collective_id=collective_id, has_side_effects=True, vmem_limit_bytes=VMEM_LIMIT
    )


def tile(index, size):
    return pl.ds(pl.multiple_of(index * size, size), size)


class Wire:
    def __init__(self, sizes, send_sem, recv_sem, local_sem, side, col_on=True, row_on=False):
        self.n, self.m = sizes
        self.me = lax.axis_index("col")
        self.row = lax.axis_index("row")
        self.send_sem, self.recv_sem, self.local_sem = send_sem, recv_sem, local_sem
        self.used = 0
        self.used_local = 0
        self.core = lax.rem(self.row, 2)
        self.layer = self.row // 2
        self.partner = self.row + 1 - 2 * self.core
        self.layers = self.m // 2
        self.col_on = col_on
        self.row_on = row_on or bool(side)
        self.side = [job(self) for job in side]

    def layer_peer(self, step):
        return lax.rem(self.layer + step, self.layers) * 2 + self.core

    def greet(self):
        barrier = pltpu.get_barrier_semaphore()
        waits = 0
        if self.col_on:
            for step in range(1, self.n):
                pl.semaphore_signal(
                    barrier, inc=1, device_id={"col": lax.rem(self.me + step, self.n)},
                    device_id_type=MESH,
                )
            waits += self.n - 1
        if self.row_on:
            for step in range(1, self.layers):
                pl.semaphore_signal(
                    barrier, inc=1, device_id={"row": self.layer_peer(step)}, device_id_type=MESH
                )
            pl.semaphore_signal(
                barrier, inc=1, device_id={"row": self.partner}, device_id_type=MESH
            )
            waits += self.layers
        pl.semaphore_wait(barrier, waits)

    def remote(self, source, target, axis, peer):
        slot = self.used
        self.used += 1
        return pltpu.make_async_remote_copy(
            src_ref=source, dst_ref=target, send_sem=self.send_sem.at[slot],
            recv_sem=self.recv_sem.at[slot], device_id={axis: peer}, device_id_type=MESH,
        )

    def local(self, source, target):
        slot = self.used_local
        self.used_local += 1
        return pltpu.make_async_copy(source, target, self.local_sem.at[slot])

    def to_all(self, source_of, target):
        copies = [
            self.remote(source_of(lax.rem(self.me + step, self.n)), target, "col",
                        lax.rem(self.me + step, self.n))
            for step in range(1, self.n)
        ]
        for copy in copies:
            copy.start()
        return copies

    def begin(self):
        for job in self.side:
            job.begin()

    def early(self):
        for job in self.side:
            job.early()

    def middle(self):
        for job in self.side:
            job.middle()

    def end(self):
        for job in self.side:
            job.end()

    def peers(self):
        if self.n == 4:
            across = self.me + 1 - 2 * lax.rem(self.me, 2)
            along = lax.rem(self.me + 2, 4)
            return [(across, 0), (along, 1), (3 - self.me, 2)]
        return [
            (lax.rem(self.me + self.n - step, self.n), self.n - step - 1)
            for step in range(1, self.n)
        ]


class Spread:
    def __init__(self, wire, ref, count):
        self.wire, self.ref, self.count = wire, ref, count
        me = wire.me
        if wire.n != 4:
            self.copies = [
                wire.remote(self.part(me), self.part(me), "col", lax.rem(me + step, wire.n))
                for step in range(1, wire.n)
            ]
            return
        (across, _), (along, _), (far, _) = wire.peers()
        self.across = [wire.remote(self.part(me, q), self.part(me, q), "col", across) for q in range(4)]
        self.along = [wire.remote(self.part(me, q), self.part(me, q), "col", along) for q in range(4)]
        self.onward = [
            wire.remote(self.part(across, q), self.part(across, q), "col", along) for q in (0, 1)
        ] + [wire.remote(self.part(along, q), self.part(along, q), "col", across) for q in (2, 3)]

    def part(self, chunk, quarter=None):
        if quarter is None:
            return self.ref.at[tile(chunk, self.count)]
        size = self.count // 4
        return self.ref.at[tile(chunk * 4 + quarter, size)]

    def start(self):
        if self.wire.n != 4:
            for copy in self.copies:
                copy.start()
            return
        for first, second in ((0, 2), (1, 3), (2, 0), (3, 1)):
            self.across[first].start()
            self.along[second].start()

    def relay(self):
        if self.wire.n != 4:
            return
        for turn in range(2):
            self.across[turn].wait_recv()
            self.onward[turn].start()
            self.along[2 + turn].wait_recv()
            self.onward[2 + turn].start()

    def arrivals(self, relay=True):
        wire = self.wire
        yield wire.me, None
        if wire.n != 4:
            for step, (peer, slot) in zip(range(1, wire.n), wire.peers()):
                self.copies[step - 1].wait_recv()
                yield peer, slot
            return
        if relay:
            self.relay()
        for (peer, slot), copies in zip(
            wire.peers(), (self.across[2:], self.along[:2], self.onward)
        ):
            for copy in copies:
                copy.wait_recv()
            yield peer, slot

    def finish(self):
        copies = self.copies if self.wire.n != 4 else self.across + self.along + self.onward
        for copy in copies:
            copy.wait_send()


class Collect:
    def __init__(self, wire, got):
        self.wire, self.got = wire, got
        self.copies = {}
        self.slots = {slot: wire.used + slot for slot in range(wire.n - 1)}
        wire.used += wire.n - 1

    def send(self, source, owner, slot):
        wire = self.wire
        copy = pltpu.make_async_remote_copy(
            src_ref=source, dst_ref=self.got.at[slot], send_sem=wire.send_sem.at[self.slots[slot]],
            recv_sem=wire.recv_sem.at[self.slots[slot]], device_id={"col": owner},
            device_id_type=MESH,
        )
        copy.start()
        self.copies[slot] = copy

    def wait(self):
        for slot in range(self.wire.n - 1):
            self.copies[slot].wait()


class RowGather:
    def __init__(self, shard, full, wire):
        self.wire = wire
        count = shard.shape[0]
        mine = full.at[tile(wire.row, count)]
        self.first = [wire.local(shard, mine), wire.remote(shard, mine, "row", wire.partner)]
        self.along = [
            wire.remote(shard, mine, "row", wire.layer_peer(step))
            for step in range(1, wire.layers)
        ]
        self.onward = []
        for step in range(1, wire.layers):
            block = full.at[tile(wire.layer_peer(wire.layers - step), count)]
            self.onward.append(wire.remote(block, block, "row", wire.partner))

    def begin(self):
        for copy in self.along + self.first:
            copy.start()

    def early(self):
        pass

    def middle(self):
        for copy, onward in zip(self.along, self.onward):
            copy.wait_recv()
            onward.start()

    def end(self):
        for copy in self.along:
            copy.wait_send()
        for copy in self.first:
            copy.wait()
        for copy in self.onward:
            copy.wait()


class RowReduce:
    def __init__(self, grads, out, held, pair, got, wire, load=True):
        self.wire, self.out, self.grads = wire, out, grads
        self.held, self.pair, self.got = held, pair, got
        self.count = held.shape[1]
        other = 1 - wire.core
        self.load = []
        if load:
            self.load = [
                wire.local(grads.at[tile(layer * 2 + wire.core, self.count)], held.at[layer])
                for layer in range(wire.layers)
            ]
        self.swap = [
            wire.remote(grads.at[tile(layer * 2 + other, self.count)], pair.at[layer], "row",
                        wire.partner)
            for layer in range(wire.layers)
        ]
        self.along = []
        for step in range(1, wire.layers):
            layer = lax.rem(wire.layer + step, wire.layers)
            self.along.append(
                wire.remote(held.at[layer], got.at[step - 1], "row", wire.layer_peer(step))
            )

    def begin(self):
        for copy in self.swap + self.load:
            copy.start()

    def early(self):
        for copy in self.load + self.swap:
            copy.wait()
        size = min(32, self.count)
        for layer in range(self.wire.layers):
            def add(rows, index, layer=layer):
                if self.load:
                    mine = self.held[layer, rows]
                else:
                    at = (layer * 2 + self.wire.core) * self.count + index * size
                    mine = self.grads[pl.ds(pl.multiple_of(at, size), size)]
                self.held[layer, rows] = (
                    mine.astype(F32) + self.pair[layer, rows].astype(F32)
                ).astype(BF16)

            row_loop(self.count, add)
        for copy in self.along:
            copy.start()

    def middle(self):
        pass

    def end(self):
        for copy in self.along:
            copy.wait()

        def add(rows, index):
            total = self.held[self.wire.layer, rows].astype(F32)
            for step in range(self.wire.layers - 1):
                total = total + self.got[step, rows].astype(F32)
            self.out[rows] = total

        row_loop(self.count, add)


def reduce_scratch(layers, count, width):
    return [
        pltpu.VMEM((layers, count, width), BF16),
        pltpu.VMEM((layers, count, width), BF16),
        pltpu.VMEM((max(1, layers - 1), count, width), BF16),
    ]


class SumAll:
    def __init__(self, pieces, shared, kept, out, got, got_shared, packed, got_row, wire):
        self.wire, self.out = wire, out
        self.pieces, self.shared, self.kept = pieces, shared, kept
        self.got, self.got_shared, self.packed, self.got_row = got, got_shared, packed, got_row
        self.col = []
        for step in range(1, wire.n):
            peer = lax.rem(wire.me + step, wire.n)
            self.col.append(wire.remote(pieces.at[peer], got.at[step - 1], "col", peer))
            if shared is not None:
                self.col.append(wire.remote(shared, got_shared.at[step - 1], "col", peer))
        self.swap = wire.remote(packed.at[0], got_row.at[0], "row", wire.partner)
        self.along = [
            wire.remote(packed.at[1], got_row.at[step], "row", wire.layer_peer(step))
            for step in range(1, wire.layers)
        ]

    def begin(self):
        for copy in self.col:
            copy.start()

    def early(self):
        for copy in self.col:
            copy.wait()
        packed = self.packed.at[0]
        first = self.pieces.shape[1]
        total = self.pieces[self.wire.me]
        for step in range(self.wire.n - 1):
            total = total + self.got[step]
        packed[0:first] = total
        if self.shared is not None:
            second = first + self.shared.shape[0]
            total = self.shared[...]
            for step in range(self.wire.n - 1):
                total = total + self.got_shared[step]
            packed[first:second] = total
            packed[second:] = self.kept[...]
        self.swap.start()

    def middle(self):
        self.swap.wait()
        self.packed[1] = self.packed[0] + self.got_row[0]
        for copy in self.along:
            copy.start()

    def end(self):
        for copy in self.along:
            copy.wait()
        total = self.packed[1]
        for step in range(1, self.wire.layers):
            total = total + self.got_row[step]
        self.out[...] = total


def sum_scratch(n, layers, first, second, third, width):
    return [
        pltpu.VMEM((n - 1, first, width), F32),
        pltpu.VMEM((n - 1, max(8, second), width), F32),
        pltpu.VMEM((2, first + second + third, width), F32),
        pltpu.VMEM((layers, first + second + third, width), F32),
    ]


def row_loop(count, body):
    size = min(32, count)

    def step(index, carry):
        body(tile(index, size), index)
        return carry

    lax.fori_loop(0, count // size, step, 0)


def block_loop(extent, body):
    size = min(256, extent)

    def step(index, carry):
        body(tile(index, size), index)
        return carry

    lax.fori_loop(0, extent // size, step, 0)


def fold8(values):
    return jnp.sum(values.reshape(values.shape[0] // 8, 8, values.shape[1]), axis=0)


def normalize(values):
    average = jnp.mean(values, axis=1, keepdims=True)
    centered = values - average
    inverse = lax.rsqrt(jnp.mean(centered * centered, axis=1, keepdims=True) + EPSILON)
    return centered * inverse, inverse


def norm_back(grad_in, normed, inverse, gains):
    scaled = grad_in * gains
    first = jnp.mean(scaled, axis=1, keepdims=True)
    second = jnp.mean(scaled * normed, axis=1, keepdims=True)
    return inverse * (scaled - first - normed * second)


def comm_call(name, collective_id, sizes, main, ins, outs, scratch, gathers=(), reduces=(), cost=10**9,
              col_on=True, more_slots=0, row_on=False):
    n, m = sizes
    layers = m // 2
    in_arrays = [item[0] for item in ins] + list(gathers) + list(reduces)
    in_specs = [item[1] for item in ins] + [vmem()] * len(gathers) + [anywhere()] * len(reduces)
    out_shapes = [jax.ShapeDtypeStruct(item[0], item[1]) for item in outs]
    out_specs = [item[2] for item in outs]
    for shard in gathers:
        out_shapes.append(jax.ShapeDtypeStruct((m * shard.shape[0], shard.shape[1]), shard.dtype))
        out_specs.append(anywhere())
    side_scratch = []
    for grads in reduces:
        count, width = grads.shape[0] // m, grads.shape[1]
        out_shapes.append(jax.ShapeDtypeStruct((count, width), F32))
        out_specs.append(vmem())
        side_scratch += reduce_scratch(layers, count, width)
    remote_slots = 8 * n + 16 + len(gathers) * 2 * layers + len(reduces) * 2 * layers + more_slots
    local_slots = 8 + len(gathers) + len(reduces) * layers + more_slots

    def kernel(*refs):
        at = 0

        def take(count):
            nonlocal at
            at += count
            return refs[at - count:at]

        main_ins = take(len(ins))
        gather_ins = take(len(gathers))
        reduce_ins = take(len(reduces))
        main_outs = take(len(outs))
        gather_outs = take(len(gathers))
        reduce_outs = take(len(reduces))
        main_scratch = take(len(scratch))
        side = [
            functools.partial(RowGather, shard, full)
            for shard, full in zip(gather_ins, gather_outs)
        ]
        for grads, out in zip(reduce_ins, reduce_outs):
            side.append(functools.partial(RowReduce, grads, out, *take(3)))
        send_sem, recv_sem, local_sem = take(3)
        wire = Wire(sizes, send_sem, recv_sem, local_sem, side, col_on, row_on)
        main(wire, main_ins, main_outs, main_scratch)

    return pl.pallas_call(
        kernel,
        name=name,
        out_shape=tuple(out_shapes),
        in_specs=in_specs,
        out_specs=tuple(out_specs),
        scratch_shapes=list(scratch) + side_scratch + [
            pltpu.SemaphoreType.DMA((remote_slots,)),
            pltpu.SemaphoreType.DMA((remote_slots,)),
            pltpu.SemaphoreType.DMA((local_slots,)),
        ],
        compiler_params=comm_params(collective_id),
        cost_estimate=pl.CostEstimate(flops=cost, bytes_accessed=10**8, transcendentals=0),
    )(*in_arrays)


def norm_rows(wire, count, source, gains, rows_ref):
    base = wire.me * count

    def work(rows, index):
        normed, _ = normalize(source[rows])
        size = min(32, count)
        rows_ref[pl.ds(pl.multiple_of(base + index * size, size), size)] = (normed * gains).astype(BF16)

    row_loop(count, work)


def cast_rows(wire, count, source, factor, rows_ref):
    base = wire.me * count

    def work(rows, index):
        size = min(32, count)
        rows_ref[pl.ds(pl.multiple_of(base + index * size, size), size)] = (
            factor * source[rows]
        ).astype(BF16)

    row_loop(count, work)


def owner_sum(wire, rows, part, got):
    total = part[rows].astype(F32)
    for slot in range(wire.n - 1):
        total = total + got[slot, rows].astype(F32)
    return total


def residual(wire, count, factor, part, got, resid, keep_ref, after_ref, squares_ref):
    squares_ref[...] = jnp.zeros_like(squares_ref)

    def work(rows, index):
        branch = owner_sum(wire, rows, part, got)
        after = resid[rows] + factor * branch
        after_ref[rows] = after
        keep = keep_ref[rows]
        squares_ref[0:8] += fold8(branch * branch * keep)
        squares_ref[8:16] += fold8(after * after * keep)

    row_loop(count, work)


def residual_back(wire, count, part, got, grad_ref, resid, gains, new_grad_ref, gain_grad_ref):
    gain_grad_ref[...] = jnp.zeros_like(gain_grad_ref)

    def work(rows, index):
        rows_grad = owner_sum(wire, rows, part, got)
        normed, inverse = normalize(resid[rows])
        new_grad_ref[rows] = grad_ref[rows] + norm_back(rows_grad, normed, inverse, gains)
        gain_grad_ref[...] += fold8(rows_grad * normed)

    row_loop(count, work)


def send_pieces(wire, count, source, pieces, out_ref):
    width = pieces.shape[2]

    def split(rows, index):
        result = source[rows].astype(BF16)
        for part in range(wire.n):
            pieces[part, rows] = result[:, part * width:(part + 1) * width]

    row_loop(count, split)
    mine = out_ref.at[tile(wire.me, count)]
    copies = wire.to_all(lambda peer: pieces.at[peer], mine)
    here = wire.local(pieces.at[wire.me], mine)
    here.start()
    return copies + [here]


def feed_forward_first(count, chunk, rows_ref, up, pre_ref, act):
    rows = tile(chunk, count)
    left = rows_ref[rows]

    def first(cols, index):
        pre = matmul(left, up[:, cols])
        pre_ref[rows, cols] = pre.astype(BF16)
        act[:, cols] = (pre * jax.nn.sigmoid(pre)).astype(BF16)

    block_loop(up.shape[1], first)


def feed_forward_second(act, down_t, target):
    hidden = act[...]

    def second(cols, index):
        target[:, cols] = matmul_nt(hidden, down_t[cols]).astype(BF16)

    block_loop(down_t.shape[0], second)


def feed_forward_main(count, gain_row, factor, enter, turn, wire, ins, outs, scratch):
    ins, outs, scratch = list(ins), list(outs), list(scratch)
    if enter:
        tokens_ref, cot_in, gain_in, keep_ref = ins[:4]
        ins = ins[4:]
        resid, cot_out, gains_ref = outs[:3]
        outs = outs[3:]
        arrived, arrived_cot, arrived_gain = scratch[:3]
        scratch = scratch[3:]
    else:
        resid, keep_ref, gains_ref = ins[:3]
        ins = ins[3:]
    if enter:
        up_shard, down_shard, next_shard = ins[:3]
        ins = ins[3:]
        up_full, down_full, next_full = outs[:3]
        outs = outs[3:]
        up, down_t = scratch[:2]
        scratch = scratch[2:]
    else:
        up, down_t = ins[:2]
        ins = ins[2:]
    if turn:
        (cot_ref,) = ins
        grad_ref, gain_grad_ref, out_ref = outs[:3]
        outs = outs[3:]
        (pieces,) = scratch[:1]
        scratch = scratch[1:]
    after_ref, squares_ref, rows_ref, pre_ref = outs
    act, part, got = scratch
    wire.greet()
    wire.begin()
    if enter:
        up_job = RowGather(up_shard, up_full, wire)
        down_job = RowGather(down_shard, down_full, wire)
        next_job = RowGather(next_shard, next_full, wire)
        up_job.begin()
        width = arrived.shape[2]
        mine = [
            wire.local(tokens_ref.at[tile(wire.me, count)], arrived.at[wire.me]),
            wire.local(gain_in, arrived_gain.at[wire.me]),
            wire.local(cot_in.at[tile(wire.me, count)], arrived_cot.at[wire.me]),
        ]
        copies = wire.to_all(lambda peer: tokens_ref.at[tile(peer, count)], arrived.at[wire.me])
        copies += wire.to_all(lambda peer: gain_in, arrived_gain.at[wire.me])
        for copy in mine:
            copy.start()
        for copy in mine + copies:
            copy.wait()
        for piece in range(wire.n):
            gains_ref[:, piece * width:(piece + 1) * width] = arrived_gain[piece]

        def place(rows, index):
            for piece in range(wire.n):
                resid[rows, piece * width:(piece + 1) * width] = arrived[piece, rows].astype(F32)

        row_loop(count, place)
    gains = gains_ref[gain_row:gain_row + 1]
    norm_rows(wire, count, resid, gains, rows_ref)
    spread = Spread(wire, rows_ref, count)
    spread.start()
    collect = Collect(wire, got)
    cot_copies = []
    if enter:
        cot_copies = wire.to_all(
            lambda peer: cot_in.at[tile(peer, count)], arrived_cot.at[wire.me]
        )
    wire.early()
    if enter:
        spread.relay()
        up_job.middle()
        down_job.begin()
        up_job.end()
        load = wire.local(up_full, up)
        load.start()
        load.wait()
        chunks = []
        for chunk, slot in spread.arrivals(relay=False):
            chunks.append((chunk, slot))
            feed_forward_first(count, chunk, rows_ref, up, pre_ref, act.at[len(chunks) - 1])
        for copy in cot_copies:
            copy.wait()

        def place_cot(rows, index):
            for piece in range(wire.n):
                cot_out[rows, piece * width:(piece + 1) * width] = arrived_cot[piece, rows].astype(F32)

        row_loop(count, place_cot)
        down_job.middle()
        next_job.begin()
        down_job.end()
        load = wire.local(down_full, down_t)
        load.start()
        load.wait()
        for place, (chunk, slot) in reversed(list(enumerate(chunks))):
            target = part.at[wire.n - 1 if slot is None else slot]
            feed_forward_second(act.at[place], down_t, target)
            if slot is not None:
                collect.send(target, chunk, slot)
        next_job.middle()
    else:
        for chunk, slot in spread.arrivals():
            target = part.at[wire.n - 1 if slot is None else slot]
            feed_forward_first(count, chunk, rows_ref, up, pre_ref, act.at[0])
            feed_forward_second(act.at[0], down_t, target)
            if slot is not None:
                collect.send(target, chunk, slot)
    wire.middle()
    collect.wait()
    own = part.at[wire.n - 1]
    residual(wire, count, factor, own, got, resid, keep_ref, after_ref, squares_ref)
    late = []
    if turn:
        final_gains = gains_ref[gain_row + 1:gain_row + 2]
        gain_grad_ref[...] = jnp.zeros_like(gain_grad_ref)

        def final(rows, index):
            normed, inverse = normalize(after_ref[rows])
            cot = cot_ref[rows]
            grad_ref[rows] = norm_back(cot, normed, inverse, final_gains)
            gain_grad_ref[...] += fold8(cot * normed)
            after_ref[rows] = normed * final_gains

        row_loop(count, final)
        late = send_pieces(wire, count, after_ref, pieces, out_ref)
    spread.finish()
    for copy in late:
        copy.wait()
    if enter:
        next_job.end()
    wire.end()


def feed_forward(sizes, name, collective_id, gain_row, up, down_t, keep, resid=None, gains=None,
                 enter=None, turn=None, **side):
    n, m = sizes
    hidden = up.shape[1]
    full = up.shape[0] * (m if enter else 1)
    if enter:
        tokens, cotangent, gain_stack, next_shard = enter
        width = tokens.shape[1]
        count = tokens.shape[0] // n
        ins = [(tokens, vmem()), (cotangent, vmem()), (gain_stack, vmem()), (keep, vmem())]
        outs = [((count, full), F32, vmem()), ((count, full), F32, vmem()), ((8, full), F32, vmem())]
        scratch = [
            pltpu.VMEM((n, count, width), BF16),
            pltpu.VMEM((n, count, width), BF16),
            pltpu.VMEM((n, 8, width), F32),
            pltpu.VMEM((full, hidden), BF16),
            pltpu.VMEM((full, hidden), BF16),
        ]
        ins += [(up, vmem()), (down_t, vmem()), (next_shard, vmem())]
        for shard in (up, down_t, next_shard):
            outs.append(((m * shard.shape[0], shard.shape[1]), BF16, anywhere()))
        side = dict(side, more_slots=6 * m, row_on=True)
    else:
        count = resid.shape[0]
        ins = [(resid, vmem()), (keep, vmem()), (gains, vmem())]
        outs, scratch = [], []
        ins += [(up, vmem()), (down_t, vmem())]
    if turn is not None:
        ins.append((turn, vmem()))
        outs += [
            ((count, full), F32, vmem()),
            ((8, full), F32, vmem()),
            ((n * count, full // n), BF16, anywhere()),
        ]
        scratch.append(pltpu.VMEM((n, count, full // n), BF16))
    outs += [
        ((count, full), F32, vmem()),
        ((16, full), F32, vmem()),
        ((n * count, full), BF16, vmem()),
        ((n * count, hidden), BF16, vmem()),
    ]
    scratch += [
        pltpu.VMEM((n if enter else 1, count, hidden), BF16),
        pltpu.VMEM((n, count, full), BF16),
        pltpu.VMEM((n - 1, count, full), BF16),
    ]
    return comm_call(
        name, collective_id, sizes,
        functools.partial(feed_forward_main, count, gain_row, 0.5, bool(enter), turn is not None),
        ins, outs, scratch, **side,
    )


def feed_forward_back_main(count, gain_row, leave, wire, ins, outs, scratch):
    grad_ref, resid, gains_ref, up, down_t, rows_ref, pre_ref = ins[:7]
    grads, pre_grad, act, part, got = scratch[:5]
    scratch = scratch[5:]
    if leave:
        gain_sum_ref, up_out, down_out, last_ref, sum_out = outs
        gain_grad_ref, up_grad_ref, down_grad_ref = scratch[:3]
        up_job = RowReduce(up_grad_ref, up_out, *scratch[3:6], wire, load=False)
        down_job = RowReduce(down_grad_ref, down_out, *scratch[6:9], wire, load=False)
        sums = SumAll(*ins[7:10], sum_out, *scratch[9:13], wire)
        gain_pieces = scratch[13]
        gain_sums = SumAll(gain_pieces, None, None, gain_sum_ref, *scratch[14:18], wire)
        new_grad_ref, pieces = scratch[18:]
    else:
        gain_grad_ref, up_grad_ref, down_grad_ref, last_ref = outs
        new_grad_ref = last_ref
    gains = gains_ref[gain_row:gain_row + 1]
    wire.greet()
    wire.begin()
    cast_rows(wire, count, grad_ref, 0.5, grads)
    spread = Spread(wire, grads, count)
    spread.start()
    collect = Collect(wire, got)
    if leave:
        sums.begin()
    hidden = up.shape[1]

    def activate(rows, cols):
        pre = pre_ref[rows, cols].astype(F32)
        act[rows, cols] = (pre * jax.nn.sigmoid(pre)).astype(BF16)

    for chunk, slot in spread.arrivals():
        rows = tile(chunk, count)
        target = part.at[wire.n - 1 if slot is None else slot]
        left = grads[rows]

        def first(cols, index):
            act_grad = matmul(left, down_t[:, cols])
            pre = pre_ref[rows, cols].astype(F32)
            sig = jax.nn.sigmoid(pre)
            act[rows, cols] = (pre * sig).astype(BF16)
            pre_grad[rows, cols] = (act_grad * (sig + pre * sig * (1.0 - sig))).astype(BF16)

        block_loop(hidden, first)
        through = pre_grad[rows]

        def second(cols, index):
            target[:, cols] = matmul_nt(through, up[cols]).astype(BF16)

        block_loop(up.shape[0], second)
        if slot is not None:
            collect.send(target, chunk, slot)
        if slot is None:
            wire.early()
            if leave:
                sums.early()
    wire.middle()
    if leave:
        sums.middle()
    size = min(256, hidden)

    def weight_grad(left_ref, right_ref, out):
        for start in range(0, hidden, size):
            cols = slice(start, start + size)

            def block(rows, index):
                out[rows, cols] = matmul_tn(left_ref[:, rows], right_ref[:, cols]).astype(BF16)

            block_loop(up.shape[0], block)

    weight_grad(grads, act, down_grad_ref)
    if leave:
        down_job.begin()
    weight_grad(rows_ref, pre_grad, up_grad_ref)
    if leave:
        up_job.begin()
        down_job.early()
    collect.wait()
    own = part.at[wire.n - 1]
    residual_back(wire, count, own, got, grad_ref, resid, gains, new_grad_ref, gain_grad_ref)
    if leave:
        late = send_pieces(wire, count, new_grad_ref, pieces, last_ref)
        width = gain_pieces.shape[2]
        for piece in range(wire.n):
            gain_pieces[piece] = gain_grad_ref[:, piece * width:(piece + 1) * width]
        gain_sums.begin()
        up_job.early()
        gain_sums.early()
        for copy in late:
            copy.wait()
        gain_sums.middle()
        sums.end()
        down_job.end()
        gain_sums.end()
        up_job.end()
    spread.finish()
    wire.end()


def feed_forward_back(sizes, name, collective_id, gain_row, grad, resid, gains, up, down_t, rows, pre,
                      leave=None, **side):
    n, m = sizes
    full, hidden = up.shape
    count = resid.shape[0]
    ins = [(item, vmem()) for item in (grad, resid, gains, up, down_t, rows, pre)]
    scratch = [
        pltpu.VMEM((n * count, full), BF16),
        pltpu.VMEM((n * count, hidden), BF16),
        pltpu.VMEM((n * count, hidden), BF16),
        pltpu.VMEM((n, count, full), BF16),
        pltpu.VMEM((n - 1, count, full), BF16),
    ]
    if leave:
        width, layers = full // n, m // 2
        heights = [leave[0].shape[1], leave[1].shape[0], leave[2].shape[0]]
        ins += [(item, vmem()) for item in leave]
        outs = [
            ((8, width), F32, vmem()),
            ((full // m, hidden), F32, vmem()),
            ((full // m, hidden), F32, vmem()),
            ((n * count, width), BF16, anywhere()),
            ((sum(heights), width), F32, vmem()),
        ]
        scratch += [
            pltpu.VMEM((8, full), F32),
            pltpu.VMEM((full, hidden), BF16),
            pltpu.VMEM((full, hidden), BF16),
        ]
        scratch += 2 * reduce_scratch(layers, full // m, hidden)
        scratch += sum_scratch(n, layers, *heights, width)
        scratch += [pltpu.VMEM((n, 8, width), F32)]
        scratch += sum_scratch(n, layers, 8, 0, 0, width)
        scratch += [pltpu.VMEM((count, full), F32), pltpu.VMEM((n, count, width), BF16)]
        side = dict(side, more_slots=8 * m + 8 * n, row_on=True)
    else:
        outs = [
            ((8, full), F32, vmem()),
            ((full, hidden), BF16, vmem()),
            ((full, hidden), BF16, vmem()),
            ((count, full), F32, vmem()),
        ]
    return comm_call(
        name, collective_id, sizes,
        functools.partial(feed_forward_back_main, count, gain_row, bool(leave)),
        ins, outs, scratch, **side,
    )


def extend_table(table):
    slots = jnp.arange(SPAN)
    signed = jnp.where(slots < SPAN - BLOCK + 1, slots, slots - SPAN)
    row_of = jnp.clip(signed - (BLOCK - LEFT), 0, LEFT + RIGHT)
    chosen = (row_of[:, None] == jnp.arange(LEFT + RIGHT + 1)[None, :]).astype(table.dtype)
    return jnp.dot(chosen, table, preferred_element_type=F32).astype(table.dtype)


def fold_table(extended):
    slots = jnp.arange(SPAN)
    signed = jnp.where(slots < SPAN - BLOCK + 1, slots, slots - SPAN)
    row_of = jnp.clip(signed - (BLOCK - LEFT), 0, LEFT + RIGHT)
    ends = jnp.repeat(jnp.asarray([0, LEFT + RIGHT]), 8)
    row_of = jnp.concatenate([row_of, ends])
    chosen = (jnp.arange(LEFT + RIGHT + 1)[:, None] == row_of[None, :]).astype(F32)
    return jnp.dot(chosen, extended, precision=lax.Precision.HIGHEST)


def column_facts(at, length, limit):
    column = lax.broadcasted_iota(jnp.int32, (1, length), 1)
    place = column + (at - BLOCK)
    key = jnp.where(place < 0, place + length, jnp.where(place >= length, place - length, place))
    return column, place, key, key < limit


def position_terms(query, table_ref, at, length):
    terms = matmul_nt(query, table_ref[...])
    rolled = pltpu.roll(terms, 0, 1, stride=1, stride_axis=0)
    column, place, key, _ = column_facts(at, length, length)
    far_left, far_right = terms[:, 0:1], terms[:, SPAN - 2 * BLOCK:SPAN - 2 * BLOCK + 1]
    far = jnp.where(key < at, far_left, far_right)
    near = jnp.where((place[:, :WINDOW] >= 0) & (place[:, :WINDOW] < length), rolled[:, :WINDOW],
                     far[:, :WINDOW])
    return jnp.concatenate([near, far[:, WINDOW:]], axis=1)


def head_mask(group, head, rows):
    if group == HEAD_DIM:
        return None
    lane = lax.broadcasted_iota(jnp.int32, (rows, group), 1)
    return (lane >= head * HEAD_DIM) & (lane < (head + 1) * HEAD_DIM)


def masked(mask, values):
    return values if mask is None else jnp.where(mask, values, jnp.zeros_like(values))


def lanes(start, size):
    return pl.ds(start, size)


def duplicate(qkv_ref, width, group, keys, values):
    length = qkv_ref.shape[0]
    for part in range(width // group):
        base = part * group
        for copy in range(2):
            place = slice(copy * length, (copy + 1) * length)
            keys[part, place] = qkv_ref[:, lanes(width + base, group)]
            values[part, place] = qkv_ref[:, lanes(2 * width + base, group)]


def attend_blocks(first, blocks, width, group, limit, qkv_ref, table_ref, keys, values, context_ref,
                  log_ref):
    length = qkv_ref.shape[0]
    heads = group // HEAD_DIM
    scale = 1.0 / math.sqrt(HEAD_DIM)

    def block(index, carry):
        at = pl.multiple_of((first + index) * BLOCK, BLOCK)
        rows = pl.ds(at, BLOCK)
        from_row = pl.multiple_of(lax.rem(at + length - BLOCK, length), BLOCK)
        _, _, _, allowed = column_facts(at, length, limit)
        for part in range(width // group):
            base = part * group
            key_rows = keys[part, pl.ds(from_row, length)]
            value_rows = values[part, pl.ds(from_row, length)]
            query_rows = qkv_ref[rows, lanes(base, group)] * jnp.asarray(scale, BF16)
            result = None
            for head in range(heads):
                mask = head_mask(group, head, BLOCK)
                query = masked(mask, query_rows)
                scores = matmul_nt(query, key_rows) + position_terms(query, table_ref, at, length)
                scores = jnp.where(allowed, scores, NEG_FILL)
                peak = jnp.max(scores, axis=1, keepdims=True)
                weights = jnp.exp(scores - peak)
                total = jnp.sum(weights, axis=1, keepdims=True)
                piece = matmul(weights.astype(BF16), value_rows) * (1.0 / total)
                result = piece if result is None else jnp.where(mask, piece, result)
                slot = part * heads + head
                log_ref[rows, slot:slot + 1] = peak + jnp.log(total)
            context_ref[rows, lanes(base, group)] = result.astype(BF16)
        return carry

    lax.fori_loop(0, blocks, block, 0)


def attention_main(count, gain_row, wire, ins, outs, scratch):
    limit_ref, resid, keep_ref, gains_ref, weights, table_ref = ins
    after_ref, squares_ref, rows_ref, qkv_ref, context_ref, log_ref = outs
    keys, values, part, got = scratch
    width = context_ref.shape[1]
    group = keys.shape[2]
    wire.greet()
    wire.begin()
    norm_rows(wire, count, resid, gains_ref[gain_row:gain_row + 1], rows_ref)
    spread = Spread(wire, rows_ref, count)
    spread.start()
    collect = Collect(wire, got)
    spread.relay()
    wire.early()
    chunks = []
    for chunk, slot in spread.arrivals(relay=False):
        chunks.append((chunk, slot))
        rows = tile(chunk, count)
        left = rows_ref[rows]

        def project(cols, index):
            qkv_ref[rows, cols] = matmul(left, weights[:, cols]).astype(BF16)

        block_loop(3 * width, project)
    wire.middle()
    duplicate(qkv_ref, width, group, keys, values)
    limit = limit_ref[0]
    size = max(count, BLOCK)
    for chunk, slot in reversed(chunks):
        first = chunk * count // BLOCK
        attend_blocks(first, size // BLOCK, width, group, limit, qkv_ref, table_ref, keys, values,
                      context_ref, log_ref)
        target = part.at[wire.n - 1 if slot is None else slot]
        left = context_ref[tile(chunk, count)]

        def leave(cols, index):
            target[:, cols] = matmul_nt(left, weights[cols, 3 * width:]).astype(BF16)

        block_loop(weights.shape[0], leave)
        if slot is not None:
            collect.send(target, chunk, slot)
    collect.wait()
    residual(wire, count, 1.0, part.at[wire.n - 1], got, resid, keep_ref, after_ref, squares_ref)
    spread.finish()
    wire.end()


def attention(sizes, name, collective_id, gain_row, limit, resid, keep, gains, weights, table, **side):
    n, m = sizes
    count, full = resid.shape
    length, width = n * count, weights.shape[1] // 4
    group = min(2 * HEAD_DIM, width)
    return comm_call(
        name, collective_id, sizes, functools.partial(attention_main, count, gain_row),
        [(limit, pl.BlockSpec(memory_space=pltpu.SMEM))]
        + [(item, vmem()) for item in (resid, keep, gains, weights, table)],
        [
            ((count, full), F32, vmem()),
            ((16, full), F32, vmem()),
            ((length, full), BF16, vmem()),
            ((length, 3 * width), BF16, vmem()),
            ((length, width), BF16, vmem()),
            ((length, max(8, width // HEAD_DIM)), F32, vmem()),
        ],
        [
            pltpu.VMEM((width // group, 2 * length, group), BF16),
            pltpu.VMEM((width // group, 2 * length, group), BF16),
            pltpu.VMEM((n, count, full), BF16),
            pltpu.VMEM((n - 1, count, full), BF16),
        ],
        cost=20 * 10**9, **side,
    )


def attend_back_core(width, group, limit, qkv_ref, table_ref, log_ref, grad_ref, out_ref,
                     table_grad_ref, keys, values, key_grad, value_grad):
    length = qkv_ref.shape[0]
    heads = group // HEAD_DIM
    scale = 1.0 / math.sqrt(HEAD_DIM)
    duplicate(qkv_ref, width, group, keys, values)
    table_grad_ref[...] = jnp.zeros_like(table_grad_ref)
    down = lax.broadcasted_iota(jnp.int32, (BLOCK, BLOCK), 0)
    across = lax.broadcasted_iota(jnp.int32, (BLOCK, BLOCK), 1)
    reverse = jnp.where(down + across == BLOCK - 1, 1.0, 0.0).astype(BF16)
    first_row = table_ref[0:1].astype(F32)
    last_row = table_ref[SPAN - 2 * BLOCK:SPAN - 2 * BLOCK + 1].astype(F32)
    for part in range(width // group):
        base = part * group
        key_grad[...] = jnp.zeros_like(key_grad)
        value_grad[...] = jnp.zeros_like(value_grad)

        def block(index, carry, base=base, part=part):
            at = pl.multiple_of(index * BLOCK, BLOCK)
            rows = pl.ds(at, BLOCK)
            from_row = pl.multiple_of(lax.rem(at + length - BLOCK, length), BLOCK)
            window = pl.ds(from_row, length)
            key_rows = keys[part, window]
            value_rows = values[part, window]
            query_rows = qkv_ref[rows, lanes(base, group)] * jnp.asarray(scale, BF16)
            grad_rows = grad_ref[rows, lanes(base, group)]
            column, place, key, allowed = column_facts(at, length, limit)
            near = (place[:, :WINDOW] >= 0) & (place[:, :WINDOW] < length)
            is_left = key < at
            result = None
            for head in range(heads):
                mask = head_mask(group, head, BLOCK)
                query = masked(mask, query_rows)
                grad = masked(mask, grad_rows)
                slot = part * heads + head
                scores = matmul_nt(query, key_rows) + position_terms(query, table_ref, at, length)
                scores = jnp.where(allowed, scores, NEG_FILL)
                probs = jnp.exp(scores - log_ref[rows, slot:slot + 1])
                prob_grad = matmul_nt(grad, value_rows)
                row_dot = jnp.sum(probs * prob_grad, axis=1, keepdims=True)
                score_grad = (probs * (prob_grad - row_dot)).astype(BF16)
                value_grad[window] += matmul_tn(probs.astype(BF16), grad)
                key_grad[window] += matmul_tn(score_grad, query)
                wide = score_grad.astype(F32)
                near_grad = jnp.where(near, score_grad[:, :WINDOW], jnp.asarray(0.0, BF16))
                far_grad = jnp.concatenate(
                    [jnp.where(near, 0.0, wide[:, :WINDOW]), wide[:, WINDOW:]], axis=1
                )
                left_sum = jnp.sum(jnp.where(is_left, far_grad, 0.0), axis=1, keepdims=True)
                right_sum = jnp.sum(jnp.where(is_left, 0.0, far_grad), axis=1, keepdims=True)
                turned = jnp.concatenate(
                    [matmul(reverse, near_grad), jnp.zeros((BLOCK, SPAN - WINDOW), F32)], axis=1
                )
                turned = pltpu.roll(
                    turned, SPAN - (BLOCK - 1), 1, stride=1, stride_axis=0
                ).astype(BF16)
                near_term = matmul(turned, table_ref[...])
                high = near_term.astype(BF16)
                low = (near_term - high.astype(F32)).astype(BF16)
                far_term = left_sum * first_row + right_sum * last_row
                piece = (
                    matmul(score_grad, key_rows) + matmul(reverse, high) + matmul(reverse, low)
                    + far_term
                ) * scale
                result = piece if result is None else jnp.where(mask, piece, result)
                table_grad_ref[0:SPAN] += matmul_tn(turned, matmul(reverse, query).astype(BF16))
                query_wide = query.astype(F32)
                table_grad_ref[SPAN:SPAN + 8] += fold8(left_sum * query_wide)
                table_grad_ref[SPAN + 8:SPAN + 16] += fold8(right_sum * query_wide)
            out_ref[rows, lanes(base, group)] = result.astype(BF16)
            return carry

        lax.fori_loop(0, length // BLOCK, block, 0)
        out_ref[:, lanes(width + base, group)] = (
            key_grad[0:length] + key_grad[length:2 * length]
        ).astype(BF16)
        out_ref[:, lanes(2 * width + base, group)] = (
            value_grad[0:length] + value_grad[length:2 * length]
        ).astype(BF16)


def attention_back_main(count, gain_row, wire, ins, outs, scratch):
    limit_ref, grad_ref, resid, gains_ref, weights, table_ref, rows_ref, qkv_ref, context_ref, log_ref = ins
    gain_grad_ref, wide_ref, table_grad_ref, new_grad_ref = outs
    grads, context_grad, qkv_grad, keys, values, key_grad, value_grad, part, got = scratch
    width = context_ref.shape[1]
    group = keys.shape[2]
    wire.greet()
    wire.begin()
    cast_rows(wire, count, grad_ref, 1.0, grads)
    spread = Spread(wire, grads, count)
    spread.start()
    collect = Collect(wire, got)
    spread.relay()
    wire.early()
    chunks = []
    for chunk, slot in spread.arrivals(relay=False):
        chunks.append((chunk, slot))
        rows = tile(chunk, count)
        context_grad[rows] = matmul(grads[rows], weights[:, 3 * width:]).astype(BF16)
    wire.middle()
    attend_back_core(width, group, limit_ref[0], qkv_ref, table_ref, log_ref, context_grad, qkv_grad,
                     table_grad_ref, keys, values, key_grad, value_grad)
    for chunk, slot in reversed(chunks):
        target = part.at[wire.n - 1 if slot is None else slot]
        left = qkv_grad[tile(chunk, count)]

        def back(cols, index):
            target[:, cols] = matmul_nt(left, weights[cols, :3 * width]).astype(BF16)

        block_loop(weights.shape[0], back)
        if slot is not None:
            collect.send(target, chunk, slot)

    def weight_grads(rows, index):
        wide_ref[rows, :3 * width] = matmul_tn(rows_ref[:, rows], qkv_grad[...]).astype(BF16)
        wide_ref[rows, 3 * width:] = matmul_tn(grads[:, rows], context_ref[...]).astype(BF16)

    block_loop(weights.shape[0], weight_grads)
    collect.wait()
    residual_back(wire, count, part.at[wire.n - 1], got, grad_ref, resid,
                  gains_ref[gain_row:gain_row + 1], new_grad_ref, gain_grad_ref)
    spread.finish()
    wire.end()


def attention_back(sizes, name, collective_id, gain_row, limit, grad, resid, gains, weights, table, rows,
                   qkv, context, log_total, **side):
    n, m = sizes
    count, full = resid.shape
    length, width = context.shape
    group = min(2 * HEAD_DIM, width)
    return comm_call(
        name, collective_id, sizes, functools.partial(attention_back_main, count, gain_row),
        [(limit, pl.BlockSpec(memory_space=pltpu.SMEM))]
        + [(item, vmem()) for item in (grad, resid, gains, weights, table, rows, qkv, context, log_total)],
        [
            ((8, full), F32, vmem()),
            ((full, 4 * width), BF16, vmem()),
            ((SPAN + 16, group), F32, vmem()),
            ((count, full), F32, vmem()),
        ],
        [
            pltpu.VMEM((length, full), BF16),
            pltpu.VMEM((length, width), BF16),
            pltpu.VMEM((length, 3 * width), BF16),
            pltpu.VMEM((width // group, 2 * length, group), BF16),
            pltpu.VMEM((width // group, 2 * length, group), BF16),
            pltpu.VMEM((2 * length, group), F32),
            pltpu.VMEM((2 * length, group), F32),
            pltpu.VMEM((n, count, full), BF16),
            pltpu.VMEM((n - 1, count, full), BF16),
        ],
        cost=50 * 10**9, **side,
    )


PAD = 32
ROWS = 64


def shifted_sets(held, low, high, size):
    for residue in range(8):
        shifts = [shift for shift in range(low, high + 1) if shift % 8 == residue]
        if shifts:
            extent = shifts[-1] - residue + size
            moved = held[residue:residue + extent]
            for shift in shifts:
                yield shift, moved[shift - residue:shift - residue + size]


def stat_rows(blocks, first, second, stats_ref):
    lane = lax.broadcasted_iota(jnp.int32, (BLOCK, BLOCK), 1)
    both = jnp.where(lane == 0, first, jnp.where(lane == 1, second, 0.0))
    stats_ref[:, blocks] = both.T[0:8]


def stat_columns(stats):
    both = jnp.concatenate([stats, jnp.zeros((BLOCK - 8, BLOCK), F32)], axis=0).T
    return both[:, 0:1], both[:, 1:2]


class Stats:
    def __init__(self, wire, mine, got):
        self.wire, self.mine, self.got = wire, mine, got
        self.copies = [
            wire.remote(mine, got.at[step - 1], "col", lax.rem(wire.me + step, wire.n))
            for step in range(1, wire.n)
        ]

    def total(self):
        for copy in self.copies:
            copy.start()
        for copy in self.copies:
            copy.wait()
        total = self.mine[...]
        for step in range(self.wire.n - 1):
            total = total + self.got[step]
        return total


def token_blocks(length, body):
    def step(index, carry):
        body(tile(index, BLOCK), index)
        return carry

    lax.fori_loop(0, length // BLOCK, step, 0)


def convolution_main(count, gain_row, taps, wire, ins, outs, scratch):
    resid, keep_ref, keep_all, gains_ref, weights, kernel_ref, depth_ref = ins
    after_ref, squares_ref, rows_ref, pre_ref, mixed_ref, stats_ref = outs
    padded, stats_mine, stats_got, act, part, got = scratch
    length, width = mixed_ref.shape
    full = gains_ref.shape[1]
    wire.greet()
    wire.begin()
    norm_rows(wire, count, resid, gains_ref[gain_row:gain_row + 1], rows_ref)
    spread = Spread(wire, rows_ref, count)
    spread.start()
    collect = Collect(wire, got)
    stats = Stats(wire, stats_mine, stats_got)
    padded[0:PAD] = jnp.zeros((PAD, width), F32)
    spread.relay()
    wire.early()
    chunks = []
    for chunk, slot in spread.arrivals(relay=False):
        chunks.append((chunk, slot))
        rows = tile(chunk, count)
        left = rows_ref[rows]
        value_pre = matmul(left, weights[:, 0:width])
        gate_pre = matmul(left, weights[:, width:2 * width])
        pre_ref[rows, 0:width] = value_pre.astype(BF16)
        pre_ref[rows, width:2 * width] = gate_pre.astype(BF16)
        at = pl.multiple_of(chunk * count + PAD, PAD)
        padded[pl.ds(at, count)] = value_pre * jax.nn.sigmoid(gate_pre) * keep_all[rows]
    wire.middle()

    def mix(index, carry):
        held = padded[pl.ds(pl.multiple_of(index * ROWS, ROWS), ROWS + PAD)]
        total = jnp.zeros((ROWS, width), F32)
        for shift, moved in shifted_sets(held, PAD - taps + 1, PAD, ROWS):
            tap = shift - (PAD - taps + 1)
            total = total + moved * kernel_ref[tap:tap + 1]
        mixed_ref[tile(index, ROWS)] = total
        return carry

    lax.fori_loop(0, length // ROWS, mix, 0)

    def sums(rows, index):
        mixed = mixed_ref[rows]
        stat_rows(rows, jnp.sum(mixed, axis=1, keepdims=True),
                  jnp.sum(mixed * mixed, axis=1, keepdims=True), stats_mine)

    token_blocks(length, sums)
    total = stats.total() * (1.0 / full)
    inverse = lax.rsqrt(total[1:2] - total[0:1] * total[0:1] + EPSILON)
    stats_ref[...] = jnp.concatenate([total[0:1], inverse, total[2:]], axis=0)

    def activate(rows, index):
        mean, scale = stat_columns(stats_ref[:, rows])
        scaled = (mixed_ref[rows] - mean) * scale * depth_ref[...]
        act[rows] = (scaled * jax.nn.sigmoid(scaled)).astype(BF16)

    token_blocks(length, activate)
    for chunk, slot in reversed(chunks):
        target = part.at[wire.n - 1 if slot is None else slot]
        left = act[tile(chunk, count)]

        def leave(cols, index):
            target[:, cols] = matmul_nt(left, weights[cols, 2 * width:]).astype(BF16)

        block_loop(weights.shape[0], leave)
        if slot is not None:
            collect.send(target, chunk, slot)
    collect.wait()
    residual(wire, count, 1.0, part.at[wire.n - 1], got, resid, keep_ref, after_ref, squares_ref)
    spread.finish()
    wire.end()


def convolution(sizes, name, collective_id, gain_row, resid, keep, keep_all, gains, weights, kernel,
                depth_gain, **side):
    n, m = sizes
    count, full = resid.shape
    length, width = n * count, weights.shape[1] // 3
    return comm_call(
        name, collective_id, sizes,
        functools.partial(convolution_main, count, gain_row, kernel.shape[0]),
        [(item, vmem()) for item in (resid, keep, keep_all, gains, weights, kernel, depth_gain)],
        [
            ((count, full), F32, vmem()),
            ((16, full), F32, vmem()),
            ((length, full), BF16, vmem()),
            ((length, 2 * width), BF16, vmem()),
            ((length, width), F32, vmem()),
            ((8, length), F32, vmem()),
        ],
        [
            pltpu.VMEM((length + PAD, width), F32),
            pltpu.VMEM((8, length), F32),
            pltpu.VMEM((n - 1, 8, length), F32),
            pltpu.VMEM((length, width), BF16),
            pltpu.VMEM((n, count, full), BF16),
            pltpu.VMEM((n - 1, count, full), BF16),
        ],
        cost=15 * 10**9, **side,
    )


def convolution_back_main(count, gain_row, taps, wire, ins, outs, scratch):
    (grad_ref, resid, keep_all, gains_ref, weights, kernel_ref, depth_ref, rows_ref, pre_ref, mixed_ref,
     stats_ref) = ins
    gain_grad_ref, wide_ref, kernel_grad_ref, depth_grad_ref, new_grad_ref = outs
    (grads, padded, padded_grad, stats_mine, stats_got, sums_ref, act, pre_grad, part, got) = scratch
    length, width = mixed_ref.shape
    full = gains_ref.shape[1]
    wire.greet()
    wire.begin()
    cast_rows(wire, count, grad_ref, 1.0, grads)
    spread = Spread(wire, grads, count)
    spread.start()
    collect = Collect(wire, got)
    stats = Stats(wire, stats_mine, stats_got)
    padded[0:PAD] = jnp.zeros((PAD, width), F32)
    padded_grad[length:] = jnp.zeros((PAD, width), F32)
    sums_ref[...] = jnp.zeros_like(sums_ref)
    depth_grad_ref[...] = jnp.zeros_like(depth_grad_ref)
    spread.relay()

    def regate(rows, index):
        value_pre = pre_ref[rows, 0:width].astype(F32)
        gate_pre = pre_ref[rows, width:2 * width].astype(F32)
        at = pl.multiple_of(index * BLOCK + PAD, PAD)
        padded[pl.ds(at, BLOCK)] = value_pre * jax.nn.sigmoid(gate_pre) * keep_all[rows]

    token_blocks(length, regate)
    wire.early()
    chunks = []
    for chunk, slot in spread.arrivals(relay=False):
        chunks.append((chunk, slot))
        rows = tile(chunk, count)
        padded_grad[rows] = matmul(grads[rows], weights[:, 2 * width:])
    wire.middle()

    def first(rows, index):
        mean, scale = stat_columns(stats_ref[:, rows])
        normed = (mixed_ref[rows] - mean) * scale
        scaled = normed * depth_ref[...]
        sig = jax.nn.sigmoid(scaled)
        act[rows] = (scaled * sig).astype(BF16)
        scaled_grad = padded_grad[rows] * (sig + scaled * sig * (1.0 - sig))
        depth_grad_ref[...] += fold8(scaled_grad * normed)
        weighted = scaled_grad * depth_ref[...]
        padded_grad[rows] = weighted
        stat_rows(rows, jnp.sum(weighted, axis=1, keepdims=True),
                  jnp.sum(weighted * normed, axis=1, keepdims=True), stats_mine)

    token_blocks(length, first)
    total = stats.total() * (1.0 / full)
    stats_mine[...] = total

    def second(rows, index):
        mean, scale = stat_columns(stats_ref[:, rows])
        normed = (mixed_ref[rows] - mean) * scale
        one, two = stat_columns(stats_mine[:, rows])
        padded_grad[rows] = scale * (padded_grad[rows] - one - normed * two)

    token_blocks(length, second)

    def unmix(index, carry):
        rows = tile(index, ROWS)
        around = pl.ds(pl.multiple_of(index * ROWS, ROWS), ROWS + PAD)
        ahead = padded_grad[around]
        total = jnp.zeros((ROWS, width), F32)
        for shift, moved in shifted_sets(ahead, 0, taps - 1, ROWS):
            tap = taps - 1 - shift
            total = total + moved * kernel_ref[tap:tap + 1]
        here = ahead[0:ROWS]
        for shift, moved in shifted_sets(padded[around], PAD - taps + 1, PAD, ROWS):
            tap = shift - (PAD - taps + 1)
            sums_ref[tap * 8:(tap + 1) * 8] += fold8(here * moved)
        gate = jax.nn.sigmoid(pre_ref[rows, width:2 * width].astype(F32))
        through = total * keep_all[rows] * gate
        pre_grad[rows, 0:width] = through.astype(BF16)
        pre_grad[rows, width:2 * width] = (
            through * pre_ref[rows, 0:width].astype(F32) * (1.0 - gate)
        ).astype(BF16)
        return carry

    lax.fori_loop(0, length // ROWS, unmix, 0)
    for tap in range(taps):
        kernel_grad_ref[tap:tap + 1] = jnp.sum(sums_ref[tap * 8:(tap + 1) * 8], axis=0, keepdims=True)
    for chunk, slot in reversed(chunks):
        target = part.at[wire.n - 1 if slot is None else slot]
        left = pre_grad[tile(chunk, count)]

        def back(cols, index):
            target[:, cols] = matmul_nt(left, weights[cols, :2 * width]).astype(BF16)

        block_loop(weights.shape[0], back)
        if slot is not None:
            collect.send(target, chunk, slot)

    def weight_grads(rows, index):
        wide_ref[rows, :2 * width] = matmul_tn(rows_ref[:, rows], pre_grad[...]).astype(BF16)
        wide_ref[rows, 2 * width:] = matmul_tn(grads[:, rows], act[...]).astype(BF16)

    block_loop(weights.shape[0], weight_grads)
    collect.wait()
    residual_back(wire, count, part.at[wire.n - 1], got, grad_ref, resid,
                  gains_ref[gain_row:gain_row + 1], new_grad_ref, gain_grad_ref)
    spread.finish()
    wire.end()


def convolution_back(sizes, name, collective_id, gain_row, grad, resid, keep_all, gains, weights, kernel,
                     depth_gain, rows, pre, mixed, stats, **side):
    n, m = sizes
    count, full = resid.shape
    length, width = mixed.shape
    taps = kernel.shape[0]
    return comm_call(
        name, collective_id, sizes,
        functools.partial(convolution_back_main, count, gain_row, taps),
        [(item, vmem()) for item in (grad, resid, keep_all, gains, weights, kernel, depth_gain, rows, pre,
                                     mixed, stats)],
        [
            ((8, full), F32, vmem()),
            ((full, 3 * width), BF16, vmem()),
            ((taps, width), F32, vmem()),
            ((8, width), F32, vmem()),
            ((count, full), F32, vmem()),
        ],
        [
            pltpu.VMEM((length, full), BF16),
            pltpu.VMEM((length + PAD, width), F32),
            pltpu.VMEM((length + PAD, width), F32),
            pltpu.VMEM((8, length), F32),
            pltpu.VMEM((n - 1, 8, length), F32),
            pltpu.VMEM((8 * taps, width), F32),
            pltpu.VMEM((length, width), BF16),
            pltpu.VMEM((length, 2 * width), BF16),
            pltpu.VMEM((n, count, full), BF16),
            pltpu.VMEM((n - 1, count, full), BF16),
        ],
        cost=20 * 10**9, **side,
    )


def body(
    layer_input,
    clip_lengths,
    first_gain,
    first_up,
    first_down,
    attend_gain,
    query_weight,
    key_weight,
    value_weight,
    output_weight,
    distance_table,
    conv_gain,
    pointwise_value,
    pointwise_gate,
    depthwise_kernel,
    depthwise_gain,
    pointwise_out,
    second_gain,
    second_up,
    second_down,
    final_gain,
    output_cotangent,
):
    n = lax.axis_size("col")
    me = lax.axis_index("col")
    width, length = layer_input.shape
    full = n * width
    count = length // n

    sizes = (n, lax.axis_size("row"))
    attend_shard = jnp.concatenate([query_weight, key_weight, value_weight, output_weight.T], axis=1)
    conv_shard = jnp.concatenate([pointwise_value, pointwise_gate, pointwise_out.T], axis=1)

    keep_all = (jnp.arange(length)[:, None] < clip_lengths).astype(F32)
    keep = (jnp.arange(count)[:, None] + me * count < clip_lengths).astype(F32)
    blank = jnp.zeros_like(first_gain)
    gain_stack = jnp.stack(
        [first_gain, attend_gain, conv_gain, second_gain, final_gain, blank, blank, blank]
    )
    table_wide = extend_table(distance_table)
    group = min(2 * HEAD_DIM, width)
    table_wide = jnp.tile(table_wide, (1, group // HEAD_DIM))
    taps = depthwise_kernel.astype(F32)

    (start, cot, gains, up_first, down_first, attend_weights, after_first, squares_first, rows_first,
     pre_first) = feed_forward(
        sizes, "first", 1, 0, first_up, first_down.T, keep,
        enter=(layer_input.T, output_cotangent.T, gain_stack, attend_shard),
    )

    (after_attend, squares_attend, rows_attend, qkv, context, log_total, conv_weights,
     up_second) = attention(
        sizes, "attend", 2, 1, clip_lengths, after_first, keep, gains, attend_weights, table_wide,
        gathers=[conv_shard, second_up],
    )
    depth_row = depthwise_gain[None]
    (after_conv, squares_conv, rows_conv, conv_pre, mixed, stats, down_second) = convolution(
        sizes, "convolve", 3, 2, after_attend, keep, keep_all, gains, conv_weights, taps, depth_row,
        gathers=[second_down.T],
    )

    (grad_second, final_part, out_tokens, _, squares_second, rows_second, pre_second) = feed_forward(
        sizes, "second", 4, 3, up_second, down_second, keep, resid=after_conv, gains=gains, turn=cot
    )

    second_part, second_up_wide, second_down_wide, grad_conv = feed_forward_back(
        sizes, "second_back", 5, 3, grad_second, after_conv, gains, up_second, down_second,
        rows_second, pre_second,
    )

    (conv_part, conv_wide, kernel_part, depth_part, grad_attend, second_up_grad,
     second_down_grad) = convolution_back(
        sizes, "convolve_back", 6, 2, grad_conv, after_attend, keep_all, gains, conv_weights, taps,
        depth_row, rows_conv, conv_pre, mixed, stats, reduces=[second_up_wide, second_down_wide],
    )
    depth_part = jnp.sum(depth_part, axis=0)
    attend_part, attend_wide, table_part, grad_first, conv_grads = attention_back(
        sizes, "attend_back", 7, 1, clip_lengths, grad_attend, after_first, gains, attend_weights,
        table_wide, rows_attend, qkv, context, log_total, reduces=[conv_wide],
    )

    table_part = sum(
        table_part[:, at:at + HEAD_DIM] for at in range(0, group, HEAD_DIM)
    )
    table_part = fold_table(table_part)
    squares = jnp.stack(
        [
            jnp.sum(piece[at:at + 8])
            for at in (0, 8)
            for piece in (squares_first, squares_attend, squares_conv, squares_second)
        ]
    )
    lengths_sum = jnp.sum(clip_lengths).astype(F32) * (me == 0).astype(F32)
    token_parts = jnp.stack(
        [jnp.sum(piece, axis=0) for piece in (attend_part, conv_part, second_part, final_part)]
    )
    token_parts = jnp.pad(token_parts, ((0, 4), (0, 0))).reshape(8, n, width).transpose(1, 0, 2)
    loose = jnp.concatenate([table_part.reshape(-1), squares, lengths_sum[None]])
    loose_rows = -(-loose.shape[0] // (8 * width)) * 8
    loose = jnp.pad(loose, (0, loose_rows * width - loose.shape[0])).reshape(loose_rows, width)
    tap_count = kernel_part.shape[0]
    kept = jnp.concatenate([kernel_part, depth_part[None]])
    kept = jnp.pad(kept, ((0, -kept.shape[0] % 8), (0, 0)))

    (first_sum, first_up_grad, first_down_grad, grad_tokens, sums, attend_grads) = feed_forward_back(
        sizes, "first_back", 0, 0, grad_first, start, gains, up_first, down_first, rows_first,
        pre_first, leave=(token_parts, loose, kept), reduces=[attend_wide],
    )
    first_down_grad, second_down_grad = first_down_grad.T, second_down_grad.T
    mine = sums[:8]
    kept = sums[8 + loose_rows:]
    loose = sums[8:8 + loose_rows].reshape(-1)
    table_size = table_part.size
    table_sum = loose[:table_size].reshape(table_part.shape)
    square_sums = loose[table_size:table_size + 8]
    masked_rms = jnp.sqrt(square_sums / (loose[table_size + 8] * full))

    return (
        out_tokens.T,
        grad_tokens.T.astype(F32),
        jnp.sum(first_sum, axis=0),
        first_up_grad,
        first_down_grad,
        mine[0],
        attend_grads[:, :width],
        attend_grads[:, width:2 * width],
        attend_grads[:, 2 * width:3 * width],
        attend_grads[:, 3 * width:].T,
        table_sum,
        mine[1],
        conv_grads[:, :width],
        conv_grads[:, width:2 * width],
        kept[:tap_count],
        kept[tap_count],
        conv_grads[:, 2 * width:].T,
        mine[2],
        second_up_grad,
        second_down_grad,
        mine[3],
        masked_rms,
    )


def solution(mesh):
    in_specs = (
        P("col", "row"),
        P("row"),
        P("col"),
        P("row", "col"),
        P("col", "row"),
        P("col"),
        P("row", "col"),
        P("row", "col"),
        P("row", "col"),
        P("col", "row"),
        P(),
        P("col"),
        P("row", "col"),
        P("row", "col"),
        P(None, "col"),
        P("col"),
        P("col", "row"),
        P("col"),
        P("row", "col"),
        P("col", "row"),
        P("col"),
        P("col", "row"),
    )
    out_specs = (
        P("col", "row"),
        P("col", "row"),
        P("col"),
        P("row", "col"),
        P("col", "row"),
        P("col"),
        P("row", "col"),
        P("row", "col"),
        P("row", "col"),
        P("col", "row"),
        P(),
        P("col"),
        P("row", "col"),
        P("row", "col"),
        P(None, "col"),
        P("col"),
        P("col", "row"),
        P("col"),
        P("row", "col"),
        P("col", "row"),
        P("col"),
        P(),
    )
    return jax.shard_map(body, mesh=mesh, in_specs=in_specs, out_specs=out_specs, check_vma=False)
```

time: 1960 us -> 673 us (0.34)
  waiting for transfers between devices: 984 us -> 0 us
  Pallas kernels: 0 us -> 613 us
  local copies, waits for them, and re-layouts: 414 us -> 28.1 us
  blocking collectives: 219 us -> 0 us
  matrix products: 206 us -> 1.66 us
  other arithmetic: 103 us -> 17.6 us
    reduce_scatter x16 -> x0, waiting for transfers between devices: 617 us -> none  [the longest x4 203 us: reduce_cols(): lax.psum_scatter(matmul(activated, weight_full), 'col', scatter_dimension...]
    pallas_call x0 -> x8, Pallas kernels: none -> 613 us  [comm_call(): pl.pallas_call(kernel, name=name, out_shape=tuple(out_shapes), in_specs=i...]
    all_gather x14 -> x0, waiting for transfers between devices: 365 us -> none  [the longest x4 139 us: normed_rows(): lax.all_gather((normed * gains).astype(jnp.bfloat16), 'col', axis=1, tile...]
    dot_general x77 -> x2, matrix products: 206 us -> 1.66 us  [the longest x1 1.4 us: fold_table(): return jnp.dot(chosen, extended, precision=lax.Precision.HIGHEST)]
    reshape x29 -> x3, local copies, waits for them, and re-layouts: 184 us -> 0.78 us  [the longest x1 0.62 us: body(): jnp.pad(loose, (0, loose_rows * width - loose.shape[0]))]
    psum x14 -> x0, blocking collectives: 182 us -> none  [the longest x6 56.8 us: norm_forward(): lax.psum((jnp.sum(hidden, axis=1), jnp.sum(hidden * hidden, axis=1)), 'col')]
    slice x27 -> x5, local copies, waits for them, and re-layouts: 73.6 us -> 3.46 us  [the longest x1 1.43 us: body(): mine[3]]
    while x48 -> x0, local copies, waits for them, and re-layouts: 66.9 us -> none
  transfers between devices with their start and end apart: 30 -> 0, of which waited for: 26 -> 0; matrix products, arithmetic and copies ran while one was open for 5% -> 0% of each run, Pallas kernels for 0% -> 0%
where the time goes in v1:
time: 673 us; the launch traced here: 663 us
  Pallas kernels  613 us (91%)
  local copies, waits for them, and re-layouts  28.1 us (4%)
  other arithmetic  17.6 us (3%)
    pallas_call x8, Pallas kernels, comm_call(): pl.pallas_call(kernel, name=name, out_shape=tuple(out_shapes), in_specs=i...  613 us
    unnamed x47, local copies, waits for them, and re-layouts  15.5 us

profile of v1, /device:TPU:0, one launch (start us, length us, event | category | flops | bytes accessed | tf_op | source)
XLA Modules:
  0.0 662.6 jit_solution(13400182730699896402)
XLA Ops:
  0.7 0.0 copy-start
  0.7 0.0 copy-start.10
  0.7 0.0 copy-start.9
  0.7 0.0 copy-start.2
  1.5 0.1 broadcast_in_dim.9
  1.5 0.1 reshape.113
  1.6 1.4 stack.66.refs_2_
  3.0 1.3 convert_element_type.31.refs_5_
  4.3 0.0 copy-done
  4.3 0.3 convolution_convert_fusion
  4.6 0.0 copy-start.3
  4.6 0.8 copy.64.refs_5_
  5.4 0.9 copy.62
  6.4 0.9 copy.63
  7.3 0.7 fusion.6.refs_3_.refs_2_.refs_1_
  8.0 1.6 pad_maximum_fusion.1.refs_6_
  9.6 1.6 pad_maximum_fusion.refs_6_
  11.2 0.0 copy-done.9
  11.2 0.8 copy.61
  12.0 0.0 copy-done.10
  12.0 0.8 copy.65
  12.9 0.8 fusion.refs_2_
  13.7 1.0 copy.59
  14.7 0.0 copy-done.3
  14.7 1.0 copy.60
  15.7 84.8 %first.1 = (f32[256,1024]{1,0:T(8,128)}, f32[256,1024]{1,0:T(8,128)}, f32[8,1024]{1,0:T(8,128)}, bf16[1024,1024]{1,0:T(8,128)(2,1)}, bf16[1024,1024]{1,0:T(8,128...) custom-call(bf16[1024,256]{1,0:T(8,128)(2,1)} %bitcast.55, ...), custom_call_target="tpu_custom_call" | custom-call | flops 1000000000 | bytes 100000000 | tf_op jit(solution)/shard_map/first/pallas_call | solution.py:484
  100.5 1.4 slice_reduce_fusion.3
  101.9 80.6 %attend.1 = (f32[256,1024]{1,0:T(8,128)}, f32[16,1024]{1,0:T(8,128)}, bf16[1024,1024]{1,0:T(8,128)(2,1)}, bf16[1024,768]{1,0:T(8,128)(2,1)}, bf16[1024,256]{1,0:...) custom-call(s32[1]{0:T(128)} %copy.79.refs_0_, ...), custom_call_target="tpu_custom_call" | custom-call | flops 20000000000 | bytes 100000000 | tf_op jit(solution)/shard_map/attend/pallas_call | solution.py:484
  182.5 1.4 slice_reduce_fusion.2
  183.9 70.7 %convolve.1 = (f32[256,1024]{1,0:T(8,128)}, f32[16,1024]{1,0:T(8,128)}, bf16[1024,1024]{1,0:T(8,128)(2,1)}, bf16[1024,512]{1,0:T(8,128)(2,1)}, f32[1024,256]{1,0...) custom-call(f32[256,1024]{1,0:T(8,128)} %get-tuple-element.78.refs_0_.refs_1_, ...), custom_call_target="tpu_custom_call" | custom-call | flops 15000000512 | bytes 100000000 | tf_op jit(solution)/shard_map/convolve/pallas_call | solution.py:484
  254.6 1.4 slice_reduce_fusion.1
  256.0 61.3 %second.1 = (f32[256,1024]{1,0:T(8,128)}, f32[8,1024]{1,0:T(8,128)}, bf16[1024,256]{1,0:T(8,128)(2,1)}, f32[256,1024]{1,0:T(8,128)}, f32[16,1024]{1,0:T(8,128)},...) custom-call(f32[256,1024]{1,0:T(8,128)} %get-tuple-element.80.refs_0_.refs_1_, ...), custom_call_target="tpu_custom_call" | custom-call | flops 1000000000 | bytes 100000000 | tf_op jit(solution)/shard_map/second/pallas_call | solution.py:484
  317.3 2.0 copy.68
  319.3 1.4 slice_reduce_fusion
  320.7 0.8 reduce_sum.133
  321.5 52.3 %second_back.1 = (f32[8,1024]{1,0:T(8,128)}, bf16[1024,1024]{1,0:T(8,128)(2,1)}, bf16[1024,1024]{1,0:T(8,128)(2,1)}, f32[256,1024]{1,0:T(8,128)}) custom-call(f32[256,1024]{1,0:T(8,128)} %get-tuple-element.85.refs_0_, f32[256,1024]{1,0:T(8,128)} %get-tuple-element.80.refs_0_.refs_1_, f32[8,1024]{1,0:T(8,128)} %get-tuple-element.76.refs_3_.refs_2_, ...), custom_call_target="tpu_custom_call" | custom-call | flops 1000000000 | bytes 100000000 | tf_op jit(solution)/shard_map/second_back/pallas_call | solution.py:484
  373.8 71.0 %convolve_back.1 = (f32[8,1024]{1,0:T(8,128)}, bf16[1024,768]{1,0:T(8,128)(2,1)}, f32[31,256]{1,0:T(8,128)}, f32[8,256]{1,0:T(8,128)}, f32[256,1024]{1,0:T(8,128...) custom-call(f32[256,1024]{1,0:T(8,128)} %get-tuple-element.88.refs_0_, f32[256,1024]{1,0:T(8,128)} %get-tuple-element.78.refs_0_.refs_1_, ...), custom_call_target="tpu_custom_call" | custom-call | flops 20000000000 | bytes 100000000 | tf_op jit(solution)/shard_map/convolve_back/pallas_call | solution.py:484
  444.8 97.6 %attend_back.1 = (f32[8,1024]{1,0:T(8,128)}, bf16[1024,1024]{1,0:T(8,128)(2,1)}, f32[528,128]{1,0:T(8,128)}, f32[256,1024]{1,0:T(8,128)}, f32[128,768]{1,0:T(8,128)}) custom-call(s32[1]{0:T(128)} %copy.79.refs_0_, f32[256,1024]{1,0:T(8,128)} %get-tuple-element.95.refs_1_, f32[256,1024]{1,0:T(8,128)} %get-tuple-element.75.refs_1_.refs_2_, ...), custom_call_target="tpu_custom_call" | custom-call | flops 49999998976 | bytes 100000000 | tf_op jit(solution)/shard_map/attend_back/pallas_call | solution.py:484
  542.5 0.6 pad_maximum_fusion.2.refs_9_
  543.1 0.8 reduce_sum.130
  543.9 0.6 select_maximum_fusion
  544.6 1.4 fusion.1
  546.0 0.1 reshape.114
  546.0 5.3 concatenate.18
  551.3 0.6 reshape.115.refs_8_
  551.9 94.5 %first_back.1 = (f32[8,256]{1,0:T(8,128)}, f32[128,1024]{1,0:T(8,128)}, f32[128,1024]{1,0:T(8,128)}, bf16[1024,256]{1,0:T(8,128)(2,1)}, f32[64,256]{1,0:T(8,128)}, /*index=5*/f32[128,1024]{1,0:T(8,128)}) custom-call(f32[256,1024]{1,0:T(8,128)} %get-tuple-element.101.refs_0_, f32[256,1024]{1,0:T(8,128)} %get-tuple-element.102.refs_1_, ...), custom_call_target="tpu_custom_call" | custom-call | flops 1000000000 | bytes 100000000 | tf_op jit(solution)/shard_map/first_back/pallas_call | solution.py:484
  646.5 1.3 reduce_sum.143
  647.8 1.4 fusion.11
  649.2 1.4 slice.113
  650.6 0.7 slice_bitcast_fusion.2
  651.4 0.6 slice.122
  652.6 0.6 fusion.10
  653.2 0.1 slice.108
  653.3 0.7 copy.72
  654.0 1.2 convert_bitcast_fusion
  655.2 1.3 copy.69
  656.5 1.0 copy.70
  657.5 1.0 copy.74
  658.5 0.0 copy-done.1
  658.5 0.8 slice_bitcast_fusion
  659.3 0.8 copy.73
  660.1 0.8 copy.71
  660.8 0.8 copy.80
  661.6 0.8 copy.81
  (32 shorter events, 0.2 us)
Async XLA Ops:
  0.7 3.7 copy-start
  0.7 11.4 %copy-start.10 = (bf16[1024,128]{1,0:T(8,128)(2,1)S(1)}, bf16[1024,128]{1,0:T(8,128)(2,1)}, u32[]{:S(2)}) copy-start(bf16[1024,128]{1,0:T(8,128)(2,1)} %param.42) | copy-start | bytes 786436
  0.7 10.5 %copy-start.9 = (bf16[1024,128]{1,0:T(8,128)(2,1)S(1)}, bf16[1024,128]{1,0:T(8,128)(2,1)}, u32[]{:S(2)}) copy-start(bf16[1024,128]{1,0:T(8,128)(2,1)} %param.27) | copy-start | bytes 786436
  0.7 13.0 %copy-start.2 = (bf16[256,1024]{1,0:T(8,128)(2,1)S(1)}, bf16[256,1024]{1,0:T(8,128)(2,1)}, u32[]{:S(2)}) copy-start(bf16[256,1024]{1,0:T(8,128)(2,1)} %param.23) | copy-start | bytes 1572868
  4.6 10.1 %copy-start.3 = (bf16[256,1024]{1,0:T(8,128)(2,1)S(1)}, bf16[256,1024]{1,0:T(8,128)(2,1)}, u32[]{:S(2)}) copy-start(bf16[256,1024]{1,0:T(8,128)(2,1)} %param.44) | copy-start | bytes 1572868
  444.8 97.6 %copy-start.14 = (f32[8,256]{1,0:T(8,128)S(1)}, f32[8,256]{1,0:T(8,128)}, u32[]{:S(2)}) copy-start(f32[8,256]{1,0:T(8,128)} %get-tuple-element.117) | copy-start | bytes 24580
  444.8 97.6 %copy-start.13 = (f32[31,256]{1,0:T(8,128)S(1)}, f32[31,256]{1,0:T(8,128)}, u32[]{:S(2)}) copy-start(f32[31,256]{1,0:T(8,128)} %get-tuple-element.116) | copy-start | bytes 95236
  444.8 99.0 %copy-start.12 = (f32[8,1024]{1,0:T(8,128)S(1)}, f32[8,1024]{1,0:T(8,128)}, u32[]{:S(2)}) copy-start(f32[8,1024]{1,0:T(8,128)} %get-tuple-element.108) | copy-start | bytes 98308
  444.8 99.1 %copy-start.11 = (f32[8,1024]{1,0:T(8,128)S(1)}, f32[8,1024]{1,0:T(8,128)}, u32[]{:S(2)}) copy-start(f32[8,1024]{1,0:T(8,128)} %get-tuple-element.109) | copy-start | bytes 98308
  646.5 10.0 %copy-start.7 = (f32[128,1024]{1,0:T(8,128)S(1)}, f32[128,1024]{1,0:T(8,128)}, u32[]{:S(2)}) copy-start(f32[128,1024]{1,0:T(8,128)} %get-tuple-element.122) | copy-start | bytes 1572868
  654.0 3.5 copy-start.5
  655.1 3.3 copy-start.1
  655.2 3.3 copy-start.8
  656.5 4.4 copy-start.6
  657.5 4.1 copy-start.4

commit v2 on v1

v2 whole, which is shorter than its diff:
```python
import functools
import math

import jax
import jax.numpy as jnp
from jax import lax
from jax.experimental import pallas as pl
from jax.experimental.pallas import tpu as pltpu
from jax.sharding import PartitionSpec as P

HEAD_DIM = 64
LEFT = 64
RIGHT = 8
EPSILON = 1e-05
NEG_FILL = -1e30
BF16 = jnp.bfloat16
F32 = jnp.float32
MESH = pl.DeviceIdType.MESH
BLOCK = 128
WINDOW = 384
SPAN = 512
VMEM_LIMIT = 60 * 1024 * 1024
MARGIN = 6 * 1024 * 1024


def matmul(left, right):
    return jnp.dot(left, right, preferred_element_type=F32)


def matmul_nt(left, right):
    return lax.dot_general(left, right, (((1,), (1,)), ((), ())), preferred_element_type=F32)


def matmul_tn(left, right):
    return lax.dot_general(left, right, (((0,), (0,)), ((), ())), preferred_element_type=F32)


def vmem():
    return pl.BlockSpec(memory_space=pltpu.VMEM)


def smem():
    return pl.BlockSpec(memory_space=pltpu.SMEM)


def hbm():
    return pl.BlockSpec(memory_space=pltpu.HBM)


def padded_bytes(shape, dtype):
    size = jnp.dtype(dtype).itemsize
    rows = 8 * 4 // size
    shape = (1,) * (2 - len(shape)) + tuple(shape)
    held = -(-shape[-1] // 128) * 128 * -(-shape[-2] // rows) * rows
    return math.prod(shape[:-2]) * held * size


def comm_params(collective_id, held):
    return pltpu.CompilerParams(
        collective_id=collective_id, has_side_effects=True,
        vmem_limit_bytes=max(VMEM_LIMIT, held + MARGIN),
    )


def tile(index, size):
    return pl.ds(pl.multiple_of(index * size, size), size)


class Wire:
    def __init__(self, sizes, send_sem, recv_sem, local_sem, side, col_on=True, row_on=False):
        self.n, self.m = sizes
        self.me = lax.axis_index("col")
        self.row = lax.axis_index("row")
        self.send_sem, self.recv_sem, self.local_sem = send_sem, recv_sem, local_sem
        self.used = 0
        self.used_local = 0
        self.core = lax.rem(self.row, 2)
        self.layer = self.row // 2
        self.partner = self.row + 1 - 2 * self.core
        self.layers = self.m // 2
        self.col_on = col_on
        self.loads, self.stores, self.stored = [], [], []
        self.row_on = row_on or bool(side)
        self.side = [job(self) for job in side]

    def layer_peer(self, step):
        return lax.rem(self.layer + step, self.layers) * 2 + self.core

    def greet(self):
        barrier = pltpu.get_barrier_semaphore()
        waits = 0
        if self.col_on:
            for step in range(1, self.n):
                pl.semaphore_signal(
                    barrier, inc=1, device_id={"col": lax.rem(self.me + step, self.n)},
                    device_id_type=MESH,
                )
            waits += self.n - 1
        if self.row_on:
            for step in range(1, self.layers):
                pl.semaphore_signal(
                    barrier, inc=1, device_id={"row": self.layer_peer(step)}, device_id_type=MESH
                )
            pl.semaphore_signal(
                barrier, inc=1, device_id={"row": self.partner}, device_id_type=MESH
            )
            waits += self.layers
        pl.semaphore_wait(barrier, waits)

    def remote(self, source, target, axis, peer):
        slot = self.used
        self.used += 1
        return pltpu.make_async_remote_copy(
            src_ref=source, dst_ref=target, send_sem=self.send_sem.at[slot],
            recv_sem=self.recv_sem.at[slot], device_id={axis: peer}, device_id_type=MESH,
        )

    def local(self, source, target):
        slot = self.used_local
        self.used_local += 1
        return pltpu.make_async_copy(source, target, self.local_sem.at[slot])

    def to_all(self, source_of, target):
        copies = [
            self.remote(source_of(lax.rem(self.me + step, self.n)), target, "col",
                        lax.rem(self.me + step, self.n))
            for step in range(1, self.n)
        ]
        for copy in copies:
            copy.start()
        return copies

    def loaded(self):
        for copy in self.loads:
            copy.wait()

    def store(self, copies):
        for copy in copies:
            copy.start()
        self.stored += copies

    def flush(self):
        self.store(self.stores)

    def settle(self):
        for copy in self.stored:
            copy.wait()

    def begin(self):
        for job in self.side:
            job.begin()

    def early(self):
        for job in self.side:
            job.early()

    def middle(self):
        for job in self.side:
            job.middle()

    def end(self):
        for job in self.side:
            job.end()

    def peers(self):
        if self.n == 4:
            across = self.me + 1 - 2 * lax.rem(self.me, 2)
            along = lax.rem(self.me + 2, 4)
            return [(across, 0), (along, 1), (3 - self.me, 2)]
        return [
            (lax.rem(self.me + self.n - step, self.n), self.n - step - 1)
            for step in range(1, self.n)
        ]


class Spread:
    def __init__(self, wire, ref, count):
        self.wire, self.ref, self.count = wire, ref, count
        me = wire.me
        if wire.n != 4:
            self.copies = [
                wire.remote(self.part(me), self.part(me), "col", lax.rem(me + step, wire.n))
                for step in range(1, wire.n)
            ]
            return
        (across, _), (along, _), (far, _) = wire.peers()
        self.across = [wire.remote(self.part(me, q), self.part(me, q), "col", across) for q in range(4)]
        self.along = [wire.remote(self.part(me, q), self.part(me, q), "col", along) for q in range(4)]
        self.onward = [
            wire.remote(self.part(across, q), self.part(across, q), "col", along) for q in (0, 1)
        ] + [wire.remote(self.part(along, q), self.part(along, q), "col", across) for q in (2, 3)]

    def part(self, chunk, quarter=None):
        if quarter is None:
            return self.ref.at[tile(chunk, self.count)]
        size = self.count // 4
        return self.ref.at[tile(chunk * 4 + quarter, size)]

    def start(self):
        if self.wire.n != 4:
            for copy in self.copies:
                copy.start()
            return
        for first, second in ((0, 2), (1, 3), (2, 0), (3, 1)):
            self.across[first].start()
            self.along[second].start()

    def relay(self):
        if self.wire.n != 4:
            return
        for turn in range(2):
            self.across[turn].wait_recv()
            self.onward[turn].start()
            self.along[2 + turn].wait_recv()
            self.onward[2 + turn].start()

    def arrivals(self, relay=True):
        wire = self.wire
        yield wire.me, None
        if wire.n != 4:
            for step, (peer, slot) in zip(range(1, wire.n), wire.peers()):
                self.copies[step - 1].wait_recv()
                yield peer, slot
            return
        if relay:
            self.relay()
        for (peer, slot), copies in zip(
            wire.peers(), (self.across[2:], self.along[:2], self.onward)
        ):
            for copy in copies:
                copy.wait_recv()
            yield peer, slot

    def finish(self):
        copies = self.copies if self.wire.n != 4 else self.across + self.along + self.onward
        for copy in copies:
            copy.wait_send()


class Collect:
    def __init__(self, wire, part, got):
        self.wire, self.part, self.got = wire, part, got
        self.relayed = wire.n == 4
        self.count = part.shape[1]
        if not self.relayed:
            self.copies = {
                slot: wire.remote(part.at[slot], got.at[slot], "col", owner)
                for owner, slot in wire.peers()
            }
            return
        (across, _), (along, _), _ = wire.peers()
        half = self.count // 2
        first, second = pl.ds(0, half), pl.ds(half, half)
        places = [got.at[place // 2, (first, second)[place % 2]] for place in range(6)]
        self.far = [
            wire.remote(part.at[2, first], places[0], "col", across),
            wire.remote(part.at[2, second], places[1], "col", along),
        ]
        self.direct = {
            0: wire.remote(part.at[0, first], places[2], "col", across),
            1: wire.remote(part.at[1, second], places[4], "col", along),
        }
        self.onward = [
            wire.remote(part.at[0, second], places[3], "col", across),
            wire.remote(part.at[1, first], places[5], "col", along),
        ]

    def send(self, slot):
        if not self.relayed:
            self.copies[slot].start()
        elif slot == 2:
            for copy in self.far:
                copy.start()
        else:
            self.direct[slot].start()

    def combine(self):
        if not self.relayed:
            return
        half = self.count // 2
        for copy, slot, at, onward in (
            (self.far[1], 0, half, self.onward[0]), (self.far[0], 1, 0, self.onward[1])
        ):
            copy.wait_recv()
            place = 1 - slot

            def add(rows, index):
                mine = pl.ds(pl.multiple_of(at + index * 32, 32), 32)
                came = pl.ds(pl.multiple_of((half if place else 0) + index * 32, 32), 32)
                self.part[slot, mine] = (
                    self.part[slot, mine].astype(F32) + self.got[0, came].astype(F32)
                ).astype(BF16)

            row_loop(half, add)
            onward.start()

    def wait(self):
        if not self.relayed:
            for copy in self.copies.values():
                copy.wait()
            return
        for copy in self.far:
            copy.wait_send()
        for copy in list(self.direct.values()) + self.onward:
            copy.wait()

    def sum_loop(self, body):
        part, got, last = self.part, self.got, self.wire.n - 1
        if not self.relayed:
            def step(rows, index):
                total = part[last, rows].astype(F32)
                for slot in range(last):
                    total = total + got[slot, rows].astype(F32)
                body(rows, total)

            row_loop(self.count, step)
            return
        half = self.count // 2
        for at, sources in ((0, ((1, 0), (2, half))), (half, ((1, half), (2, 0)))):
            def step(rows, index, at=at, sources=sources):
                mine = pl.ds(pl.multiple_of(at + index * 32, 32), 32)
                total = part[last, mine].astype(F32)
                for slot, start in sources:
                    total = total + got[
                        slot, pl.ds(pl.multiple_of(start + index * 32, 32), 32)
                    ].astype(F32)
                body(mine, total)

            row_loop(half, step)


class RowChain:
    def __init__(self, shard, full, wire):
        self.wire, self.shard, self.full = wire, shard, full
        self.count = shard.shape[0]
        self.steps = wire.layers - 1
        self.base = wire.used
        wire.used += 4 * self.steps
        mine = full.at[tile(wire.row, self.count)]
        self.own = [wire.local(shard, mine), wire.remote(shard, mine, "row", wire.partner)]

    def block(self, layer):
        return self.full.at[tile(layer * 2 + self.wire.core, self.count)]

    def copy(self, kind, step, layer, peer):
        slot = self.base + kind * self.steps + step
        wire = self.wire
        source = self.shard if kind < 2 and step == 0 else self.block(layer)
        return pltpu.make_async_remote_copy(
            src_ref=source, dst_ref=self.block(layer), send_sem=wire.send_sem.at[slot],
            recv_sem=wire.recv_sem.at[slot], device_id={"row": peer}, device_id_type=MESH,
        )

    def up(self, step):
        wire = self.wire
        return self.copy(0, step, wire.layer - step, wire.row + 2)

    def down(self, step):
        wire = self.wire
        return self.copy(1, step, wire.layer + step, wire.row - 2)

    def begin(self):
        wire = self.wire
        pl.when(wire.layer + 1 < wire.layers)(lambda: self.up(0).start())
        pl.when(wire.layer > 0)(lambda: self.down(0).start())
        for copy in self.own:
            copy.start()

    def advance(self, step):
        wire = self.wire

        @pl.when(wire.layer - 1 - step >= 0)
        def _():
            self.copy(0, step, wire.layer - 1 - step, wire.row).wait_recv()
            if step + 1 < self.steps:
                pl.when(wire.layer + 1 < wire.layers)(lambda: self.up(step + 1).start())
            self.copy(2, step, wire.layer - 1 - step, wire.partner).start()

        @pl.when(wire.layer + 1 + step < wire.layers)
        def _():
            self.copy(1, step, wire.layer + 1 + step, wire.row).wait_recv()
            if step + 1 < self.steps:
                pl.when(wire.layer > 0)(lambda: self.down(step + 1).start())
            self.copy(3, step, wire.layer + 1 + step, wire.partner).start()

    def end(self):
        wire = self.wire
        for step in range(self.steps):
            pl.when((wire.layer + 1 < wire.layers) & (wire.layer - step >= 0))(
                lambda step=step: self.up(step).wait_send()
            )
            pl.when((wire.layer > 0) & (wire.layer + step < wire.layers))(
                lambda step=step: self.down(step).wait_send()
            )
            pl.when(wire.layer - 1 - step >= 0)(
                lambda step=step: self.copy(2, step, wire.layer - 1 - step, wire.partner).wait()
            )
            pl.when(wire.layer + 1 + step < wire.layers)(
                lambda step=step: self.copy(3, step, wire.layer + 1 + step, wire.partner).wait()
            )
        for copy in self.own:
            copy.wait()


class RowGather:
    def __init__(self, shard, full, wire):
        self.wire = wire
        count = shard.shape[0]
        mine = full.at[tile(wire.row, count)]
        self.first = [wire.local(shard, mine), wire.remote(shard, mine, "row", wire.partner)]
        self.along = [
            wire.remote(shard, mine, "row", wire.layer_peer(step))
            for step in range(1, wire.layers)
        ]
        self.onward = []
        for step in range(1, wire.layers):
            block = full.at[tile(wire.layer_peer(wire.layers - step), count)]
            self.onward.append(wire.remote(block, block, "row", wire.partner))

    def begin(self):
        for copy in self.along + self.first:
            copy.start()

    def early(self):
        pass

    def middle(self):
        for copy, onward in zip(self.along, self.onward):
            copy.wait_recv()
            onward.start()

    def end(self):
        for copy in self.along:
            copy.wait_send()
        for copy in self.first:
            copy.wait()
        for copy in self.onward:
            copy.wait()


class RowReduce:
    def __init__(self, grads, pieces, outs, held, pair, got, total, *rest, load=True):
        *parts, wire = rest
        self.wire, self.out, self.grads = wire, total, grads
        self.pieces = pieces
        self.parts = parts or [total]
        self.keep = [wire.local(part, out) for part, out in zip(self.parts, outs)]
        self.held, self.pair, self.got = held, pair, got
        self.count = held.shape[1]
        other = 1 - wire.core
        self.load = []
        if load:
            self.load = [
                wire.local(grads.at[tile(layer * 2 + wire.core, self.count)], held.at[layer])
                for layer in range(wire.layers)
            ]
        self.swap = [
            wire.remote(grads.at[tile(layer * 2 + other, self.count)], pair.at[layer], "row",
                        wire.partner)
            for layer in range(wire.layers)
        ]
        self.along = []
        for step in range(1, wire.layers):
            layer = lax.rem(wire.layer + step, wire.layers)
            self.along.append(
                wire.remote(held.at[layer], got.at[step - 1], "row", wire.layer_peer(step))
            )

    def begin(self):
        for copy in self.swap + self.load:
            copy.start()

    def early(self):
        for copy in self.load + self.swap:
            copy.wait()
        size = min(32, self.count)
        for layer in range(self.wire.layers):
            def add(rows, index, layer=layer):
                if self.load:
                    mine = self.held[layer, rows]
                else:
                    at = (layer * 2 + self.wire.core) * self.count + index * size
                    mine = self.grads[pl.ds(pl.multiple_of(at, size), size)]
                self.held[layer, rows] = (
                    mine.astype(F32) + self.pair[layer, rows].astype(F32)
                ).astype(BF16)

            row_loop(self.count, add)
        for copy in self.along:
            copy.start()

    def middle(self):
        pass

    def end(self):
        for copy in self.along:
            copy.wait()

        def add(rows, index):
            total = self.held[self.wire.layer, rows].astype(F32)
            for step in range(self.wire.layers - 1):
                total = total + self.got[step, rows].astype(F32)
            self.out[rows] = total

        row_loop(self.count, add)
        if len(self.parts) > 1 or self.pieces[0][1]:
            at = 0
            for part, (width, flip) in zip(self.parts, self.pieces):
                piece = self.out[:, at:at + width]
                part[...] = piece.T if flip else piece
                at += width
        self.wire.store(self.keep)


def piece_shapes(count, pieces):
    return [(width, count) if flip else (count, width) for width, flip in pieces]


def reduce_scratch(layers, count, width, pieces):
    apart = len(pieces) > 1 or pieces[0][1]
    parts = [pltpu.VMEM(shape, F32) for shape in piece_shapes(count, pieces)] if apart else []
    return parts_last(layers, count, width) + parts


def parts_last(layers, count, width):
    return [
        pltpu.VMEM((layers, count, width), BF16),
        pltpu.VMEM((layers, count, width), BF16),
        pltpu.VMEM((max(1, layers - 1), count, width), BF16),
        pltpu.VMEM((count, width), F32),
    ]


class SumItem:
    def __init__(self, kind, source, out, got, packed, got_row, wire):
        self.wire, self.kind, self.source, self.out = wire, kind, source, out
        self.got, self.packed, self.got_row = got, packed, got_row
        self.col = []
        if kind != "own":
            for step in range(1, wire.n):
                peer = lax.rem(wire.me + step, wire.n)
                piece = source.at[peer] if kind == "piece" else source
                self.col.append(wire.remote(piece, got.at[step - 1], "col", peer))
        self.swap = wire.remote(packed.at[0], got_row.at[0], "row", wire.partner)
        self.along = [
            wire.remote(packed.at[1], got_row.at[step], "row", wire.layer_peer(step))
            for step in range(1, wire.layers)
        ]

    def begin(self):
        for copy in self.col:
            copy.start()

    def early(self):
        for copy in self.col:
            copy.wait()
        total = self.source[self.wire.me] if self.kind == "piece" else self.source[...]
        if self.kind != "own":
            for step in range(self.wire.n - 1):
                total = total + self.got[step]
        self.packed[0] = total
        self.swap.start()

    def middle(self):
        self.swap.wait()
        self.packed[1] = self.packed[0] + self.got_row[0]
        for copy in self.along:
            copy.start()

    def end(self):
        for copy in self.along:
            copy.wait()
        total = self.packed[1]
        for step in range(1, self.wire.layers):
            total = total + self.got_row[step]
        self.out[...] = total


def sum_scratch(n, layers, shape):
    return [
        pltpu.VMEM(shape, F32),
        pltpu.VMEM((n - 1,) + shape, F32),
        pltpu.VMEM((2,) + shape, F32),
        pltpu.VMEM((layers,) + shape, F32),
    ]


def join(pieces, target):
    at = 0
    for ref, flip in pieces:
        width = ref.shape[0] if flip else ref.shape[1]
        target[:, at:at + width] = ref[...].T if flip else ref[...]
        at += width


def joined_shape(pieces):
    rows = {array.shape[1] if flip else array.shape[0] for array, flip in pieces}
    return rows.pop(), sum(array.shape[0] if flip else array.shape[1] for array, flip in pieces)


def row_loop(count, body):
    size = min(32, count)

    def step(index, carry):
        body(tile(index, size), index)
        return carry

    lax.fori_loop(0, count // size, step, 0)


def block_loop(extent, body):
    size = min(256, extent)

    def step(index, carry):
        body(tile(index, size), index)
        return carry

    lax.fori_loop(0, extent // size, step, 0)


def fold8(values):
    return jnp.sum(values.reshape(values.shape[0] // 8, 8, values.shape[1]), axis=0)


def normalize(values):
    average = jnp.mean(values, axis=1, keepdims=True)
    centered = values - average
    inverse = lax.rsqrt(jnp.mean(centered * centered, axis=1, keepdims=True) + EPSILON)
    return centered * inverse, inverse


def norm_back(grad_in, normed, inverse, gains):
    scaled = grad_in * gains
    first = jnp.mean(scaled, axis=1, keepdims=True)
    second = jnp.mean(scaled * normed, axis=1, keepdims=True)
    return inverse * (scaled - first - normed * second)


def comm_call(name, collective_id, sizes, main, ins, outs, scratch, gathers=(), reduces=(), cost=10**9,
              col_on=True, more_slots=0, row_on=False):
    n, m = sizes
    layers = m // 2
    gather_pieces = [piece for pieces in gathers for piece in pieces]
    in_arrays = [item[0] for item in ins] + [array for array, _ in gather_pieces]
    in_arrays += [grads for grads, _ in reduces]
    in_specs = [hbm() if item[1] == "load" else item[1] for item in ins]
    in_specs += [vmem()] * len(gather_pieces) + [hbm()] * len(reduces)
    out_shapes = [jax.ShapeDtypeStruct(item[0], item[1]) for item in outs]
    out_specs = [hbm() if item[2] == "store" else item[2] for item in outs]
    copied = [pltpu.VMEM(item[0].shape, item[0].dtype) for item in ins if item[1] == "load"]
    copied += [pltpu.VMEM(item[0], item[1]) for item in outs if item[2] == "store"]
    side_scratch = []
    for pieces in gathers:
        rows, width = joined_shape(pieces)
        out_shapes.append(jax.ShapeDtypeStruct((m * rows, width), BF16))
        out_specs.append(hbm())
        side_scratch.append(pltpu.VMEM((rows, width), BF16))
    reduce_counts = []
    for grads, pieces in reduces:
        count, width = grads.shape[0] // m, grads.shape[1]
        for shape in piece_shapes(count, pieces):
            out_shapes.append(jax.ShapeDtypeStruct(shape, F32))
            out_specs.append(hbm())
        made = reduce_scratch(layers, count, width, pieces)
        reduce_counts.append(len(made))
        side_scratch += made
    every_scratch = copied + list(scratch) + side_scratch
    held = sum(padded_bytes(item.shape, item.dtype) for item in every_scratch)
    remote_slots = 8 * n + 16 + len(gathers) * 2 * layers + len(reduces) * 2 * layers + more_slots
    local_slots = 12 + len(copied) + len(gathers) + len(reduces) * (layers + 4) + more_slots

    def kernel(*refs):
        at = 0

        def take(count):
            nonlocal at
            at += count
            return refs[at - count:at]

        main_ins = list(take(len(ins)))
        gather_ins = [
            [(ref, flip) for ref, (_, flip) in zip(take(len(pieces)), pieces)] for pieces in gathers
        ]
        reduce_ins = take(len(reduces))
        main_outs = list(take(len(outs)))
        gather_outs = take(len(gathers))
        reduce_outs = [take(len(pieces)) for _, pieces in reduces]
        loads, stores = [], []
        for place, item in enumerate(ins):
            if item[1] == "load":
                (held_ref,) = take(1)
                loads.append((main_ins[place], held_ref))
                main_ins[place] = held_ref
        for place, item in enumerate(outs):
            if item[2] == "store":
                (held_ref,) = take(1)
                stores.append((held_ref, main_outs[place]))
                main_outs[place] = held_ref
        main_scratch = take(len(scratch))
        side = []
        for pieces, full in zip(gather_ins, gather_outs):
            (shard,) = take(1)
            join(pieces, shard)
            side.append(functools.partial(RowGather, shard, full))
        for grads, out, (_, pieces), size in zip(reduce_ins, reduce_outs, reduces, reduce_counts):
            side.append(functools.partial(RowReduce, grads, pieces, out, *take(size)))
        send_sem, recv_sem, local_sem = take(3)
        wire = Wire(sizes, send_sem, recv_sem, local_sem, side, col_on, row_on)
        wire.loads = [wire.local(*pair) for pair in loads]
        wire.stores = [wire.local(*pair) for pair in stores]
        for copy in wire.loads:
            copy.start()
        main(wire, main_ins, main_outs, main_scratch)
        wire.settle()

    return pl.pallas_call(
        kernel,
        name=name,
        out_shape=tuple(out_shapes),
        in_specs=in_specs,
        out_specs=tuple(out_specs),
        scratch_shapes=every_scratch + [
            pltpu.SemaphoreType.DMA((remote_slots,)),
            pltpu.SemaphoreType.DMA((remote_slots,)),
            pltpu.SemaphoreType.DMA((local_slots,)),
        ],
        compiler_params=comm_params(collective_id, held),
        cost_estimate=pl.CostEstimate(flops=cost, bytes_accessed=10**8, transcendentals=0),
    )(*in_arrays)


def norm_rows(wire, count, source, gains, rows_ref):
    base = wire.me * count

    def work(rows, index):
        normed, _ = normalize(source[rows])
        size = min(32, count)
        rows_ref[pl.ds(pl.multiple_of(base + index * size, size), size)] = (normed * gains).astype(BF16)

    row_loop(count, work)


def cast_rows(wire, count, source, factor, rows_ref):
    base = wire.me * count

    def work(rows, index):
        size = min(32, count)
        rows_ref[pl.ds(pl.multiple_of(base + index * size, size), size)] = (
            factor * source[rows]
        ).astype(BF16)

    row_loop(count, work)


def keep_rows(limit, start, rows):
    place = lax.broadcasted_iota(jnp.int32, (rows, 1), 0) + start
    return jnp.where(place < limit, 1.0, 0.0)


def residual(collect, factor, resid, limit, after_ref, squares_ref):
    squares_ref[...] = jnp.zeros_like(squares_ref)
    base = collect.wire.me * collect.count

    def work(rows, branch):
        after = resid[rows] + factor * branch
        after_ref[rows] = after
        keep = keep_rows(limit, base + rows.start, branch.shape[0])
        squares_ref[0:8] += fold8(branch * branch * keep)
        squares_ref[8:16] += fold8(after * after * keep)

    collect.sum_loop(work)


def residual_back(collect, grad_ref, resid, gains, new_grad_ref, gain_grad_ref):
    gain_grad_ref[...] = jnp.zeros_like(gain_grad_ref)

    def work(rows, rows_grad):
        normed, inverse = normalize(resid[rows])
        new_grad_ref[rows] = grad_ref[rows] + norm_back(rows_grad, normed, inverse, gains)
        gain_grad_ref[...] += fold8(rows_grad * normed)

    collect.sum_loop(work)


def send_pieces(wire, count, source, pieces, out_ref):
    width = pieces.shape[2]

    def split(rows, index):
        result = source[rows].astype(BF16)
        for part in range(wire.n):
            pieces[part, rows] = result[:, part * width:(part + 1) * width]

    row_loop(count, split)
    mine = out_ref.at[tile(wire.me, count)]
    copies = wire.to_all(lambda peer: pieces.at[peer], mine)
    here = wire.local(pieces.at[wire.me], mine)
    here.start()
    return copies + [here]


def feed_forward_first(count, chunk, rows_ref, up, pre_ref, act):
    rows = tile(chunk, count)
    left = rows_ref[rows]

    def first(cols, index):
        pre = matmul(left, up[:, cols])
        pre_ref[rows, cols] = pre.astype(BF16)
        act[:, cols] = (pre * jax.nn.sigmoid(pre)).astype(BF16)

    block_loop(up.shape[1], first)


def feed_forward_second(act, down_t, target):
    hidden = act[...]

    def second(cols, index):
        target[:, cols] = matmul_nt(hidden, down_t[cols]).astype(BF16)

    block_loop(down_t.shape[0], second)


def feed_forward_main(count, gain_row, factor, enter, turn, wire, ins, outs, scratch):
    ins, outs, scratch = list(ins), list(outs), list(scratch)
    if enter:
        limit_ref, tokens_ref, cot_in = ins[:3]
        gain_ins = ins[3:8]
        up_shard, down_ref = ins[8:10]
        next_pieces = [(ref, flip) for ref, flip in zip(ins[10:], enter)]
        ins = []
        resid, cot_out, gains_ref, up, down_t, next_full = outs[:6]
        outs = outs[6:]
        arrived, arrived_cot, arrived_gain, gain_in, down_shard, next_shard = scratch[:6]
        scratch = scratch[6:]
    else:
        limit_ref, resid, gains_ref = ins[:3]
        ins = ins[3:]
    if enter:
        for place, ref in enumerate(gain_ins):
            gain_in[place:place + 1] = ref[...]
        gain_in[len(gain_ins):] = jnp.zeros((8 - len(gain_ins), gain_in.shape[1]), F32)
        join([(down_ref, True)], down_shard)
        join(next_pieces, next_shard)
    else:
        up, down_t = ins[:2]
        ins = ins[2:]
    if turn:
        (cot_ref,) = ins
        grad_ref, gain_grad_ref, out_ref = outs[:3]
        outs = outs[3:]
        pieces, after_ref = scratch[:2]
        scratch = scratch[2:]
    else:
        after_ref = outs.pop(0)
    squares_ref, rows_ref, pre_ref = outs
    act, part, got = scratch
    wire.greet()
    wire.begin()
    if enter:
        up_job = RowChain(up_shard, up, wire)
        down_job = RowChain(down_shard, down_t, wire)
        next_job = RowChain(next_shard, next_full, wire)
        up_job.begin()
        width = arrived_gain.shape[2]
        turned = tokens_ref.shape[0] == width

        def share(ref, peer):
            return ref.at[:, tile(peer, count)] if turned else ref.at[tile(peer, count)]

        def settle(came, target):
            for piece in range(wire.n):
                cols = slice(piece * width, (piece + 1) * width)
                if turned:
                    target[:, cols] = came[piece].astype(F32).T
                else:
                    target[:, cols] = came[piece].astype(F32)

        mine = [
            wire.local(share(tokens_ref, wire.me), arrived.at[wire.me]),
            wire.local(gain_in, arrived_gain.at[wire.me]),
            wire.local(share(cot_in, wire.me), arrived_cot.at[wire.me]),
        ]
        copies = wire.to_all(lambda peer: share(tokens_ref, peer), arrived.at[wire.me])
        copies += wire.to_all(lambda peer: gain_in, arrived_gain.at[wire.me])
        for copy in mine:
            copy.start()
        for copy in mine + copies:
            copy.wait()
        for piece in range(wire.n):
            gains_ref[:, piece * width:(piece + 1) * width] = arrived_gain[piece]

        settle(arrived, resid)
    gains = gains_ref[gain_row:gain_row + 1]
    norm_rows(wire, count, resid, gains, rows_ref)
    spread = Spread(wire, rows_ref, count)
    spread.start()
    wire.loaded()
    collect = Collect(wire, part, got)
    cot_copies = []
    if enter:
        cot_copies = wire.to_all(
            lambda peer: share(cot_in, peer), arrived_cot.at[wire.me]
        )
    wire.early()
    if enter:
        up_job.advance(0)
        spread.relay()
        for step in range(1, up_job.steps):
            up_job.advance(step)
        down_job.begin()
        up_job.end()
        chunks = []
        for chunk, slot in spread.arrivals(relay=False):
            chunks.append((chunk, slot))
            feed_forward_first(count, chunk, rows_ref, up, pre_ref, act.at[len(chunks) - 1])
            if len(chunks) - 1 < down_job.steps:
                down_job.advance(len(chunks) - 1)
        for copy in cot_copies:
            copy.wait()

        settle(arrived_cot, cot_out)
        next_job.begin()
        down_job.end()
        for place, (chunk, slot) in reversed(list(enumerate(chunks))):
            target = part.at[wire.n - 1 if slot is None else slot]
            feed_forward_second(act.at[place], down_t, target)
            if slot is not None:
                collect.send(slot)
            if len(chunks) - 1 - place < next_job.steps:
                next_job.advance(len(chunks) - 1 - place)
        collect.combine()
        for step in range(len(chunks), next_job.steps):
            next_job.advance(step)
    else:
        for chunk, slot in spread.arrivals():
            target = part.at[wire.n - 1 if slot is None else slot]
            feed_forward_first(count, chunk, rows_ref, up, pre_ref, act.at[0])
            feed_forward_second(act.at[0], down_t, target)
            if slot is not None:
                collect.send(slot)
        collect.combine()
    wire.middle()
    wire.flush()
    collect.wait()
    residual(collect, factor, resid, limit_ref[0], after_ref, squares_ref)
    late = []
    if turn:
        final_gains = gains_ref[gain_row + 1:gain_row + 2]
        gain_grad_ref[...] = jnp.zeros_like(gain_grad_ref)

        def final(rows, index):
            normed, inverse = normalize(after_ref[rows])
            cot = cot_ref[rows]
            grad_ref[rows] = norm_back(cot, normed, inverse, final_gains)
            gain_grad_ref[...] += fold8(cot * normed)
            after_ref[rows] = normed * final_gains

        row_loop(count, final)
        late = send_pieces(wire, count, after_ref, pieces, out_ref)
    spread.finish()
    for copy in late:
        copy.wait()
    if enter:
        next_job.end()
    wire.end()


def feed_forward(sizes, name, collective_id, gain_row, up, down_t, limit, resid=None, gains=None,
                 enter=None, turn=None, **side):
    n, m = sizes
    hidden = up.shape[1]
    full = up.shape[0] * (m if enter else 1)
    next_pieces = None
    if enter:
        tokens, cotangent, gain_parts, next_pieces = enter
        turned = tokens.shape[0] * n == full
        width, length = tokens.shape if turned else tokens.shape[::-1]
        count = length // n
        came = (n, width, count) if turned else (n, count, width)
        ins = [(limit, smem()), (tokens, vmem()), (cotangent, vmem())]
        ins += [(part, vmem()) for part in gain_parts] + [(up, vmem()), (down_t, vmem())]
        ins += [(array, vmem()) for array, _ in next_pieces]
        down_shape, next_shape = (full // m, hidden), joined_shape(next_pieces)
        outs = [((count, full), F32, "store"), ((count, full), F32, "store"), ((8, full), F32, vmem())]
        scratch = [
            pltpu.VMEM(came, BF16),
            pltpu.VMEM(came, BF16),
            pltpu.VMEM((n, 8, width), F32),
            pltpu.VMEM((8, width), F32),
            pltpu.VMEM(down_shape, BF16),
            pltpu.VMEM(next_shape, BF16),
        ]
        for shape, spec in ((down_shape, "store"), (down_shape, "store"), (next_shape, hbm())):
            outs.append(((m * shape[0], shape[1]), BF16, spec))
        side = dict(side, more_slots=6 * m, row_on=True)
    else:
        count = resid.shape[0]
        ins = [(limit, smem()), (resid, vmem()), (gains, vmem())]
        outs, scratch = [], []
        ins += [(up, "load"), (down_t, "load")]
    if turn is not None:
        ins.append((turn, "load"))
        outs += [
            ((count, full), F32, vmem()),
            ((8, full), F32, vmem()),
            ((n * count, full // n), BF16, hbm()),
        ]
        scratch.append(pltpu.VMEM((n, count, full // n), BF16))
    if turn is None:
        outs.append(((count, full), F32, vmem()))
    else:
        scratch.append(pltpu.VMEM((count, full), F32))
    outs += [
        ((16, full), F32, vmem()),
        ((n * count, full), BF16, "store"),
        ((n * count, hidden), BF16, "store"),
    ]
    scratch += [
        pltpu.VMEM((n if enter else 1, count, hidden), BF16),
        pltpu.VMEM((n, count, full), BF16),
        pltpu.VMEM((n - 1, count, full), BF16),
    ]
    return comm_call(
        name, collective_id, sizes,
        functools.partial(
            feed_forward_main, count, gain_row, 0.5, enter and [flip for _, flip in next_pieces],
            turn is not None,
        ),
        ins, outs, scratch, **side,
    )


def lane_sum(values):
    total = values[:, 0:BLOCK]
    for at in range(BLOCK, values.shape[1], BLOCK):
        total = total + values[:, at:at + BLOCK]
    return total


def feed_forward_back_main(count, gain_row, leave, wire, ins, outs, scratch):
    grad_ref, resid, gains_ref, up, down_t, rows_ref, pre_ref = ins[:7]
    ins = ins[7:]
    grads, pre_grad, act, part, got = scratch[:5]
    scratch = list(scratch[5:])
    hidden = up.shape[1]
    full = up.shape[0]

    def take(size):
        taken, scratch[:size] = scratch[:size], []
        return taken

    if leave:
        up_width, down_pieces, reduce_sizes = leave
        limit_ref = ins[0]
        gain_parts, squares, table_part, tap_part, depth_part = ins[1:5], ins[5:9], *ins[9:12]
        gain_outs, table_out, rms_out, tap_out, depth_out = outs[:5], *outs[5:9]
        up_out, down_out, last_ref = outs[9:12]
        gain_grad_ref, up_grad_ref, down_grad_ref, new_grad_ref, pieces = take(5)
        width = pieces.shape[2]
        up_job = RowReduce(up_grad_ref, [(hidden, False)], [up_out], *take(reduce_sizes[0]), wire,
                           load=False)
        down_job = RowReduce(down_grad_ref, [(hidden, True)], [down_out], *take(reduce_sizes[1]), wire,
                             load=False)
        gain_pieces, square_parts, first_pieces = take(3)
        items = [
            SumItem(kind, source, *take(4), wire)
            for kind, source in (
                ("piece", gain_pieces), ("all", table_part), ("all", square_parts),
                ("own", tap_part), ("own", depth_part),
            )
        ]
        gain_item = SumItem("piece", first_pieces, *take(4), wire)
    else:
        (tokens_ref,) = ins
        gain_grad_ref, up_grad_ref, down_grad_ref, last_ref, turned_ref = outs
        new_grad_ref = last_ref
        items = []
    gains = gains_ref[gain_row:gain_row + 1]
    wire.greet()
    wire.begin()
    cast_rows(wire, count, grad_ref, 0.5, grads)
    spread = Spread(wire, grads, count)
    spread.start()
    if leave:
        gain_pieces[...] = jnp.zeros_like(gain_pieces)
        square_parts[...] = jnp.zeros_like(square_parts)
        for place, ref in enumerate(gain_parts):
            row = jnp.sum(ref[...], axis=0, keepdims=True)
            for piece in range(wire.n):
                gain_pieces[piece, place:place + 1] = row[:, piece * width:(piece + 1) * width]
        for place, ref in enumerate(squares):
            for at in (0, 1):
                rows = ref[at * 8:(at + 1) * 8]
                square_parts[at * 4 + place:at * 4 + place + 1] = lane_sum(
                    jnp.sum(rows, axis=0, keepdims=True)
                )
        lane = lax.broadcasted_iota(jnp.int32, (1, BLOCK), 1)
        once = jnp.where(wire.me == 0, limit_ref[0], 0)
        square_parts[8:9] = jnp.where(lane == 0, once, 0).astype(F32)
        for item in items:
            item.begin()
    wire.loaded()
    collect = Collect(wire, part, got)
    for chunk, slot in spread.arrivals():
        rows = tile(chunk, count)
        target = part.at[wire.n - 1 if slot is None else slot]
        left = grads[rows]

        def first(cols, index):
            act_grad = matmul(left, down_t[:, cols])
            pre = pre_ref[rows, cols].astype(F32)
            sig = jax.nn.sigmoid(pre)
            act[rows, cols] = (pre * sig).astype(BF16)
            pre_grad[rows, cols] = (act_grad * (sig + pre * sig * (1.0 - sig))).astype(BF16)

        block_loop(hidden, first)
        through = pre_grad[rows]

        def second(cols, index):
            target[:, cols] = matmul_nt(through, up[cols]).astype(BF16)

        block_loop(full, second)
        if slot is not None:
            collect.send(slot)
        if slot is None:
            wire.early()
            for item in items:
                item.early()
            if not leave:
                turned_ref[...] = tokens_ref[...].T
        elif slot == 0:
            for item in items:
                item.middle()
    wire.middle()
    size = min(256, hidden)

    def weight_grad(left_ref, right_ref, out):
        for start in range(0, hidden, size):
            cols = slice(start, start + size)

            def block(rows, index):
                out[rows, cols] = matmul_tn(left_ref[:, rows], right_ref[:, cols]).astype(BF16)

            block_loop(full, block)

    weight_grad(grads, act, down_grad_ref)
    if leave:
        down_job.begin()
    collect.combine()
    weight_grad(rows_ref, pre_grad, up_grad_ref)
    if leave:
        up_job.begin()
        down_job.early()
    wire.flush()
    collect.wait()
    residual_back(collect, grad_ref, resid, gains, new_grad_ref, gain_grad_ref)
    if leave:
        for piece in range(wire.n):
            first_pieces[piece] = gain_grad_ref[:, piece * width:(piece + 1) * width]
        gain_item.begin()
        late = send_pieces(wire, count, new_grad_ref, pieces, last_ref)
        up_job.early()
        gain_item.early()
        for item in items:
            item.end()
        gain_item.middle()
        totals = [item.out for item in items]
        for place, ref in enumerate(gain_outs[1:]):
            ref[...] = totals[0][place:place + 1]
        table = totals[1][...]
        for at in range(HEAD_DIM, table.shape[1], HEAD_DIM):
            table = table[:, 0:HEAD_DIM] + table[:, at:at + HEAD_DIM]
        table_out[...] = table[0:LEFT + RIGHT + 1]
        sums = jnp.sum(totals[2][...], axis=1, keepdims=True)
        rms_out[...] = jnp.broadcast_to(jnp.sqrt(sums[0:8] / (sums[8:9] * full)), rms_out.shape)
        tap_out[...] = totals[3][0:tap_out.shape[0]]
        depth_out[...] = jnp.sum(totals[4][...], axis=0, keepdims=True)
        for copy in late:
            copy.wait()
        wire.end()
        down_job.end()
        gain_item.end()
        gain_outs[0][...] = jnp.sum(gain_item.out[...], axis=0, keepdims=True)
        up_job.end()
    spread.finish()
    if not leave:
        wire.end()


def feed_forward_back(sizes, name, collective_id, gain_row, grad, resid, gains, up, down_t, rows, pre,
                      leave=None, tokens=None, taps=0, **side):
    n, m = sizes
    full, hidden = up.shape
    count = resid.shape[0]
    width = full // n
    ins = [(grad, vmem()), (resid, "load"), (gains, vmem())]
    ins += [(item, "load") for item in (up, down_t, rows, pre)]
    scratch = [
        pltpu.VMEM((n * count, full), BF16),
        pltpu.VMEM((n * count, hidden), BF16),
        pltpu.VMEM((n * count, hidden), BF16),
        pltpu.VMEM((n, count, full), BF16),
        pltpu.VMEM((n - 1, count, full), BF16),
    ]
    extra = None
    if leave:
        limit, gain_parts, squares, table_part, tap_part, depth_part = leave
        layers = m // 2
        ins.append((limit, smem()))
        ins += [(item, vmem()) for item in (*gain_parts, *squares, table_part, tap_part, depth_part)]
        outs = [((1, width), F32, vmem())] * 5
        outs += [
            ((LEFT + RIGHT + 1, HEAD_DIM), F32, vmem()),
            ((8, BLOCK), F32, vmem()),
            ((taps, width), F32, vmem()),
            ((1, width), F32, vmem()),
            ((full // m, hidden), F32, hbm()),
            ((hidden, full // m), F32, hbm()),
            ((n * count, width), BF16, hbm()),
        ]
        scratch += [
            pltpu.VMEM((8, full), F32),
            pltpu.VMEM((full, hidden), BF16),
            pltpu.VMEM((full, hidden), BF16),
            pltpu.VMEM((count, full), F32),
            pltpu.VMEM((n, count, width), BF16),
        ]
        reduces = [
            reduce_scratch(layers, full // m, hidden, [(hidden, flip)]) for flip in (False, True)
        ]
        scratch += reduces[0] + reduces[1]
        extra = (hidden, None, [len(made) for made in reduces])
        scratch += [
            pltpu.VMEM((n, 8, width), F32), pltpu.VMEM((16, BLOCK), F32), pltpu.VMEM((n, 8, width), F32)
        ]
        for shape in ((8, width), table_part.shape, (16, BLOCK), tap_part.shape, depth_part.shape,
                      (8, width)):
            scratch += sum_scratch(n, layers, shape)
        side = dict(side, more_slots=16 * m + 8 * n, row_on=True)
    else:
        ins.append((tokens, "load"))
        outs = [
            ((8, full), F32, vmem()),
            ((full, hidden), BF16, "store"),
            ((full, hidden), BF16, "store"),
            ((count, full), F32, vmem()),
            ((tokens.shape[1], tokens.shape[0]), BF16, "store"),
        ]
    return comm_call(
        name, collective_id, sizes,
        functools.partial(feed_forward_back_main, count, gain_row, extra),
        ins, outs, scratch, **side,
    )


def slot_rows(axis):
    slots = lax.broadcasted_iota(jnp.int32, (LEFT + RIGHT + 8, SPAN), axis)
    signed = jnp.where(slots < SPAN - BLOCK + 1, slots, slots - SPAN)
    return jnp.clip(signed - (BLOCK - LEFT), 0, LEFT + RIGHT)


def extend_table(table, copies):
    slots = jnp.arange(SPAN)
    signed = jnp.where(slots < SPAN - BLOCK + 1, slots, slots - SPAN)
    row_of = jnp.clip(signed - (BLOCK - LEFT), 0, LEFT + RIGHT)
    chosen = (row_of[:, None] == jnp.arange(LEFT + RIGHT + 1)[None, :]).astype(table.dtype)
    return jnp.tile(matmul(chosen, table).astype(table.dtype), (1, copies))


def fill_far(far_ref, table_ref, limit):
    blocks, length, _ = far_ref.shape
    lane = lax.broadcasted_iota(jnp.int32, (1, BLOCK), 1)

    def row(at, mark):
        ends = table_ref[at:at + 1].astype(F32)
        if ends.shape[1] < BLOCK:
            ends = jnp.concatenate([ends, jnp.zeros((1, BLOCK - ends.shape[1]), F32)], axis=1)
        return jnp.where(lane < HEAD_DIM, ends, jnp.where(lane == mark, 1.0, 0.0))

    first = row(0, HEAD_DIM + 1)
    last = row(SPAN - 2 * BLOCK, HEAD_DIM + 2)

    def block(step, carry):
        index, piece = step // (length // BLOCK), lax.rem(step, length // BLOCK)
        at = index * BLOCK
        column = lax.broadcasted_iota(jnp.int32, (BLOCK, 1), 0) + piece * BLOCK
        place = column + at - BLOCK
        key = jnp.where(place < 0, place + length, jnp.where(place >= length, place - length, place))
        near = (column < WINDOW) & (place >= 0) & (place < length)
        left = jnp.where(near | (key >= at), 0.0, 1.0)
        right = jnp.where(near | (key < at), 0.0, 1.0)
        bias = jnp.where(key < limit, 0.0, NEG_FILL)
        terms = left * first + right * last + jnp.where(lane == HEAD_DIM, bias, 0.0)
        far_ref[index, tile(piece, BLOCK)] = terms.astype(BF16)
        return carry

    lax.fori_loop(0, blocks * (length // BLOCK), block, 0)


def duplicate(qkv_ref, width, group, keys, values):
    length = qkv_ref.shape[0]
    for part in range(width // group):
        base = part * group
        for copy in range(2):
            place = slice(copy * length, (copy + 1) * length)
            keys[part, place] = qkv_ref[:, width + base:width + base + group]
            values[part, place] = qkv_ref[:, 2 * width + base:2 * width + base + group]


def by_head(values, group):
    if group == HEAD_DIM:
        return values
    lane = lax.broadcasted_iota(jnp.int32, (BLOCK, group), 1)
    zero = jnp.zeros_like(values)
    return jnp.concatenate(
        [
            jnp.where((lane >= at) & (lane < at + HEAD_DIM), values, zero)
            for at in range(0, group, HEAD_DIM)
        ],
        axis=0,
    )


def own_lanes(values, group):
    if group == HEAD_DIM:
        return values
    lane = lax.broadcasted_iota(jnp.int32, (BLOCK, group), 1)
    return jnp.where(lane < HEAD_DIM, values[0:BLOCK], values[BLOCK:2 * BLOCK])


def far_queries(values, group):
    wide = values.astype(F32)
    if group == HEAD_DIM:
        lane = lax.broadcasted_iota(jnp.int32, (BLOCK, BLOCK - HEAD_DIM), 1)
        return jnp.concatenate([wide, jnp.where(lane == 0, 1.0, 0.0)], axis=1).astype(BF16)
    lane = lax.broadcasted_iota(jnp.int32, (BLOCK, BLOCK), 1)
    rest = jnp.where(lane == HEAD_DIM, 1.0, 0.0)
    return jnp.concatenate(
        [
            jnp.where(lane < HEAD_DIM, wide, rest),
            jnp.where(lane < HEAD_DIM, pltpu.roll(wide, HEAD_DIM, 1), rest),
        ],
        axis=0,
    ).astype(BF16)


def near_mask(at, length):
    place = lax.broadcasted_iota(jnp.int32, (1, WINDOW), 1) + (at - BLOCK)
    return (place >= 0) & (place < length)


def near_terms(query, table, at, length):
    terms = matmul_nt(query, table)
    halves = [
        pltpu.roll(terms[start:start + BLOCK], 0, 1, stride=1, stride_axis=0)[:, :WINDOW]
        for start in range(0, query.shape[0], BLOCK)
    ]
    return jnp.where(near_mask(at, length), jnp.concatenate(halves, axis=0), 0.0)


def attend_blocks(first, blocks, width, group, qkv_ref, table_ref, far_ref, keys, values, context_ref,
                  log_ref):
    length = qkv_ref.shape[0]
    heads = group // HEAD_DIM
    parts = width // group
    scale = 1.0 / math.sqrt(HEAD_DIM)

    def block(step, carry):
        index, part = first + step // parts, lax.rem(step, parts)
        at = pl.multiple_of(index * BLOCK, BLOCK)
        rows = pl.ds(at, BLOCK)
        cols = tile(part, group) if parts > 1 else slice(0, group)
        window = pl.ds(pl.multiple_of(lax.rem(at + length - BLOCK, length), BLOCK), length)
        query_rows = qkv_ref[rows, cols] * jnp.asarray(scale, BF16)
        query = by_head(query_rows, group)
        extra = far_queries(query_rows, group)
        if group == 2 * HEAD_DIM:
            scores = matmul_nt(
                jnp.concatenate([query, extra], axis=1),
                jnp.concatenate([keys[part, window], far_ref[index]], axis=1),
            )
        else:
            scores = matmul_nt(query, keys[part, window]) + matmul_nt(extra, far_ref[index])
        near = scores[:, :WINDOW] + near_terms(query, table_ref[...], at, length)
        scores = jnp.concatenate([near, scores[:, WINDOW:]], axis=1)
        peak = jnp.max(scores, axis=1, keepdims=True)
        weights = jnp.exp(scores - peak)
        total = jnp.sum(weights, axis=1, keepdims=True)
        mixed = matmul(weights.astype(BF16), values[part, window]) * (1.0 / total)
        context_ref[rows, cols] = own_lanes(mixed, group).astype(BF16)
        log = peak + jnp.log(total)
        lane = lax.broadcasted_iota(jnp.int32, (BLOCK, BLOCK), 1)
        square = jnp.where(lane == 0, log[0:BLOCK], 0.0)
        for head in range(1, heads):
            square = jnp.where(lane == head, log[head * BLOCK:(head + 1) * BLOCK], square)
        log_ref[part, :, rows] = square.T[0:8]
        return carry

    lax.fori_loop(0, blocks * parts, block, 0)


def attend_back_core(width, group, qkv_ref, table_ref, far_ref, log_ref, grad_ref, out_ref,
                     table_grad_ref, keys, values, key_grad, value_grad, slot_grad, end_grad):
    length = qkv_ref.shape[0]
    heads = group // HEAD_DIM
    parts = width // group
    scale = 1.0 / math.sqrt(HEAD_DIM)
    duplicate(qkv_ref, width, group, keys, values)
    slot_grad[...] = jnp.zeros_like(slot_grad)
    end_grad[...] = jnp.zeros_like(end_grad)
    key_grad[...] = jnp.zeros_like(key_grad)
    value_grad[...] = jnp.zeros_like(value_grad)
    down = lax.broadcasted_iota(jnp.int32, (BLOCK, BLOCK), 0)
    across = lax.broadcasted_iota(jnp.int32, (BLOCK, BLOCK), 1)
    reverse = jnp.where(down + across == BLOCK - 1, 1.0, 0.0).astype(BF16)

    def flip(values_in):
        return jnp.concatenate(
            [
                matmul(reverse, values_in[start:start + BLOCK])
                for start in range(0, heads * BLOCK, BLOCK)
            ],
            axis=0,
        )

    def block(step, carry):
        index, part = step // parts, lax.rem(step, parts)
        at = pl.multiple_of(index * BLOCK, BLOCK)
        rows = pl.ds(at, BLOCK)
        cols = tile(part, group) if parts > 1 else slice(0, group)
        window = pl.ds(pl.multiple_of(lax.rem(at + length - BLOCK, length), BLOCK), length)
        key_rows = keys[part, window]
        far_rows = far_ref[index]
        query_rows = qkv_ref[rows, cols] * jnp.asarray(scale, BF16)
        query = by_head(query_rows, group)
        extra = far_queries(query_rows, group)
        grad = by_head(grad_ref[rows, cols], group)
        if group == 2 * HEAD_DIM:
            key_wide = jnp.concatenate([key_rows, far_rows], axis=1)
            scores = matmul_nt(key_wide, jnp.concatenate([query, extra], axis=1))
        else:
            scores = matmul_nt(key_rows, query) + matmul_nt(far_rows, extra)
        near = scores[:WINDOW] + near_terms(query, table_ref[...], at, length).T
        scores = jnp.concatenate([near, scores[WINDOW:]], axis=0)
        log = jnp.concatenate([log_ref[part, head:head + 1, rows] for head in range(heads)], axis=1)
        probs = jnp.exp(scores - log)
        prob_grad = matmul_nt(values[part, window], grad)
        row_dot = jnp.sum(probs * prob_grad, axis=0, keepdims=True)
        score_grad = (probs * (prob_grad - row_dot)).astype(BF16)
        value_grad[part, window] += matmul(probs.astype(BF16), grad)
        key_grad[part, window] += matmul(score_grad, query)
        turned_back = score_grad.T
        if group == 2 * HEAD_DIM:
            both = matmul(turned_back, key_wide)
            direct, ends = both[:, :group], both[:, group:]
        else:
            direct, ends = matmul(turned_back, key_rows), matmul(turned_back, far_rows)
        left_sum, right_sum = ends[:, HEAD_DIM + 1:HEAD_DIM + 2], ends[:, HEAD_DIM + 2:HEAD_DIM + 3]
        query_wide = query.astype(F32)
        end_grad[0:8] += fold8(left_sum * query_wide)
        end_grad[8:16] += fold8(right_sum * query_wide)
        near_grad = jnp.where(
            near_mask(at, length), turned_back[:, :WINDOW], jnp.asarray(0.0, BF16)
        )
        flipped = flip(near_grad)
        skewed = []
        for start in range(0, heads * BLOCK, BLOCK):
            padded = jnp.concatenate(
                [flipped[start:start + BLOCK], jnp.zeros((BLOCK, SPAN - WINDOW), F32)], axis=1
            )
            skewed.append(pltpu.roll(padded, SPAN - (BLOCK - 1), 1, stride=1, stride_axis=0))
        straight = jnp.concatenate(skewed, axis=0).astype(BF16)
        term = matmul(straight, table_ref[...])
        high = term.astype(BF16)
        low = (term - high.astype(F32)).astype(BF16)
        direct = direct + flip(high) + flip(low)
        result = own_lanes(direct, group)
        if heads == 1:
            result = result + ends[:, :HEAD_DIM]
        else:
            lane = lax.broadcasted_iota(jnp.int32, (BLOCK, BLOCK), 1)
            result = result + jnp.where(
                lane < HEAD_DIM, ends[0:BLOCK], pltpu.roll(ends[BLOCK:2 * BLOCK], HEAD_DIM, 1)
            )
        out_ref[rows, cols] = (result * scale).astype(BF16)
        slot_grad[...] += matmul_tn(flip(query).astype(BF16), straight)
        return carry

    lax.fori_loop(0, length // BLOCK * parts, block, 0)
    for part in range(parts):
        base = width + part * group
        out_ref[:, base:base + group] = (
            key_grad[part, 0:length] + key_grad[part, length:2 * length]
        ).astype(BF16)
        out_ref[:, width + base:width + base + group] = (
            value_grad[part, 0:length] + value_grad[part, length:2 * length]
        ).astype(BF16)
    chosen = jnp.where(
        slot_rows(1) == lax.broadcasted_iota(jnp.int32, (LEFT + RIGHT + 8, SPAN), 0), 1.0, 0.0
    )
    table_grad_ref[...] = lax.dot_general(
        chosen, slot_grad[...], (((1,), (1,)), ((), ())), precision=lax.Precision.HIGHEST,
        preferred_element_type=F32,
    )
    table_grad_ref[0:1] += jnp.sum(end_grad[0:8], axis=0, keepdims=True)
    table_grad_ref[LEFT + RIGHT:LEFT + RIGHT + 1] += jnp.sum(end_grad[8:16], axis=0, keepdims=True)


def attention_main(count, gain_row, wire, ins, outs, scratch):
    limit_ref, resid, gains_ref, weights, table_ref = ins
    after_ref, squares_ref, rows_ref, qkv_ref, context_ref, log_ref = outs
    far_ref, keys, values, part, got = scratch
    width = context_ref.shape[1]
    group = keys.shape[2]
    wire.greet()
    wire.begin()
    norm_rows(wire, count, resid, gains_ref[gain_row:gain_row + 1], rows_ref)
    spread = Spread(wire, rows_ref, count)
    spread.start()
    wire.loaded()
    collect = Collect(wire, part, got)
    spread.relay()
    wire.early()
    fill_far(far_ref, table_ref, limit_ref[0])
    chunks = []
    for chunk, slot in spread.arrivals(relay=False):
        chunks.append((chunk, slot))
        rows = tile(chunk, count)
        left = rows_ref[rows]

        def project(cols, index):
            qkv_ref[rows, cols] = matmul(left, weights[:, cols]).astype(BF16)

        block_loop(3 * width, project)
    duplicate(qkv_ref, width, group, keys, values)
    size = max(count, BLOCK)
    for chunk, slot in reversed(chunks):
        first = chunk * count // BLOCK
        attend_blocks(first, size // BLOCK, width, group, qkv_ref, table_ref, far_ref, keys, values,
                      context_ref, log_ref)
        target = part.at[wire.n - 1 if slot is None else slot]
        left = context_ref[tile(chunk, count)]

        def leave(cols, index):
            target[:, cols] = matmul_nt(left, weights[cols, 3 * width:]).astype(BF16)

        block_loop(weights.shape[0], leave)
        if slot is not None:
            collect.send(slot)
        if slot == 0:
            collect.combine()
            wire.middle()
    wire.flush()
    collect.wait()
    residual(collect, 1.0, resid, limit_ref[0], after_ref, squares_ref)
    spread.finish()
    wire.end()


def attention(sizes, name, collective_id, gain_row, limit, resid, gains, weights, table, **side):
    n, m = sizes
    count, full = resid.shape
    length, width = n * count, weights.shape[1] // 4
    group = min(2 * HEAD_DIM, width)
    return comm_call(
        name, collective_id, sizes, functools.partial(attention_main, count, gain_row),
        [(limit, smem()), (resid, vmem()), (gains, vmem()), (weights, "load"), (table, "load")],
        [
            ((count, full), F32, vmem()),
            ((16, full), F32, vmem()),
            ((length, full), BF16, "store"),
            ((length, 3 * width), BF16, "store"),
            ((length, width), BF16, "store"),
            ((width // group, 8, length), F32, "store"),
        ],
        [
            pltpu.VMEM((length // BLOCK, length, BLOCK), BF16),
            pltpu.VMEM((width // group, 2 * length, group), BF16),
            pltpu.VMEM((width // group, 2 * length, group), BF16),
            pltpu.VMEM((n, count, full), BF16),
            pltpu.VMEM((n - 1, count, full), BF16),
        ],
        cost=20 * 10**9, **side,
    )


def attention_back_main(count, gain_row, wire, ins, outs, scratch):
    (limit_ref, grad_ref, resid, gains_ref, weights, table_ref, rows_ref, qkv_ref, context_ref,
     log_ref) = ins
    gain_grad_ref, wide_ref, table_grad_ref, new_grad_ref = outs
    (far_ref, grads, context_grad, qkv_grad, keys, values, key_grad, value_grad, slot_grad, end_grad, part,
     got) = scratch
    width = context_ref.shape[1]
    group = keys.shape[2]
    wire.greet()
    wire.begin()
    cast_rows(wire, count, grad_ref, 1.0, grads)
    spread = Spread(wire, grads, count)
    spread.start()
    wire.loaded()
    collect = Collect(wire, part, got)
    spread.relay()
    wire.early()
    fill_far(far_ref, table_ref, limit_ref[0])
    chunks = []
    for chunk, slot in spread.arrivals(relay=False):
        chunks.append((chunk, slot))
        rows = tile(chunk, count)
        context_grad[rows] = matmul(grads[rows], weights[:, 3 * width:]).astype(BF16)
    wire.middle()
    attend_back_core(width, group, qkv_ref, table_ref, far_ref, log_ref, context_grad, qkv_grad,
                     table_grad_ref, keys, values, key_grad, value_grad, slot_grad, end_grad)
    for chunk, slot in reversed(chunks):
        target = part.at[wire.n - 1 if slot is None else slot]
        left = qkv_grad[tile(chunk, count)]

        def back(cols, index):
            target[:, cols] = matmul_nt(left, weights[cols, :3 * width]).astype(BF16)

        block_loop(weights.shape[0], back)
        if slot is not None:
            collect.send(slot)
    collect.combine()

    def weight_grads(rows, index):
        wide_ref[rows, :3 * width] = matmul_tn(rows_ref[:, rows], qkv_grad[...]).astype(BF16)
        wide_ref[rows, 3 * width:] = matmul_tn(grads[:, rows], context_ref[...]).astype(BF16)

    block_loop(weights.shape[0], weight_grads)
    wire.flush()
    wire.end()
    collect.wait()
    residual_back(collect, grad_ref, resid, gains_ref[gain_row:gain_row + 1], new_grad_ref,
                  gain_grad_ref)
    spread.finish()


def attention_back(sizes, name, collective_id, gain_row, limit, grad, resid, gains, weights, table, rows,
                   qkv, context, log_total, **side):
    n, m = sizes
    count, full = resid.shape
    length, width = context.shape
    group = min(2 * HEAD_DIM, width)
    return comm_call(
        name, collective_id, sizes, functools.partial(attention_back_main, count, gain_row),
        [(limit, smem()), (grad, vmem()), (resid, "load"), (gains, vmem())]
        + [(item, "load") for item in (weights, table, rows, qkv, context, log_total)],
        [
            ((8, full), F32, vmem()),
            ((full, 4 * width), BF16, "store"),
            ((LEFT + RIGHT + 8, group), F32, vmem()),
            ((count, full), F32, vmem()),
        ],
        [
            pltpu.VMEM((length // BLOCK, length, BLOCK), BF16),
            pltpu.VMEM((length, full), BF16),
            pltpu.VMEM((length, width), BF16),
            pltpu.VMEM((length, 3 * width), BF16),
            pltpu.VMEM((width // group, 2 * length, group), BF16),
            pltpu.VMEM((width // group, 2 * length, group), BF16),
            pltpu.VMEM((width // group, 2 * length, group), F32),
            pltpu.VMEM((width // group, 2 * length, group), F32),
            pltpu.VMEM((group, SPAN), F32),
            pltpu.VMEM((16, group), F32),
            pltpu.VMEM((n, count, full), BF16),
            pltpu.VMEM((n - 1, count, full), BF16),
        ],
        cost=50 * 10**9, **side,
    )


PAD = 32
ROWS = 64


def shifted_sets(held, low, high, size):
    for residue in range(8):
        shifts = [shift for shift in range(low, high + 1) if shift % 8 == residue]
        if shifts:
            extent = shifts[-1] - residue + size
            moved = held[residue:residue + extent]
            for shift in shifts:
                yield shift, moved[shift - residue:shift - residue + size]


def stat_rows(blocks, first, second, stats_ref):
    lane = lax.broadcasted_iota(jnp.int32, (BLOCK, BLOCK), 1)
    both = jnp.where(lane == 0, first, jnp.where(lane == 1, second, 0.0))
    stats_ref[:, blocks] = both.T[0:8]


def stat_columns(stats):
    both = jnp.concatenate([stats, jnp.zeros((BLOCK - 8, BLOCK), F32)], axis=0).T
    return both[:, 0:1], both[:, 1:2]


class Stats:
    def __init__(self, wire, mine, got):
        self.wire, self.mine, self.got = wire, mine, got
        self.copies = [
            wire.remote(mine, got.at[step - 1], "col", lax.rem(wire.me + step, wire.n))
            for step in range(1, wire.n)
        ]

    def total(self):
        for copy in self.copies:
            copy.start()
        for copy in self.copies:
            copy.wait()
        total = self.mine[...]
        for step in range(self.wire.n - 1):
            total = total + self.got[step]
        return total


def token_blocks(length, body):
    def step(index, carry):
        body(tile(index, BLOCK), index)
        return carry

    lax.fori_loop(0, length // BLOCK, step, 0)


def convolution_main(count, gain_row, taps, wire, ins, outs, scratch):
    limit_ref, resid, gains_ref, weights, taps_ref, depth_ref = ins
    after_ref, squares_ref, rows_ref, pre_ref, mixed_ref, stats_ref = outs
    kernel_ref, padded, stats_mine, stats_got, act, part, got = scratch
    length, width = mixed_ref.shape
    full = gains_ref.shape[1]
    wire.greet()
    wire.begin()
    norm_rows(wire, count, resid, gains_ref[gain_row:gain_row + 1], rows_ref)
    spread = Spread(wire, rows_ref, count)
    spread.start()
    wire.loaded()
    collect = Collect(wire, part, got)
    stats = Stats(wire, stats_mine, stats_got)
    padded[0:PAD] = jnp.zeros((PAD, width), F32)
    kernel_ref[0:taps] = taps_ref[...].astype(F32)
    spread.relay()
    wire.early()
    chunks = []
    for chunk, slot in spread.arrivals(relay=False):
        chunks.append((chunk, slot))
        rows = tile(chunk, count)
        left = rows_ref[rows]
        value_pre = matmul(left, weights[:, 0:width])
        gate_pre = matmul(left, weights[:, width:2 * width])
        pre_ref[rows, 0:width] = value_pre.astype(BF16)
        pre_ref[rows, width:2 * width] = gate_pre.astype(BF16)
        at = pl.multiple_of(chunk * count + PAD, PAD)
        keep = keep_rows(limit_ref[0], chunk * count, count)
        padded[pl.ds(at, count)] = value_pre * jax.nn.sigmoid(gate_pre) * keep

    def mix(index, carry):
        held = padded[pl.ds(pl.multiple_of(index * ROWS, ROWS), ROWS + PAD)]
        total = jnp.zeros((ROWS, width), F32)
        for shift, moved in shifted_sets(held, PAD - taps + 1, PAD, ROWS):
            tap = shift - (PAD - taps + 1)
            total = total + moved * kernel_ref[tap:tap + 1]
        mixed_ref[tile(index, ROWS)] = total
        return carry

    lax.fori_loop(0, length // ROWS, mix, 0)

    def sums(rows, index):
        mixed = mixed_ref[rows]
        stat_rows(rows, jnp.sum(mixed, axis=1, keepdims=True),
                  jnp.sum(mixed * mixed, axis=1, keepdims=True), stats_mine)

    token_blocks(length, sums)
    total = stats.total() * (1.0 / full)
    inverse = lax.rsqrt(total[1:2] - total[0:1] * total[0:1] + EPSILON)
    stats_ref[...] = jnp.concatenate([total[0:1], inverse, total[2:]], axis=0)

    def activate(rows, index):
        mean, scale = stat_columns(stats_ref[:, rows])
        scaled = (mixed_ref[rows] - mean) * scale * depth_ref[...]
        act[rows] = (scaled * jax.nn.sigmoid(scaled)).astype(BF16)

    token_blocks(length, activate)
    wire.middle()
    for chunk, slot in reversed(chunks):
        target = part.at[wire.n - 1 if slot is None else slot]
        left = act[tile(chunk, count)]

        def leave(cols, index):
            target[:, cols] = matmul_nt(left, weights[cols, 2 * width:]).astype(BF16)

        block_loop(weights.shape[0], leave)
        if slot is not None:
            collect.send(slot)
    collect.combine()
    wire.flush()
    collect.wait()
    residual(collect, 1.0, resid, limit_ref[0], after_ref, squares_ref)
    spread.finish()
    wire.end()


def convolution(sizes, name, collective_id, gain_row, limit, resid, gains, weights, kernel, depth_gain,
                **side):
    n, m = sizes
    count, full = resid.shape
    length, width = n * count, weights.shape[1] // 3
    return comm_call(
        name, collective_id, sizes,
        functools.partial(convolution_main, count, gain_row, kernel.shape[0]),
        [(limit, smem()), (resid, vmem()), (gains, vmem()), (weights, "load"), (kernel, vmem()),
         (depth_gain, vmem())],
        [
            ((count, full), F32, vmem()),
            ((16, full), F32, vmem()),
            ((length, full), BF16, "store"),
            ((length, 2 * width), BF16, "store"),
            ((length, width), F32, "store"),
            ((8, length), F32, "store"),
        ],
        [
            pltpu.VMEM((PAD, width), F32),
            pltpu.VMEM((length + PAD, width), F32),
            pltpu.VMEM((8, length), F32),
            pltpu.VMEM((n - 1, 8, length), F32),
            pltpu.VMEM((length, width), BF16),
            pltpu.VMEM((n, count, full), BF16),
            pltpu.VMEM((n - 1, count, full), BF16),
        ],
        cost=15 * 10**9, **side,
    )


def convolution_back_main(count, gain_row, taps, wire, ins, outs, scratch):
    (limit_ref, grad_ref, resid, gains_ref, weights, taps_ref, depth_ref, rows_ref, pre_ref, mixed_ref,
     stats_ref) = ins
    gain_grad_ref, wide_ref, kernel_grad_ref, depth_grad_ref, new_grad_ref = outs
    (kernel_ref, grads, padded, padded_grad, stats_mine, stats_got, sums_ref, act, pre_grad, part, got) = scratch
    length, width = mixed_ref.shape
    full = gains_ref.shape[1]
    wire.greet()
    wire.begin()
    cast_rows(wire, count, grad_ref, 1.0, grads)
    spread = Spread(wire, grads, count)
    spread.start()
    wire.loaded()
    collect = Collect(wire, part, got)
    stats = Stats(wire, stats_mine, stats_got)
    padded[0:PAD] = jnp.zeros((PAD, width), F32)
    padded_grad[length:] = jnp.zeros((PAD, width), F32)
    sums_ref[...] = jnp.zeros_like(sums_ref)
    depth_grad_ref[...] = jnp.zeros_like(depth_grad_ref)
    kernel_ref[0:taps] = taps_ref[...].astype(F32)
    kernel_grad_ref[...] = jnp.zeros_like(kernel_grad_ref)
    spread.relay()

    def regate(rows, index):
        value_pre = pre_ref[rows, 0:width].astype(F32)
        gate_pre = pre_ref[rows, width:2 * width].astype(F32)
        at = pl.multiple_of(index * BLOCK + PAD, PAD)
        keep = keep_rows(limit_ref[0], index * BLOCK, BLOCK)
        padded[pl.ds(at, BLOCK)] = value_pre * jax.nn.sigmoid(gate_pre) * keep

    token_blocks(length, regate)
    wire.early()
    chunks = []
    for chunk, slot in spread.arrivals(relay=False):
        chunks.append((chunk, slot))
        rows = tile(chunk, count)
        padded_grad[rows] = matmul(grads[rows], weights[:, 2 * width:])
    wire.middle()

    def first(rows, index):
        mean, scale = stat_columns(stats_ref[:, rows])
        normed = (mixed_ref[rows] - mean) * scale
        scaled = normed * depth_ref[...]
        sig = jax.nn.sigmoid(scaled)
        act[rows] = (scaled * sig).astype(BF16)
        scaled_grad = padded_grad[rows] * (sig + scaled * sig * (1.0 - sig))
        depth_grad_ref[...] += fold8(scaled_grad * normed)
        weighted = scaled_grad * depth_ref[...]
        padded_grad[rows] = weighted
        stat_rows(rows, jnp.sum(weighted, axis=1, keepdims=True),
                  jnp.sum(weighted * normed, axis=1, keepdims=True), stats_mine)

    token_blocks(length, first)
    total = stats.total() * (1.0 / full)
    stats_mine[...] = total

    def second(rows, index):
        mean, scale = stat_columns(stats_ref[:, rows])
        normed = (mixed_ref[rows] - mean) * scale
        one, two = stat_columns(stats_mine[:, rows])
        padded_grad[rows] = scale * (padded_grad[rows] - one - normed * two)

    token_blocks(length, second)

    def unmix(index, carry):
        rows = tile(index, ROWS)
        around = pl.ds(pl.multiple_of(index * ROWS, ROWS), ROWS + PAD)
        ahead = padded_grad[around]
        total = jnp.zeros((ROWS, width), F32)
        for shift, moved in shifted_sets(ahead, 0, taps - 1, ROWS):
            tap = taps - 1 - shift
            total = total + moved * kernel_ref[tap:tap + 1]
        here = ahead[0:ROWS]
        for shift, moved in shifted_sets(padded[around], PAD - taps + 1, PAD, ROWS):
            tap = shift - (PAD - taps + 1)
            sums_ref[tap * 8:(tap + 1) * 8] += fold8(here * moved)
        gate = jax.nn.sigmoid(pre_ref[rows, width:2 * width].astype(F32))
        through = total * keep_rows(limit_ref[0], index * ROWS, ROWS) * gate
        pre_grad[rows, 0:width] = through.astype(BF16)
        pre_grad[rows, width:2 * width] = (
            through * pre_ref[rows, 0:width].astype(F32) * (1.0 - gate)
        ).astype(BF16)
        return carry

    lax.fori_loop(0, length // ROWS, unmix, 0)
    for tap in range(taps):
        kernel_grad_ref[tap:tap + 1] = jnp.sum(sums_ref[tap * 8:(tap + 1) * 8], axis=0, keepdims=True)
    for chunk, slot in reversed(chunks):
        target = part.at[wire.n - 1 if slot is None else slot]
        left = pre_grad[tile(chunk, count)]

        def back(cols, index):
            target[:, cols] = matmul_nt(left, weights[cols, :2 * width]).astype(BF16)

        block_loop(weights.shape[0], back)
        if slot is not None:
            collect.send(slot)
    collect.combine()

    def weight_grads(rows, index):
        wide_ref[rows, :2 * width] = matmul_tn(rows_ref[:, rows], pre_grad[...]).astype(BF16)
        wide_ref[rows, 2 * width:] = matmul_tn(grads[:, rows], act[...]).astype(BF16)

    block_loop(weights.shape[0], weight_grads)
    wire.flush()
    wire.end()
    collect.wait()
    residual_back(collect, grad_ref, resid, gains_ref[gain_row:gain_row + 1], new_grad_ref,
                  gain_grad_ref)
    spread.finish()


def convolution_back(sizes, name, collective_id, gain_row, limit, grad, resid, gains, weights, kernel,
                     depth_gain, rows, pre, mixed, stats, **side):
    n, m = sizes
    count, full = resid.shape
    length, width = mixed.shape
    taps = kernel.shape[0]
    return comm_call(
        name, collective_id, sizes,
        functools.partial(convolution_back_main, count, gain_row, taps),
        [(limit, smem()), (grad, vmem()), (resid, "load"), (gains, vmem()), (weights, "load"),
         (kernel, vmem()), (depth_gain, vmem())]
        + [(item, "load") for item in (rows, pre, mixed, stats)],
        [
            ((8, full), F32, vmem()),
            ((full, 3 * width), BF16, "store"),
            ((PAD, width), F32, vmem()),
            ((8, width), F32, vmem()),
            ((count, full), F32, vmem()),
        ],
        [
            pltpu.VMEM((PAD, width), F32),
            pltpu.VMEM((length, full), BF16),
            pltpu.VMEM((length + PAD, width), F32),
            pltpu.VMEM((length + PAD, width), F32),
            pltpu.VMEM((8, length), F32),
            pltpu.VMEM((n - 1, 8, length), F32),
            pltpu.VMEM((8 * taps, width), F32),
            pltpu.VMEM((length, width), BF16),
            pltpu.VMEM((length, 2 * width), BF16),
            pltpu.VMEM((n, count, full), BF16),
            pltpu.VMEM((n - 1, count, full), BF16),
        ],
        cost=20 * 10**9, **side,
    )


def results_kernel(*refs):
    sources, targets = refs[:len(refs) // 2], refs[len(refs) // 2:]
    for source, target in zip(sources, targets):
        if source.shape != target.shape:
            target[...] = source[...].astype(target.dtype).T
        else:
            target[...] = source[...]


def results(arrays, shapes):
    return pl.pallas_call(
        results_kernel,
        name="results",
        out_shape=tuple(shapes),
        in_specs=[vmem()] * len(arrays),
        out_specs=tuple(vmem() for _ in arrays),
        compiler_params=pltpu.CompilerParams(vmem_limit_bytes=VMEM_LIMIT),
    )(*arrays)


def body(
    layer_input,
    clip_lengths,
    first_gain,
    first_up,
    first_down,
    attend_gain,
    query_weight,
    key_weight,
    value_weight,
    output_weight,
    distance_table,
    conv_gain,
    pointwise_value,
    pointwise_gate,
    depthwise_kernel,
    depthwise_gain,
    pointwise_out,
    second_gain,
    second_up,
    second_down,
    final_gain,
    output_cotangent,
):
    n = lax.axis_size("col")
    me = lax.axis_index("col")
    width, length = layer_input.shape
    full = n * width
    count = length // n

    sizes = (n, lax.axis_size("row"))
    group = min(2 * HEAD_DIM, width)
    table_wide = extend_table(distance_table, group // HEAD_DIM)
    limit = clip_lengths
    tap_count = depthwise_kernel.shape[0]
    gain_parts = [
        gain[None] for gain in (first_gain, attend_gain, conv_gain, second_gain, final_gain)
    ]
    attend_pieces = [
        (query_weight, False), (key_weight, False), (value_weight, False), (output_weight, True)
    ]
    conv_pieces = [(pointwise_value, False), (pointwise_gate, False), (pointwise_out, True)]
    hidden = first_up.shape[1]
    tokens_in = (layer_input, output_cotangent)
    if count % BLOCK:
        tokens_in = (layer_input.T, output_cotangent.T)

    (start, cot, gains, up_first, down_first, attend_weights, after_first, squares_first, rows_first,
     pre_first) = feed_forward(
        sizes, "first", 1, 0, first_up, first_down, limit,
        enter=(*tokens_in, gain_parts, attend_pieces),
    )
    (after_attend, squares_attend, rows_attend, qkv, context, log_total, conv_weights,
     up_second) = attention(
        sizes, "attend", 2, 1, limit, after_first, gains, attend_weights, table_wide,
        gathers=[conv_pieces, [(second_up, False)]],
    )
    depth_row = depthwise_gain[None]
    (after_conv, squares_conv, rows_conv, conv_pre, mixed, stats, down_second) = convolution(
        sizes, "convolve", 3, 2, limit, after_attend, gains, conv_weights, depthwise_kernel, depth_row,
        gathers=[[(second_down, True)]],
    )
    (grad_second, final_part, out_tokens, squares_second, rows_second, pre_second) = feed_forward(
        sizes, "second", 4, 3, up_second, down_second, limit, resid=after_conv, gains=gains, turn=cot
    )

    second_part, second_up_wide, second_down_wide, grad_conv, layer_output = feed_forward_back(
        sizes, "second_back", 5, 3, grad_second, after_conv, gains, up_second, down_second,
        rows_second, pre_second, tokens=out_tokens,
    )
    conv_part, conv_wide, kernel_part, depth_part, grad_attend, second_up_grad = convolution_back(
        sizes, "convolve_back", 6, 2, limit, grad_conv, after_attend, gains, conv_weights,
        depthwise_kernel, depth_row, rows_conv, conv_pre, mixed, stats,
        reduces=[(second_up_wide, [(hidden, False)])],
    )
    (attend_part, attend_wide, table_part, grad_first, second_down_grad, value_grad, gate_grad,
     out_grad) = attention_back(
        sizes, "attend_back", 7, 1, limit, grad_attend, after_first, gains, attend_weights,
        table_wide, rows_attend, qkv, context, log_total,
        reduces=[
            (second_down_wide, [(hidden, True)]),
            (conv_wide, [(width, False), (width, False), (width, True)]),
        ],
    )
    (first_sum, attend_sum, conv_sum, second_sum, final_sum, table_sum, masked_rms, kernel_sum,
     depth_sum, first_up_grad, first_down_grad, grad_tokens, query_grad, key_grad, attend_value_grad,
     output_grad) = feed_forward_back(
        sizes, "first_back", 0, 0, grad_first, start, gains, up_first, down_first, rows_first,
        pre_first, taps=tap_count,
        leave=(
            limit, (attend_part, conv_part, second_part, final_part),
            (squares_first, squares_attend, squares_conv, squares_second), table_part, kernel_part,
            depth_part,
        ),
        reduces=[(attend_wide, [(width, False), (width, False), (width, False), (width, True)])],
    )

    arrays = [
        layer_output, grad_tokens, first_sum, first_up_grad, first_down_grad, attend_sum, query_grad,
        key_grad, attend_value_grad, output_grad, table_sum, conv_sum, value_grad, gate_grad, kernel_sum,
        depth_sum, out_grad, second_sum, second_up_grad, second_down_grad, final_sum, masked_rms,
    ]
    shapes = [jax.ShapeDtypeStruct(array.shape, array.dtype) for array in arrays]
    shapes[1] = jax.ShapeDtypeStruct(grad_tokens.shape[::-1], F32)
    arrays = results(arrays, shapes)
    outputs = [array[0] if array.shape[0] == 1 else array for array in arrays]
    return (*outputs[:-1], outputs[-1][:, 0])


def solution(mesh):
    in_specs = (
        P("col", "row"),
        P("row"),
        P("col"),
        P("row", "col"),
        P("col", "row"),
        P("col"),
        P("row", "col"),
        P("row", "col"),
        P("row", "col"),
        P("col", "row"),
        P(),
        P("col"),
        P("row", "col"),
        P("row", "col"),
        P(None, "col"),
        P("col"),
        P("col", "row"),
        P("col"),
        P("row", "col"),
        P("col", "row"),
        P("col"),
        P("col", "row"),
    )
    out_specs = (
        P("col", "row"),
        P("col", "row"),
        P("col"),
        P("row", "col"),
        P("col", "row"),
        P("col"),
        P("row", "col"),
        P("row", "col"),
        P("row", "col"),
        P("col", "row"),
        P(),
        P("col"),
        P("row", "col"),
        P("row", "col"),
        P(None, "col"),
        P("col"),
        P("col", "row"),
        P("col"),
        P("row", "col"),
        P("col", "row"),
        P("col"),
        P(),
    )
    return jax.shard_map(body, mesh=mesh, in_specs=in_specs, out_specs=out_specs, check_vma=False)
```

time: 673 us -> 534 us (0.79)
  Pallas kernels: 613 us -> 521 us
  local copies, waits for them, and re-layouts: 28.1 us -> 3.6 us
  other arithmetic: 17.6 us -> 0.01 us
    pallas_call x8, Pallas kernels: 613 us -> 517 us  [comm_call(): pl.pallas_call(kernel, name=name, out_shape=tuple(out_shapes), in_specs=i...]
    unnamed x47 -> x3, local copies, waits for them, and re-layouts: 15.5 us -> 1.52 us
    reduce_sum x10 -> x0, other arithmetic: 8.47 us -> none  [the longest x4 5.56 us: body(): jnp.sum(piece[at:at + 8])]
where the time goes in v2:
time: 534 us; the launch traced here: 527 us
  Pallas kernels  521 us (98%)
    pallas_call x8, Pallas kernels, comm_call(): pl.pallas_call(kernel, name=name, out_shape=tuple(out_shapes), in_specs=i...  517 us

profile of v2, /device:TPU:0, one launch (start us, length us, event | category | flops | bytes accessed | tf_op | source)
XLA Modules:
  0.0 526.7 jit_solution(12928917936765187676)
XLA Ops:
  0.7 0.0 copy-start
  1.3 0.0 copy-done
  1.4 0.3 convolution_convert_fusion
  1.7 0.8 copy.46.refs_4_.refs_5_
  2.4 80.2 %first.1 = (f32[256,1024]{1,0:T(8,128)}, f32[256,1024]{1,0:T(8,128)}, f32[8,1024]{1,0:T(8,128)}, bf16[1024,1024]{1,0:T(8,128)(2,1)}, bf16[1024,1024]{1,0:T(8,128...) custom-call(s32[1]{0:T(128)S(6)} %copy.49.refs_0_.refs_7_, ...), custom_call_target="tpu_custom_call" | custom-call | flops 1000000000 | bytes 100000000 | tf_op jit(solution)/shard_map/first/pallas_call | solution.py:716
  82.7 51.1 %attend.1 = (f32[256,1024]{1,0:T(8,128)}, f32[16,1024]{1,0:T(8,128)}, bf16[1024,1024]{1,0:T(8,128)(2,1)}, bf16[1024,768]{1,0:T(8,128)(2,1)}, bf16[1024,256]{1,0:...) custom-call(s32[1]{0:T(128)S(6)} %copy.49.refs_0_.refs_7_, ...), custom_call_target="tpu_custom_call" | custom-call | flops 20000000000 | bytes 100000000 | tf_op jit(solution)/shard_map/attend/pallas_call | solution.py:716
  133.8 54.7 %convolve.1 = (f32[256,1024]{1,0:T(8,128)}, f32[16,1024]{1,0:T(8,128)}, bf16[1024,1024]{1,0:T(8,128)(2,1)}, bf16[1024,512]{1,0:T(8,128)(2,1)}, f32[1024,256]{1,0...) custom-call(s32[1]{0:T(128)S(6)} %copy.49.refs_0_.refs_7_, f32[256,1024]{1,0:T(8,128)} %get-tuple-element.113.refs_1_.refs_2_, ...), custom_call_target="tpu_custom_call" | custom-call | flops 15000000512 | bytes 100000000 | tf_op jit(solution)/shard_map/convolve/pallas_call | solution.py:716
  188.5 52.5 %second.1 = (f32[256,1024]{1,0:T(8,128)}, f32[8,1024]{1,0:T(8,128)}, bf16[1024,256]{1,0:T(8,128)(2,1)}, f32[16,1024]{1,0:T(8,128)}, bf16[1024,1024]{1,0:T(8,128)(2,1)}, /*index=5*/bf16[1024,1024]{1,0:T(8,128)(2,1)}) custom-call(s32[1]{0:T(128)S(6)} %copy.49.refs_0_.refs_7_, f32[256,1024]{1,0:T(8,128)} %get-tuple-element.115.refs_1_, ...), custom_call_target="tpu_custom_call" | custom-call | flops 1000000000 | bytes 100000000 | tf_op jit(solution)/shard_map/second/pallas_call | solution.py:716
  241.0 42.0 %second_back.1 = (f32[8,1024]{1,0:T(8,128)}, bf16[1024,1024]{1,0:T(8,128)(2,1)}, bf16[1024,1024]{1,0:T(8,128)(2,1)}, f32[256,1024]{1,0:T(8,128)}, bf16[256,1024]{1,0:T(8,128)(2,1)}) custom-call(f32[256,1024]{1,0:T(8,128)} %get-tuple-element.119.refs_0_, f32[256,1024]{1,0:T(8,128)} %get-tuple-element.115.refs_1_, ...), custom_call_target="tpu_custom_call" | custom-call | flops 1000000000 | bytes 100000000 | tf_op jit(solution)/shard_map/second_back/pallas_call | solution.py:716
  283.1 59.5 %convolve_back.1 = (f32[8,1024]{1,0:T(8,128)}, bf16[1024,768]{1,0:T(8,128)(2,1)}, f32[32,256]{1,0:T(8,128)}, f32[8,256]{1,0:T(8,128)}, f32[256,1024]{1,0:T(8,128)}, /*index=5*/f32[128,1024]{1,0:T(8,128)}) custom-call(s32[1]{0:T(128)S(6)} %copy.49.refs_0_.refs_7_, f32[256,1024]{1,0:T(8,128)} %get-tuple-element.124.refs_1_, ...), custom_call_target="tpu_custom_call" | custom-call | flops 20000000000 | bytes 100000000 | tf_op jit(solution)/shard_map/convolve_back/pallas_call | solution.py:716
  342.5 81.5 %attend_back.1 = (f32[8,1024]{1,0:T(8,128)}, bf16[1024,1024]{1,0:T(8,128)(2,1)}, f32[80,128]{1,0:T(8,128)}, f32[256,1024]{1,0:T(8,128)}, f32[1024,128]{1,0:T(8,1...) custom-call(s32[1]{0:T(128)S(6)} %copy.49.refs_0_.refs_7_, ...), custom_call_target="tpu_custom_call" | custom-call | flops 49999998976 | bytes 100000000 | tf_op jit(solution)/shard_map/attend_back/pallas_call | solution.py:716
  424.1 95.1 %first_back.1 = (f32[1,256]{1,0:T(1,128)}, f32[1,256]{1,0:T(1,128)}, f32[1,256]{1,0:T(1,128)}, f32[1,256]{1,0:T(1,128)}, f32[1,256]{1,0:T(1,128)}, /*index=5*/f3...) custom-call(f32[256,1024]{1,0:T(8,128)} %get-tuple-element.137.refs_, ...), custom_call_target="tpu_custom_call" | custom-call | flops 1000000000 | bytes 100000000 | tf_op jit(solution)/shard_map/first_back/pallas_call | solution.py:716
  519.2 4.6 results.1
  523.8 1.3 slice_reduce_fusion
  525.1 1.5 copy.48
  (2 shorter events, 0.0 us)
Async XLA Ops:
  0.7 0.7 copy-start

commit v3 on v2

--- a/solution.py
+++ b/solution.py
@@ -447,54 +447,79 @@
         self.keep = [wire.local(part, out) for part, out in zip(self.parts, outs)]
         self.held, self.pair, self.got = held, pair, got
         self.count = held.shape[1]
-        other = 1 - wire.core
         self.load = []
         if load:
             self.load = [
                 wire.local(grads.at[tile(layer * 2 + wire.core, self.count)], held.at[layer])
                 for layer in range(wire.layers)
             ]
-        self.swap = [
-            wire.remote(grads.at[tile(layer * 2 + other, self.count)], pair.at[layer], "row",
-                        wire.partner)
-            for layer in range(wire.layers)
-        ]
-        self.along = []
-        for step in range(1, wire.layers):
-            layer = lax.rem(wire.layer + step, wire.layers)
-            self.along.append(
-                wire.remote(held.at[layer], got.at[step - 1], "row", wire.layer_peer(step))
-            )
+        self.base = wire.used
+        wire.used += 2 * wire.layers
+
+    def layer_of(self, step):
+        return lax.rem(self.wire.layer + 1 + step, self.wire.layers)
+
+    def between(self, source, target, slot, peer):
+        wire = self.wire
+        return pltpu.make_async_remote_copy(
+            src_ref=source, dst_ref=target, send_sem=wire.send_sem.at[self.base + slot],
+            recv_sem=wire.recv_sem.at[self.base + slot], device_id={"row": peer}, device_id_type=MESH,
+        )
+
+    def swap(self, step):
+        layer = self.layer_of(step)
+        block = layer * 2 + 1 - self.wire.core
+        return self.between(self.grads.at[tile(block, self.count)], self.pair.at[layer], step,
+                            self.wire.partner)
+
+    def along(self, step):
+        layer = self.layer_of(step)
+        return self.between(self.held.at[layer], self.got.at[step], self.wire.layers + step,
+                            layer * 2 + self.wire.core)
+
+    def begin_step(self, step):
+        self.swap(step).start()
+
+    def early_step(self, step):
+        self.swap(step).wait()
+        layer = self.layer_of(step)
+        size = min(32, self.count)
+
+        def add(rows, index):
+            if self.load:
+                mine = self.held[layer, rows]
+            else:
+                at = (layer * 2 + self.wire.core) * self.count + index * size
+                mine = self.grads[pl.ds(pl.multiple_of(at, size), size)]
+            self.held[layer, rows] = (
+                mine.astype(F32) + self.pair[layer, rows].astype(F32)
+            ).astype(BF16)
+
+        row_loop(self.count, add)
+        pl.when(step < self.wire.layers - 1)(lambda: self.along(step).start())
 
     def begin(self):
-        for copy in self.swap + self.load:
+        for step in range(self.wire.layers):
+            self.begin_step(step)
+        for copy in self.load:
             copy.start()
 
     def early(self):
-        for copy in self.load + self.swap:
+        for copy in self.load:
             copy.wait()
-        size = min(32, self.count)
-        for layer in range(self.wire.layers):
-            def add(rows, index, layer=layer):
-                if self.load:
-                    mine = self.held[layer, rows]
-                else:
-                    at = (layer * 2 + self.wire.core) * self.count + index * size
-                    mine = self.grads[pl.ds(pl.multiple_of(at, size), size)]
-                self.held[layer, rows] = (
-                    mine.astype(F32) + self.pair[layer, rows].astype(F32)
-                ).astype(BF16)
-
-            row_loop(self.count, add)
-        for copy in self.along:
-            copy.start()
+
+        def one(step, carry):
+            self.early_step(step)
+            return carry
+
+        lax.fori_loop(0, self.wire.layers, one, 0)
 
     def middle(self):
         pass
 
     def end(self):
-        for copy in self.along:
-            copy.wait()
+        for step in range(self.wire.layers - 1):
+            self.along(step).wait()
 
         def add(rows, index):
             total = self.held[self.wire.layer, rows].astype(F32)
@@ -796,6 +821,35 @@
     here = wire.local(pieces.at[wire.me], mine)
     here.start()
     return copies + [here]
+
+
+def send_shares(wire, chunks, collect, share, last=None):
+    part = collect.part
+    if wire.n == 4:
+        across_bit, along_bit = lax.rem(wire.me, 2), wire.me // 2
+
+        def turn(step, carry):
+            left = 3 - step
+            flip_across, flip_along = lax.rem(left, 2), left // 2
+            chunk = (
+                across_bit + flip_across - 2 * across_bit * flip_across
+                + 2 * (along_bit + flip_along - 2 * along_bit * flip_along)
+            )
+            share(chunk, part.at[lax.rem(left + 3, 4)])
+            for place in range(3):
+                pl.when(step == place)(lambda place=place: collect.send(2 - place))
+            if last is not None:
+                pl.when(step == 2)(last)
+            return carry
+
+        lax.fori_loop(0, 4, turn, 0)
+    else:
+        for chunk, slot in reversed(chunks):
+            share(chunk, part.at[wire.n - 1 if slot is None else slot])
+            if slot is not None:
+                collect.send(slot)
+        if last is not None:
+            last()
 
 
 def feed_forward_first(count, chunk, rows_ref, up, pre_ref, act):
@@ -1074,6 +1128,7 @@
         gain_grad_ref, up_grad_ref, down_grad_ref, last_ref, turned_ref = outs
         new_grad_ref = last_ref
         items = []
+        down_job = up_job = None
     gains = gains_ref[gain_row:gain_row + 1]
     wire.greet()
     wire.begin()
@@ -1100,9 +1155,8 @@
             item.begin()
     wire.loaded()
     collect = Collect(wire, part, got)
-    for chunk, slot in spread.arrivals():
+    def first_leg(chunk):
         rows = tile(chunk, count)
-        target = part.at[wire.n - 1 if slot is None else slot]
         left = grads[rows]
 
         def first(cols, index):
@@ -1113,7 +1167,10 @@
             pre_grad[rows, cols] = (act_grad * (sig + pre * sig * (1.0 - sig))).astype(BF16)
 
         block_loop(hidden, first)
-        through = pre_grad[rows]
+
+    def second_leg(chunk, slot):
+        target = part.at[wire.n - 1 if slot is None else slot]
+        through = pre_grad[tile(chunk, count)]
 
         def second(cols, index):
             target[:, cols] = matmul_nt(through, up[cols]).astype(BF16)
@@ -1121,6 +1178,36 @@
         block_loop(full, second)
         if slot is not None:
             collect.send(slot)
+
+    def weight_rows(left_ref, right_ref, out, rows):
+        left = left_ref[:, rows]
+
+        def piece(cols, index):
+            out[rows, cols] = matmul_tn(left, right_ref[:, cols]).astype(BF16)
+
+        block_loop(hidden, piece)
+
+    def weight_grad(left_ref, right_ref, out, job=None):
+        if job is None:
+            block_loop(full, lambda rows, index: weight_rows(left_ref, right_ref, out, rows))
+            return
+
+        def layer(step, carry):
+            weight_rows(left_ref, right_ref, out, tile(job.layer_of(step), 2 * job.count))
+            job.begin_step(step)
+            pl.when(step > 0)(lambda: job.early_step(step - 1))
+            return carry
+
+        lax.fori_loop(0, wire.layers, layer, 0)
+        job.early_step(wire.layers - 1)
+
+    late_leg = None
+    for place, (chunk, slot) in enumerate(spread.arrivals()):
+        first_leg(chunk)
+        if leave and place == wire.n - 1:
+            late_leg = (chunk, slot)
+        else:
+            second_leg(chunk, slot)
         if slot is None:
             wire.early()
             for item in items:
@@ -1131,25 +1218,14 @@
             for item in items:
                 item.middle()
     wire.middle()
-    size = min(256, hidden)
-
-    def weight_grad(left_ref, right_ref, out):
-        for start in range(0, hidden, size):
-            cols = slice(start, start + size)
-
-            def block(rows, index):
-                out[rows, cols] = matmul_tn(left_ref[:, rows], right_ref[:, cols]).astype(BF16)
-
-            block_loop(full, block)
-
-    weight_grad(grads, act, down_grad_ref)
+    weight_grad(grads, act, down_grad_ref, down_job)
     if leave:
-        down_job.begin()
-    collect.combine()
-    weight_grad(rows_ref, pre_grad, up_grad_ref)
-    if leave:
-        up_job.begin()
-        down_job.early()
+        second_leg(*late_leg)
+        weight_grad(rows_ref, pre_grad, up_grad_ref, up_job)
+        collect.combine()
+    else:
+        collect.combine()
+        weight_grad(rows_ref, pre_grad, up_grad_ref)
     wire.flush()
     collect.wait()
     residual_back(collect, grad_ref, resid, gains, new_grad_ref, gain_grad_ref)
@@ -1158,7 +1234,6 @@
             first_pieces[piece] = gain_grad_ref[:, piece * width:(piece + 1) * width]
         gain_item.begin()
         late = send_pieces(wire, count, new_grad_ref, pieces, last_ref)
-        up_job.early()
         gain_item.early()
         for item in items:
             item.end()
@@ -1358,7 +1433,7 @@
 
 
 def attend_blocks(first, blocks, width, group, qkv_ref, table_ref, far_ref, keys, values, context_ref,
-                  log_ref):
+                  log_ref, weights):
     length = qkv_ref.shape[0]
     heads = group // HEAD_DIM
     parts = width // group
@@ -1380,14 +1455,28 @@
             )
         else:
             scores = matmul_nt(query, keys[part, window]) + matmul_nt(extra, far_ref[index])
-        near = scores[:, :WINDOW] + near_terms(query, table_ref[...], at, length)
-        scores = jnp.concatenate([near, scores[:, WINDOW:]], axis=1)
-        peak = jnp.max(scores, axis=1, keepdims=True)
-        weights = jnp.exp(scores - peak)
-        total = jnp.sum(weights, axis=1, keepdims=True)
-        mixed = matmul(weights.astype(BF16), values[part, window]) * (1.0 / total)
+        near = near_terms(query, table_ref[...], at, length)
+        size = 32
+        peaks, totals = [], []
+        for start in range(0, heads * BLOCK, size):
+            some = slice(start, start + size)
+            first_part = scores[some, :WINDOW] + near[some]
+            last_part = scores[some, WINDOW:]
+            peak = jnp.maximum(
+                jnp.max(first_part, axis=1, keepdims=True), jnp.max(last_part, axis=1, keepdims=True)
+            )
+            first_part = jnp.exp(first_part - peak)
+            last_part = jnp.exp(last_part - peak)
+            weights[some, :WINDOW] = first_part.astype(BF16)
+            weights[some, WINDOW:] = last_part.astype(BF16)
+            peaks.append(peak)
+            totals.append(
+                jnp.sum(first_part, axis=1, keepdims=True) + jnp.sum(last_part, axis=1, keepdims=True)
+            )
+        total = jnp.concatenate(totals, axis=0)
+        mixed = matmul(weights[...], values[part, window]) * (1.0 / total)
         context_ref[rows, cols] = own_lanes(mixed, group).astype(BF16)
-        log = peak + jnp.log(total)
+        log = jnp.concatenate(peaks, axis=0) + jnp.log(total)
         lane = lax.broadcasted_iota(jnp.int32, (BLOCK, BLOCK), 1)
         square = jnp.where(lane == 0, log[0:BLOCK], 0.0)
         for head in range(1, heads):
@@ -1399,7 +1488,8 @@
 
 
 def attend_back_core(width, group, qkv_ref, table_ref, far_ref, log_ref, grad_ref, out_ref,
-                     table_grad_ref, keys, values, key_grad, value_grad, slot_grad, end_grad):
+                     table_grad_ref, keys, values, key_grad, value_grad, slot_grad, end_grad, probs,
+                     prob_grads, back):
     length = qkv_ref.shape[0]
     heads = group // HEAD_DIM
     parts = width // group
@@ -1434,30 +1524,47 @@
         query = by_head(query_rows, group)
         extra = far_queries(query_rows, group)
         grad = by_head(grad_ref[rows, cols], group)
+        query_wide = [query, extra]
         if group == 2 * HEAD_DIM:
-            key_wide = jnp.concatenate([key_rows, far_rows], axis=1)
-            scores = matmul_nt(key_wide, jnp.concatenate([query, extra], axis=1))
+            query_wide = [jnp.concatenate(query_wide, axis=1)]
+            key_wide = [jnp.concatenate([key_rows, far_rows], axis=1)]
         else:
-            scores = matmul_nt(key_rows, query) + matmul_nt(far_rows, extra)
-        near = scores[:WINDOW] + near_terms(query, table_ref[...], at, length).T
-        scores = jnp.concatenate([near, scores[WINDOW:]], axis=0)
+            key_wide = [key_rows, far_rows]
+        near = near_terms(query, table_ref[...], at, length)
         log = jnp.concatenate([log_ref[part, head:head + 1, rows] for head in range(heads)], axis=1)
-        probs = jnp.exp(scores - log)
-        prob_grad = matmul_nt(values[part, window], grad)
-        row_dot = jnp.sum(probs * prob_grad, axis=0, keepdims=True)
-        score_grad = (probs * (prob_grad - row_dot)).astype(BF16)
-        value_grad[part, window] += matmul(probs.astype(BF16), grad)
-        key_grad[part, window] += matmul(score_grad, query)
-        turned_back = score_grad.T
+        value_rows = values[part, window]
+        row_dot = jnp.zeros((8, heads * BLOCK), F32)
+        for start in range(0, length, BLOCK):
+            some = slice(start, start + BLOCK)
+            scores = sum(
+                matmul_nt(left[some], right) for left, right in zip(key_wide, query_wide)
+            )
+            if start < WINDOW:
+                scores = scores + near[:, some].T
+            prob = jnp.exp(scores - log)
+            prob_grad = matmul_nt(value_rows[some], grad)
+            row_dot = row_dot + fold8(prob * prob_grad)
+            probs[some] = prob
+            prob_grads[some] = prob_grad
+        row_dot = jnp.sum(row_dot, axis=0, keepdims=True)
+        for start in range(0, length, BLOCK):
+            some = slice(start, start + BLOCK)
+            there = pl.ds(pl.multiple_of(window.start + start, BLOCK), BLOCK)
+            prob = probs[some]
+            score_grad = (prob * (prob_grads[some] - row_dot)).astype(BF16)
+            value_grad[part, there] += matmul(prob.astype(BF16), grad)
+            key_grad[part, there] += matmul(score_grad, query)
+            back[:, some] = score_grad.T
+        turned_back = back[...]
         if group == 2 * HEAD_DIM:
-            both = matmul(turned_back, key_wide)
+            both = matmul(turned_back, key_wide[0])
             direct, ends = both[:, :group], both[:, group:]
         else:
             direct, ends = matmul(turned_back, key_rows), matmul(turned_back, far_rows)
         left_sum, right_sum = ends[:, HEAD_DIM + 1:HEAD_DIM + 2], ends[:, HEAD_DIM + 2:HEAD_DIM + 3]
-        query_wide = query.astype(F32)
-        end_grad[0:8] += fold8(left_sum * query_wide)
-        end_grad[8:16] += fold8(right_sum * query_wide)
+        query_full = query.astype(F32)
+        end_grad[0:8] += fold8(left_sum * query_full)
+        end_grad[8:16] += fold8(right_sum * query_full)
         near_grad = jnp.where(
             near_mask(at, length), turned_back[:, :WINDOW], jnp.asarray(0.0, BF16)
         )
@@ -1508,7 +1615,7 @@
 def attention_main(count, gain_row, wire, ins, outs, scratch):
     limit_ref, resid, gains_ref, weights, table_ref = ins
     after_ref, squares_ref, rows_ref, qkv_ref, context_ref, log_ref = outs
-    far_ref, keys, values, part, got = scratch
+    far_ref, keys, values, weights_ref, part, got = scratch
     width = context_ref.shape[1]
     group = keys.shape[2]
     wire.greet()
@@ -1532,23 +1639,24 @@
 
         block_loop(3 * width, project)
     duplicate(qkv_ref, width, group, keys, values)
+    wire.side[0].middle()
     size = max(count, BLOCK)
-    for chunk, slot in reversed(chunks):
-        first = chunk * count // BLOCK
-        attend_blocks(first, size // BLOCK, width, group, qkv_ref, table_ref, far_ref, keys, values,
-                      context_ref, log_ref)
-        target = part.at[wire.n - 1 if slot is None else slot]
+
+    def share(chunk, target):
+        attend_blocks(chunk * count // BLOCK, size // BLOCK, width, group, qkv_ref, table_ref, far_ref,
+                      keys, values, context_ref, log_ref, weights_ref)
         left = context_ref[tile(chunk, count)]
 
         def leave(cols, index):
             target[:, cols] = matmul_nt(left, weights[cols, 3 * width:]).astype(BF16)
 
         block_loop(weights.shape[0], leave)
-        if slot is not None:
-            collect.send(slot)
-        if slot == 0:
-            collect.combine()
-            wire.middle()
+
+    def last():
+        collect.combine()
+        wire.side[1].middle()
+
+    send_shares(wire, chunks, collect, share, last)
     wire.flush()
     collect.wait()
     residual(collect, 1.0, resid, limit_ref[0], after_ref, squares_ref)
@@ -1576,6 +1684,7 @@
             pltpu.VMEM((length // BLOCK, length, BLOCK), BF16),
             pltpu.VMEM((width // group, 2 * length, group), BF16),
             pltpu.VMEM((width // group, 2 * length, group), BF16),
+            pltpu.VMEM((group // HEAD_DIM * BLOCK, length), BF16),
             pltpu.VMEM((n, count, full), BF16),
             pltpu.VMEM((n - 1, count, full), BF16),
         ],
@@ -1587,8 +1696,8 @@
     (limit_ref, grad_ref, resid, gains_ref, weights, table_ref, rows_ref, qkv_ref, context_ref,
      log_ref) = ins
     gain_grad_ref, wide_ref, table_grad_ref, new_grad_ref = outs
-    (far_ref, grads, context_grad, qkv_grad, keys, values, key_grad, value_grad, slot_grad, end_grad, part,
-     got) = scratch
+    (far_ref, grads, context_grad, qkv_grad, keys, values, key_grad, value_grad, slot_grad, end_grad,
+     probs, prob_grads, back, part, got) = scratch
     width = context_ref.shape[1]
     group = keys.shape[2]
     wire.greet()
@@ -1608,17 +1717,17 @@
         context_grad[rows] = matmul(grads[rows], weights[:, 3 * width:]).astype(BF16)
     wire.middle()
     attend_back_core(width, group, qkv_ref, table_ref, far_ref, log_ref, context_grad, qkv_grad,
-                     table_grad_ref, keys, values, key_grad, value_grad, slot_grad, end_grad)
-    for chunk, slot in reversed(chunks):
-        target = part.at[wire.n - 1 if slot is None else slot]
+                     table_grad_ref, keys, values, key_grad, value_grad, slot_grad, end_grad, probs,
+                     prob_grads, back)
+    def share(chunk, target):
         left = qkv_grad[tile(chunk, count)]
 
         def back(cols, index):
             target[:, cols] = matmul_nt(left, weights[cols, :3 * width]).astype(BF16)
 
         block_loop(weights.shape[0], back)
-        if slot is not None:
-            collect.send(slot)
+
+    send_shares(wire, chunks, collect, share)
     collect.combine()
 
     def weight_grads(rows, index):
@@ -1661,6 +1770,9 @@
             pltpu.VMEM((width // group, 2 * length, group), F32),
             pltpu.VMEM((group, SPAN), F32),
             pltpu.VMEM((16, group), F32),
+            pltpu.VMEM((length, group // HEAD_DIM * BLOCK), F32),
+            pltpu.VMEM((length, group // HEAD_DIM * BLOCK), F32),
+            pltpu.VMEM((group // HEAD_DIM * BLOCK, length), BF16),
             pltpu.VMEM((n, count, full), BF16),
             pltpu.VMEM((n - 1, count, full), BF16),
         ],
@@ -1689,7 +1801,7 @@
 
 
 def stat_columns(stats):
-    both = jnp.concatenate([stats, jnp.zeros((BLOCK - 8, BLOCK), F32)], axis=0).T
+    both = jnp.concatenate([stats, jnp.zeros((BLOCK - 8, stats.shape[1]), F32)], axis=0).T
     return both[:, 0:1], both[:, 1:2]
 
 
@@ -1772,24 +1884,28 @@
     inverse = lax.rsqrt(total[1:2] - total[0:1] * total[0:1] + EPSILON)
     stats_ref[...] = jnp.concatenate([total[0:1], inverse, total[2:]], axis=0)
 
-    def activate(rows, index):
-        mean, scale = stat_columns(stats_ref[:, rows])
-        scaled = (mixed_ref[rows] - mean) * scale * depth_ref[...]
-        act[rows] = (scaled * jax.nn.sigmoid(scaled)).astype(BF16)
-
-    token_blocks(length, activate)
-    wire.middle()
-    for chunk, slot in reversed(chunks):
-        target = part.at[wire.n - 1 if slot is None else slot]
-        left = act[tile(chunk, count)]
+    def share(chunk, target):
+        def activate(index, carry):
+            rows = tile(chunk * count // BLOCK + index, BLOCK)
+            mean, scale = stat_columns(stats_ref[:, rows])
+            scaled = (mixed_ref[rows] - mean) * scale * depth_ref[...]
+            act[tile(index, BLOCK)] = (scaled * jax.nn.sigmoid(scaled)).astype(BF16)
+            return carry
+
+        lax.fori_loop(0, -(-count // BLOCK), activate, 0)
+        if count % BLOCK:
+            at = lax.rem(chunk * count, BLOCK)
+            left = act[pl.ds(pl.multiple_of(at, count), count)]
+        else:
+            left = act[...]
 
         def leave(cols, index):
             target[:, cols] = matmul_nt(left, weights[cols, 2 * width:]).astype(BF16)
 
         block_loop(weights.shape[0], leave)
-        if slot is not None:
-            collect.send(slot)
-    collect.combine()
+
+    send_shares(wire, chunks, collect, share, collect.combine)
+    wire.middle()
     wire.flush()
     collect.wait()
     residual(collect, 1.0, resid, limit_ref[0], after_ref, squares_ref)
@@ -1820,7 +1936,7 @@
             pltpu.VMEM((length + PAD, width), F32),
             pltpu.VMEM((8, length), F32),
             pltpu.VMEM((n - 1, 8, length), F32),
-            pltpu.VMEM((length, width), BF16),
+            pltpu.VMEM((max(count, BLOCK), width), BF16),
             pltpu.VMEM((n, count, full), BF16),
             pltpu.VMEM((n - 1, count, full), BF16),
         ],
@@ -1892,40 +2008,45 @@
 
     token_blocks(length, second)
 
-    def unmix(index, carry):
-        rows = tile(index, ROWS)
+    def share(chunk, target):
+        def unmix(index, carry):
+            start = chunk * count + index * ROWS
+            rows = pl.ds(pl.multiple_of(start, ROWS), ROWS)
+            ahead = padded_grad[pl.ds(pl.multiple_of(start, ROWS), ROWS + PAD)]
+            total = jnp.zeros((ROWS, width), F32)
+            for shift, moved in shifted_sets(ahead, 0, taps - 1, ROWS):
+                tap = taps - 1 - shift
+                total = total + moved * kernel_ref[tap:tap + 1]
+            gate = jax.nn.sigmoid(pre_ref[rows, width:2 * width].astype(F32))
+            through = total * keep_rows(limit_ref[0], start, ROWS) * gate
+            pre_grad[rows, 0:width] = through.astype(BF16)
+            pre_grad[rows, width:2 * width] = (
+                through * pre_ref[rows, 0:width].astype(F32) * (1.0 - gate)
+            ).astype(BF16)
+            return carry
+
+        lax.fori_loop(0, count // ROWS, unmix, 0)
+        left = pre_grad[tile(chunk, count)]
+
+        def back(cols, index):
+            target[:, cols] = matmul_nt(left, weights[cols, :2 * width]).astype(BF16)
+
+        block_loop(weights.shape[0], back)
+
+    send_shares(wire, chunks, collect, share)
+    collect.combine()
+
+    def tap_grads(index, carry):
+        here = padded_grad[tile(index, ROWS)]
         around = pl.ds(pl.multiple_of(index * ROWS, ROWS), ROWS + PAD)
-        ahead = padded_grad[around]
-        total = jnp.zeros((ROWS, width), F32)
-        for shift, moved in shifted_sets(ahead, 0, taps - 1, ROWS):
-            tap = taps - 1 - shift
-            total = total + moved * kernel_ref[tap:tap + 1]
-        here = ahead[0:ROWS]
         for shift, moved in shifted_sets(padded[around], PAD - taps + 1, PAD, ROWS):
             tap = shift - (PAD - taps + 1)
             sums_ref[tap * 8:(tap + 1) * 8] += fold8(here * moved)
-        gate = jax.nn.sigmoid(pre_ref[rows, width:2 * width].astype(F32))
-        through = total * keep_rows(limit_ref[0], index * ROWS, ROWS) * gate
-        pre_grad[rows, 0:width] = through.astype(BF16)
-        pre_grad[rows, width:2 * width] = (
-            through * pre_ref[rows, 0:width].astype(F32) * (1.0 - gate)
-        ).astype(BF16)
         return carry
 
-    lax.fori_loop(0, length // ROWS, unmix, 0)
+    lax.fori_loop(0, length // ROWS, tap_grads, 0)
     for tap in range(taps):
         kernel_grad_ref[tap:tap + 1] = jnp.sum(sums_ref[tap * 8:(tap + 1) * 8], axis=0, keepdims=True)
-    for chunk, slot in reversed(chunks):
-        target = part.at[wire.n - 1 if slot is None else slot]
-        left = pre_grad[tile(chunk, count)]
-
-        def back(cols, index):
-            target[:, cols] = matmul_nt(left, weights[cols, :2 * width]).astype(BF16)
-
-        block_loop(weights.shape[0], back)
-        if slot is not None:
-            collect.send(slot)
-    collect.combine()
 
     def weight_grads(rows, index):
         wide_ref[rows, :2 * width] = matmul_tn(rows_ref[:, rows], pre_grad[...]).astype(BF16)
@@ -1979,7 +2100,9 @@
 def results_kernel(*refs):
     sources, targets = refs[:len(refs) // 2], refs[len(refs) // 2:]
     for source, target in zip(sources, targets):
-        if source.shape != target.shape:
+        if target.shape[0] == 1 and source.shape[0] == 8:
+            target[...] = source[...].T[0:1]
+        elif source.shape != target.shape:
             target[...] = source[...].astype(target.dtype).T
         else:
             target[...] = source[...]
@@ -2100,9 +2223,9 @@
     ]
     shapes = [jax.ShapeDtypeStruct(array.shape, array.dtype) for array in arrays]
     shapes[1] = jax.ShapeDtypeStruct(grad_tokens.shape[::-1], F32)
+    shapes[-1] = jax.ShapeDtypeStruct((1, 8), F32)
     arrays = results(arrays, shapes)
-    outputs = [array[0] if array.shape[0] == 1 else array for array in arrays]
-    return (*outputs[:-1], outputs[-1][:, 0])
+    return tuple(array[0] if array.shape[0] == 1 else array for array in arrays)
 
 
 def solution(mesh):

time: 534 us -> 520 us (0.974); the launches traced: 527 us -> 519 us
  Pallas kernels: 521 us -> 515 us
    pallas_call x8, Pallas kernels: 517 us -> 511 us  [comm_call(): pl.pallas_call(kernel, name=name, out_shape=tuple(out_shapes), in_specs=i...]
where the time goes in v3:
time: 520 us; the launch traced here: 519 us
  Pallas kernels  515 us (99%)
    pallas_call x8, Pallas kernels, comm_call(): pl.pallas_call(kernel, name=name, out_shape=tuple(out_shapes), in_specs=i...  511 us

profile of v3, /device:TPU:0, one launch (start us, length us, event | category | flops | bytes accessed | tf_op | source)
XLA Modules:
  0.0 519.3 jit_solution(14021436765806360371)
XLA Ops:
  0.7 0.0 copy-start
  1.3 0.0 copy-done
  1.4 0.3 convolution_convert_fusion
  1.7 0.8 copy.46.refs_4_.refs_5_
  2.4 80.3 %first.1 = (f32[256,1024]{1,0:T(8,128)}, f32[256,1024]{1,0:T(8,128)}, f32[8,1024]{1,0:T(8,128)}, bf16[1024,1024]{1,0:T(8,128)(2,1)}, bf16[1024,1024]{1,0:T(8,128...) custom-call(s32[1]{0:T(128)S(6)} %copy.49.refs_0_.refs_7_, ...), custom_call_target="tpu_custom_call" | custom-call | flops 1000000000 | bytes 100000000 | tf_op jit(solution)/shard_map/first/pallas_call | solution.py:741
  82.7 51.7 %attend.1 = (f32[256,1024]{1,0:T(8,128)}, f32[16,1024]{1,0:T(8,128)}, bf16[1024,1024]{1,0:T(8,128)(2,1)}, bf16[1024,768]{1,0:T(8,128)(2,1)}, bf16[1024,256]{1,0:...) custom-call(s32[1]{0:T(128)S(6)} %copy.49.refs_0_.refs_7_, ...), custom_call_target="tpu_custom_call" | custom-call | flops 20000000000 | bytes 100000000 | tf_op jit(solution)/shard_map/attend/pallas_call | solution.py:741
  134.4 53.8 %convolve.1 = (f32[256,1024]{1,0:T(8,128)}, f32[16,1024]{1,0:T(8,128)}, bf16[1024,1024]{1,0:T(8,128)(2,1)}, bf16[1024,512]{1,0:T(8,128)(2,1)}, f32[1024,256]{1,0...) custom-call(s32[1]{0:T(128)S(6)} %copy.49.refs_0_.refs_7_, f32[256,1024]{1,0:T(8,128)} %get-tuple-element.113.refs_1_.refs_2_, ...), custom_call_target="tpu_custom_call" | custom-call | flops 15000000512 | bytes 100000000 | tf_op jit(solution)/shard_map/convolve/pallas_call | solution.py:741
  188.2 51.7 %second.1 = (f32[256,1024]{1,0:T(8,128)}, f32[8,1024]{1,0:T(8,128)}, bf16[1024,256]{1,0:T(8,128)(2,1)}, f32[16,1024]{1,0:T(8,128)}, bf16[1024,1024]{1,0:T(8,128)(2,1)}, /*index=5*/bf16[1024,1024]{1,0:T(8,128)(2,1)}) custom-call(s32[1]{0:T(128)S(6)} %copy.49.refs_0_.refs_7_, f32[256,1024]{1,0:T(8,128)} %get-tuple-element.115.refs_1_, ...), custom_call_target="tpu_custom_call" | custom-call | flops 1000000000 | bytes 100000000 | tf_op jit(solution)/shard_map/second/pallas_call | solution.py:741
  239.9 42.8 %second_back.1 = (f32[8,1024]{1,0:T(8,128)}, bf16[1024,1024]{1,0:T(8,128)(2,1)}, bf16[1024,1024]{1,0:T(8,128)(2,1)}, f32[256,1024]{1,0:T(8,128)}, bf16[256,1024]{1,0:T(8,128)(2,1)}) custom-call(f32[256,1024]{1,0:T(8,128)} %get-tuple-element.119.refs_0_, f32[256,1024]{1,0:T(8,128)} %get-tuple-element.115.refs_1_, ...), custom_call_target="tpu_custom_call" | custom-call | flops 1000000000 | bytes 100000000 | tf_op jit(solution)/shard_map/second_back/pallas_call | solution.py:741
  282.8 53.7 %convolve_back.1 = (f32[8,1024]{1,0:T(8,128)}, bf16[1024,768]{1,0:T(8,128)(2,1)}, f32[32,256]{1,0:T(8,128)}, f32[8,256]{1,0:T(8,128)}, f32[256,1024]{1,0:T(8,128)}, /*index=5*/f32[128,1024]{1,0:T(8,128)}) custom-call(s32[1]{0:T(128)S(6)} %copy.49.refs_0_.refs_7_, f32[256,1024]{1,0:T(8,128)} %get-tuple-element.124.refs_1_, ...), custom_call_target="tpu_custom_call" | custom-call | flops 20000000000 | bytes 100000000 | tf_op jit(solution)/shard_map/convolve_back/pallas_call | solution.py:741
  336.4 83.4 %attend_back.1 = (f32[8,1024]{1,0:T(8,128)}, bf16[1024,1024]{1,0:T(8,128)(2,1)}, f32[80,128]{1,0:T(8,128)}, f32[256,1024]{1,0:T(8,128)}, f32[1024,128]{1,0:T(8,1...) custom-call(s32[1]{0:T(128)S(6)} %copy.49.refs_0_.refs_7_, ...), custom_call_target="tpu_custom_call" | custom-call | flops 49999998976 | bytes 100000000 | tf_op jit(solution)/shard_map/attend_back/pallas_call | solution.py:741
  419.8 93.4 %first_back.1 = (f32[1,256]{1,0:T(1,128)}, f32[1,256]{1,0:T(1,128)}, f32[1,256]{1,0:T(1,128)}, f32[1,256]{1,0:T(1,128)}, f32[1,256]{1,0:T(1,128)}, /*index=5*/f3...) custom-call(f32[256,1024]{1,0:T(8,128)} %get-tuple-element.137.refs_, ...), custom_call_target="tpu_custom_call" | custom-call | flops 1000000000 | bytes 100000000 | tf_op jit(solution)/shard_map/first_back/pallas_call | solution.py:741
  513.3 4.6 results.1
  517.9 1.5 copy.48
  (2 shorter events, 0.0 us)
Async XLA Ops:
  0.7 0.7 copy-start

commit v4 on v3

--- a/solution.py
+++ b/solution.py
@@ -209,10 +209,17 @@
         if self.wire.n != 4:
             return
         for turn in range(2):
-            self.across[turn].wait_recv()
-            self.onward[turn].start()
-            self.along[2 + turn].wait_recv()
-            self.onward[2 + turn].start()
+            self.relay_turn(turn)
+
+    def relay_turn(self, turn):
+        self.across[turn].wait_recv()
+        self.onward[turn].start()
+        self.along[2 + turn].wait_recv()
+        self.onward[2 + turn].start()
+
+    def wait_place(self, place):
+        for copy in (self.across[2:], self.along[:2], self.onward)[place - 1]:
+            copy.wait_recv()
 
     def arrivals(self, relay=True):
         wire = self.wire
@@ -224,11 +231,8 @@
             return
         if relay:
             self.relay()
-        for (peer, slot), copies in zip(
-            wire.peers(), (self.across[2:], self.along[:2], self.onward)
-        ):
-            for copy in copies:
-                copy.wait_recv()
+        for place, (peer, slot) in enumerate(wire.peers()):
+            self.wait_place(place + 1)
             yield peer, slot
 
     def finish(self):
@@ -823,19 +827,21 @@
     return copies + [here]
 
 
+def flipped(wire, place):
+    flip_across, flip_along = lax.rem(place, 2), place // 2
+    across_bit, along_bit = lax.rem(wire.me, 2), wire.me // 2
+    return (
+        across_bit + flip_across - 2 * across_bit * flip_across
+        + 2 * (along_bit + flip_along - 2 * along_bit * flip_along)
+    )
+
+
 def send_shares(wire, chunks, collect, share, last=None):
     part = collect.part
     if wire.n == 4:
-        across_bit, along_bit = lax.rem(wire.me, 2), wire.me // 2
-
         def turn(step, carry):
             left = 3 - step
-            flip_across, flip_along = lax.rem(left, 2), left // 2
-            chunk = (
-                across_bit + flip_across - 2 * across_bit * flip_across
-                + 2 * (along_bit + flip_along - 2 * along_bit * flip_along)
-            )
-            share(chunk, part.at[lax.rem(left + 3, 4)])
+            share(flipped(wire, left), part.at[lax.rem(left + 3, 4)])
             for place in range(3):
                 pl.when(step == place)(lambda place=place: collect.send(2 - place))
             if last is not None:
@@ -1489,7 +1495,7 @@
 
 def attend_back_core(width, group, qkv_ref, table_ref, far_ref, log_ref, grad_ref, out_ref,
                      table_grad_ref, keys, values, key_grad, value_grad, slot_grad, end_grad, probs,
-                     prob_grads, back):
+                     prob_grads, back, blocks_in_turn):
     length = qkv_ref.shape[0]
     heads = group // HEAD_DIM
     parts = width // group
@@ -1512,8 +1518,7 @@
             axis=0,
         )
 
-    def block(step, carry):
-        index, part = step // parts, lax.rem(step, parts)
+    def block(index, part):
         at = pl.multiple_of(index * BLOCK, BLOCK)
         rows = pl.ds(at, BLOCK)
         cols = tile(part, group) if parts > 1 else slice(0, group)
@@ -1590,9 +1595,8 @@
             )
         out_ref[rows, cols] = (result * scale).astype(BF16)
         slot_grad[...] += matmul_tn(flip(query).astype(BF16), straight)
-        return carry
-
-    lax.fori_loop(0, length // BLOCK * parts, block, 0)
+
+    blocks_in_turn(block, parts)
     for part in range(parts):
         base = width + part * group
         out_ref[:, base:base + group] = (
@@ -1707,18 +1711,53 @@
     spread.start()
     wire.loaded()
     collect = Collect(wire, part, got)
-    spread.relay()
-    wire.early()
     fill_far(far_ref, table_ref, limit_ref[0])
     chunks = []
-    for chunk, slot in spread.arrivals(relay=False):
-        chunks.append((chunk, slot))
+    per_chunk = max(count, BLOCK) // BLOCK
+
+    def down_gradient(chunk):
         rows = tile(chunk, count)
         context_grad[rows] = matmul(grads[rows], weights[:, 3 * width:]).astype(BF16)
-    wire.middle()
+
+    def in_turn(block, parts):
+        if wire.n == 4:
+            def turn(place, carry):
+                pl.when(place == 1)(wire.early)
+                for at in (1, 2, 3):
+                    pl.when(place == at)(lambda at=at: spread.wait_place(at))
+                chunk = flipped(wire, place)
+                down_gradient(chunk)
+
+                def one(step, carry):
+                    block(chunk * per_chunk + step // parts, lax.rem(step, parts))
+                    final = per_chunk * parts - 1
+                    for turn_of, after in ((0, min(1, final)), (1, final)):
+                        pl.when((place == 0) & (step == after))(
+                            lambda turn_of=turn_of: spread.relay_turn(turn_of)
+                        )
+                    return carry
+
+                lax.fori_loop(0, per_chunk * parts, one, 0)
+                return carry
+
+            lax.fori_loop(0, 4, turn, 0)
+            return
+        wire.early()
+        for chunk, slot in spread.arrivals():
+            chunks.append((chunk, slot))
+            down_gradient(chunk)
+
+        def one(step, carry):
+            block(step // parts, lax.rem(step, parts))
+            return carry
+
+        lax.fori_loop(0, wire.n * count // BLOCK * parts, one, 0)
+
     attend_back_core(width, group, qkv_ref, table_ref, far_ref, log_ref, context_grad, qkv_grad,
                      table_grad_ref, keys, values, key_grad, value_grad, slot_grad, end_grad, probs,
-                     prob_grads, back)
+                     prob_grads, back, in_turn)
+    wire.middle()
+
     def share(chunk, target):
         left = qkv_grad[tile(chunk, count)]
 
@@ -1976,13 +2015,6 @@
 
     token_blocks(length, regate)
     wire.early()
-    chunks = []
-    for chunk, slot in spread.arrivals(relay=False):
-        chunks.append((chunk, slot))
-        rows = tile(chunk, count)
-        padded_grad[rows] = matmul(grads[rows], weights[:, 2 * width:])
-    wire.middle()
-
     def first(rows, index):
         mean, scale = stat_columns(stats_ref[:, rows])
         normed = (mixed_ref[rows] - mean) * scale
@@ -1996,7 +2028,20 @@
         stat_rows(rows, jnp.sum(weighted, axis=1, keepdims=True),
                   jnp.sum(weighted * normed, axis=1, keepdims=True), stats_mine)
 
-    token_blocks(length, first)
+    chunks = []
+    for chunk, slot in spread.arrivals(relay=False):
+        chunks.append((chunk, slot))
+        rows = tile(chunk, count)
+        padded_grad[rows] = matmul(grads[rows], weights[:, 2 * width:])
+        if count % BLOCK == 0:
+            def some(index, carry):
+                first(tile(chunk * (count // BLOCK) + index, BLOCK), index)
+                return carry
+
+            lax.fori_loop(0, count // BLOCK, some, 0)
+    wire.middle()
+    if count % BLOCK:
+        token_blocks(length, first)
     total = stats.total() * (1.0 / full)
     stats_mine[...] = total
 

time: 520 us -> 507 us (0.975)
  Pallas kernels: 515 us -> 503 us
    pallas_call x8, Pallas kernels: 511 us -> 498 us  [comm_call(): pl.pallas_call(kernel, name=name, out_shape=tuple(out_shapes), in_specs=i...]
where the time goes in v4:
time: 507 us
  Pallas kernels  503 us (99%)
    pallas_call x8, Pallas kernels, comm_call(): pl.pallas_call(kernel, name=name, out_shape=tuple(out_shapes), in_specs=i...  498 us

profile of v4, /device:TPU:0, one launch (start us, length us, event | category | flops | bytes accessed | tf_op | source)
XLA Modules:
  0.0 506.8 jit_solution(3319460733429242439)
XLA Ops:
  0.7 0.0 copy-start
  1.3 0.0 copy-done
  1.4 0.3 convolution_convert_fusion
  1.7 0.8 copy.46.refs_4_.refs_5_
  2.4 80.3 %first.1 = (f32[256,1024]{1,0:T(8,128)}, f32[256,1024]{1,0:T(8,128)}, f32[8,1024]{1,0:T(8,128)}, bf16[1024,1024]{1,0:T(8,128)(2,1)}, bf16[1024,1024]{1,0:T(8,128...) custom-call(s32[1]{0:T(128)S(6)} %copy.49.refs_0_.refs_7_, ...), custom_call_target="tpu_custom_call" | custom-call | flops 1000000000 | bytes 100000000 | tf_op jit(solution)/shard_map/first/pallas_call | solution.py:745
  82.7 51.7 %attend.1 = (f32[256,1024]{1,0:T(8,128)}, f32[16,1024]{1,0:T(8,128)}, bf16[1024,1024]{1,0:T(8,128)(2,1)}, bf16[1024,768]{1,0:T(8,128)(2,1)}, bf16[1024,256]{1,0:...) custom-call(s32[1]{0:T(128)S(6)} %copy.49.refs_0_.refs_7_, ...), custom_call_target="tpu_custom_call" | custom-call | flops 20000000000 | bytes 100000000 | tf_op jit(solution)/shard_map/attend/pallas_call | solution.py:745
  134.4 53.8 %convolve.1 = (f32[256,1024]{1,0:T(8,128)}, f32[16,1024]{1,0:T(8,128)}, bf16[1024,1024]{1,0:T(8,128)(2,1)}, bf16[1024,512]{1,0:T(8,128)(2,1)}, f32[1024,256]{1,0...) custom-call(s32[1]{0:T(128)S(6)} %copy.49.refs_0_.refs_7_, f32[256,1024]{1,0:T(8,128)} %get-tuple-element.113.refs_1_.refs_2_, ...), custom_call_target="tpu_custom_call" | custom-call | flops 15000000512 | bytes 100000000 | tf_op jit(solution)/shard_map/convolve/pallas_call | solution.py:745
  188.2 51.7 %second.1 = (f32[256,1024]{1,0:T(8,128)}, f32[8,1024]{1,0:T(8,128)}, bf16[1024,256]{1,0:T(8,128)(2,1)}, f32[16,1024]{1,0:T(8,128)}, bf16[1024,1024]{1,0:T(8,128)(2,1)}, /*index=5*/bf16[1024,1024]{1,0:T(8,128)(2,1)}) custom-call(s32[1]{0:T(128)S(6)} %copy.49.refs_0_.refs_7_, f32[256,1024]{1,0:T(8,128)} %get-tuple-element.115.refs_1_, ...), custom_call_target="tpu_custom_call" | custom-call | flops 1000000000 | bytes 100000000 | tf_op jit(solution)/shard_map/second/pallas_call | solution.py:745
  239.9 42.8 %second_back.1 = (f32[8,1024]{1,0:T(8,128)}, bf16[1024,1024]{1,0:T(8,128)(2,1)}, bf16[1024,1024]{1,0:T(8,128)(2,1)}, f32[256,1024]{1,0:T(8,128)}, bf16[256,1024]{1,0:T(8,128)(2,1)}) custom-call(f32[256,1024]{1,0:T(8,128)} %get-tuple-element.119.refs_0_, f32[256,1024]{1,0:T(8,128)} %get-tuple-element.115.refs_1_, ...), custom_call_target="tpu_custom_call" | custom-call | flops 1000000000 | bytes 100000000 | tf_op jit(solution)/shard_map/second_back/pallas_call | solution.py:745
  282.8 53.1 %convolve_back.1 = (f32[8,1024]{1,0:T(8,128)}, bf16[1024,768]{1,0:T(8,128)(2,1)}, f32[32,256]{1,0:T(8,128)}, f32[8,256]{1,0:T(8,128)}, f32[256,1024]{1,0:T(8,128)}, /*index=5*/f32[128,1024]{1,0:T(8,128)}) custom-call(s32[1]{0:T(128)S(6)} %copy.49.refs_0_.refs_7_, f32[256,1024]{1,0:T(8,128)} %get-tuple-element.124.refs_1_, ...), custom_call_target="tpu_custom_call" | custom-call | flops 20000000000 | bytes 100000000 | tf_op jit(solution)/shard_map/convolve_back/pallas_call | solution.py:745
  335.9 72.8 %attend_back.1 = (f32[8,1024]{1,0:T(8,128)}, bf16[1024,1024]{1,0:T(8,128)(2,1)}, f32[80,128]{1,0:T(8,128)}, f32[256,1024]{1,0:T(8,128)}, f32[1024,128]{1,0:T(8,1...) custom-call(s32[1]{0:T(128)S(6)} %copy.49.refs_0_.refs_7_, ...), custom_call_target="tpu_custom_call" | custom-call | flops 49999998976 | bytes 100000000 | tf_op jit(solution)/shard_map/attend_back/pallas_call | solution.py:745
  408.7 92.1 %first_back.1 = (f32[1,256]{1,0:T(1,128)}, f32[1,256]{1,0:T(1,128)}, f32[1,256]{1,0:T(1,128)}, f32[1,256]{1,0:T(1,128)}, f32[1,256]{1,0:T(1,128)}, /*index=5*/f3...) custom-call(f32[256,1024]{1,0:T(8,128)} %get-tuple-element.137.refs_, ...), custom_call_target="tpu_custom_call" | custom-call | flops 1000000000 | bytes 100000000 | tf_op jit(solution)/shard_map/first_back/pallas_call | solution.py:745
  500.7 4.6 results.1
  505.3 1.5 copy.48
  (2 shorter events, 0.0 us)
Async XLA Ops:
  0.7 0.7 copy-start

commit v5 on v4

--- a/solution.py
+++ b/solution.py
@@ -811,7 +811,7 @@
     collect.sum_loop(work)
 
 
-def send_pieces(wire, count, source, pieces, out_ref):
+def split_pieces(wire, count, source, pieces):
     width = pieces.shape[2]
 
     def split(rows, index):
@@ -820,6 +820,10 @@
             pieces[part, rows] = result[:, part * width:(part + 1) * width]
 
     row_loop(count, split)
+
+
+def send_pieces(wire, count, source, pieces, out_ref):
+    split_pieces(wire, count, source, pieces)
     mine = out_ref.at[tile(wire.me, count)]
     copies = wire.to_all(lambda peer: pieces.at[peer], mine)
     here = wire.local(pieces.at[wire.me], mine)
@@ -955,15 +959,11 @@
     spread.start()
     wire.loaded()
     collect = Collect(wire, part, got)
-    cot_copies = []
-    if enter:
-        cot_copies = wire.to_all(
-            lambda peer: share(cot_in, peer), arrived_cot.at[wire.me]
-        )
     wire.early()
     if enter:
         up_job.advance(0)
         spread.relay()
+        cot_copies = wire.to_all(lambda peer: share(cot_in, peer), arrived_cot.at[wire.me])
         for step in range(1, up_job.steps):
             up_job.advance(step)
         down_job.begin()
@@ -1002,7 +1002,6 @@
     wire.flush()
     collect.wait()
     residual(collect, factor, resid, limit_ref[0], after_ref, squares_ref)
-    late = []
     if turn:
         final_gains = gains_ref[gain_row + 1:gain_row + 2]
         gain_grad_ref[...] = jnp.zeros_like(gain_grad_ref)
@@ -1015,10 +1014,9 @@
             after_ref[rows] = normed * final_gains
 
         row_loop(count, final)
-        late = send_pieces(wire, count, after_ref, pieces, out_ref)
+        split_pieces(wire, count, after_ref, pieces)
+        wire.store([wire.local(pieces, out_ref)])
     spread.finish()
-    for copy in late:
-        copy.wait()
     if enter:
         next_job.end()
     wire.end()
@@ -1062,7 +1060,7 @@
         outs += [
             ((count, full), F32, vmem()),
             ((8, full), F32, vmem()),
-            ((n * count, full // n), BF16, hbm()),
+            ((n, count, full // n), BF16, hbm()),
         ]
         scratch.append(pltpu.VMEM((n, count, full // n), BF16))
     if turn is None:
@@ -1130,8 +1128,7 @@
         ]
         gain_item = SumItem("piece", first_pieces, *take(4), wire)
     else:
-        (tokens_ref,) = ins
-        gain_grad_ref, up_grad_ref, down_grad_ref, last_ref, turned_ref = outs
+        gain_grad_ref, up_grad_ref, down_grad_ref, last_ref = outs
         new_grad_ref = last_ref
         items = []
         down_job = up_job = None
@@ -1209,23 +1206,30 @@
 
     late_leg = None
     for place, (chunk, slot) in enumerate(spread.arrivals()):
-        first_leg(chunk)
         if leave and place == wire.n - 1:
             late_leg = (chunk, slot)
         else:
+            first_leg(chunk)
             second_leg(chunk, slot)
+        if leave and place == wire.n - 2:
+            rows = tile(wire.peers()[-1][0], count)
+
+            def activate(cols, index):
+                pre = pre_ref[rows, cols].astype(F32)
+                act[rows, cols] = (pre * jax.nn.sigmoid(pre)).astype(BF16)
+
+            block_loop(hidden, activate)
         if slot is None:
             wire.early()
             for item in items:
                 item.early()
-            if not leave:
-                turned_ref[...] = tokens_ref[...].T
         elif slot == 0:
             for item in items:
                 item.middle()
     wire.middle()
     weight_grad(grads, act, down_grad_ref, down_job)
     if leave:
+        first_leg(late_leg[0])
         second_leg(*late_leg)
         weight_grad(rows_ref, pre_grad, up_grad_ref, up_job)
         collect.combine()
@@ -1268,7 +1272,7 @@
 
 
 def feed_forward_back(sizes, name, collective_id, gain_row, grad, resid, gains, up, down_t, rows, pre,
-                      leave=None, tokens=None, taps=0, **side):
+                      leave=None, taps=0, **side):
     n, m = sizes
     full, hidden = up.shape
     count = resid.shape[0]
@@ -1318,13 +1322,11 @@
             scratch += sum_scratch(n, layers, shape)
         side = dict(side, more_slots=16 * m + 8 * n, row_on=True)
     else:
-        ins.append((tokens, "load"))
         outs = [
             ((8, full), F32, vmem()),
             ((full, hidden), BF16, "store"),
             ((full, hidden), BF16, "store"),
             ((count, full), F32, vmem()),
-            ((tokens.shape[1], tokens.shape[0]), BF16, "store"),
         ]
     return comm_call(
         name, collective_id, sizes,
@@ -1698,10 +1700,10 @@
 
 def attention_back_main(count, gain_row, wire, ins, outs, scratch):
     (limit_ref, grad_ref, resid, gains_ref, weights, table_ref, rows_ref, qkv_ref, context_ref,
-     log_ref) = ins
-    gain_grad_ref, wide_ref, table_grad_ref, new_grad_ref = outs
+     log_ref, pieces) = ins
+    gain_grad_ref, wide_ref, table_grad_ref, new_grad_ref, result_ref = outs
     (far_ref, grads, context_grad, qkv_grad, keys, values, key_grad, value_grad, slot_grad, end_grad,
-     probs, prob_grads, back, part, got) = scratch
+     probs, prob_grads, back, part, got, came) = scratch
     width = context_ref.shape[1]
     group = keys.shape[2]
     wire.greet()
@@ -1715,6 +1717,18 @@
     chunks = []
     per_chunk = max(count, BLOCK) // BLOCK
 
+    mine = came.at[tile(wire.me, count)]
+    output_copies = [
+        wire.remote(pieces.at[lax.rem(wire.me + step, wire.n)], mine, "col",
+                    lax.rem(wire.me + step, wire.n))
+        for step in range(1, wire.n)
+    ]
+    output_copies.append(wire.local(pieces.at[wire.me], mine))
+
+    def send_output():
+        for copy in output_copies:
+            copy.start()
+
     def down_gradient(chunk):
         rows = tile(chunk, count)
         context_grad[rows] = matmul(grads[rows], weights[:, 3 * width:]).astype(BF16)
@@ -1725,6 +1739,7 @@
                 pl.when(place == 1)(wire.early)
                 for at in (1, 2, 3):
                     pl.when(place == at)(lambda at=at: spread.wait_place(at))
+                pl.when(place == 3)(send_output)
                 chunk = flipped(wire, place)
                 down_gradient(chunk)
 
@@ -1746,6 +1761,7 @@
         for chunk, slot in spread.arrivals():
             chunks.append((chunk, slot))
             down_gradient(chunk)
+        send_output()
 
         def one(step, carry):
             block(step // parts, lax.rem(step, parts))
@@ -1768,6 +1784,9 @@
 
     send_shares(wire, chunks, collect, share)
     collect.combine()
+    for copy in output_copies:
+        copy.wait()
+    result_ref[...] = came[...].T
 
     def weight_grads(rows, index):
         wide_ref[rows, :3 * width] = matmul_tn(rows_ref[:, rows], qkv_grad[...]).astype(BF16)
@@ -1783,7 +1802,7 @@
 
 
 def attention_back(sizes, name, collective_id, gain_row, limit, grad, resid, gains, weights, table, rows,
-                   qkv, context, log_total, **side):
+                   qkv, context, log_total, pieces, **side):
     n, m = sizes
     count, full = resid.shape
     length, width = context.shape
@@ -1791,12 +1810,13 @@
     return comm_call(
         name, collective_id, sizes, functools.partial(attention_back_main, count, gain_row),
         [(limit, smem()), (grad, vmem()), (resid, "load"), (gains, vmem())]
-        + [(item, "load") for item in (weights, table, rows, qkv, context, log_total)],
+        + [(item, "load") for item in (weights, table, rows, qkv, context, log_total, pieces)],
         [
             ((8, full), F32, vmem()),
             ((full, 4 * width), BF16, "store"),
             ((LEFT + RIGHT + 8, group), F32, vmem()),
             ((count, full), F32, vmem()),
+            ((width, length), BF16, "store"),
         ],
         [
             pltpu.VMEM((length // BLOCK, length, BLOCK), BF16),
@@ -1814,6 +1834,7 @@
             pltpu.VMEM((group // HEAD_DIM * BLOCK, length), BF16),
             pltpu.VMEM((n, count, full), BF16),
             pltpu.VMEM((n - 1, count, full), BF16),
+            pltpu.VMEM((length, width), BF16),
         ],
         cost=50 * 10**9, **side,
     )
@@ -2230,19 +2251,19 @@
         sizes, "second", 4, 3, up_second, down_second, limit, resid=after_conv, gains=gains, turn=cot
     )
 
-    second_part, second_up_wide, second_down_wide, grad_conv, layer_output = feed_forward_back(
+    second_part, second_up_wide, second_down_wide, grad_conv = feed_forward_back(
         sizes, "second_back", 5, 3, grad_second, after_conv, gains, up_second, down_second,
-        rows_second, pre_second, tokens=out_tokens,
+        rows_second, pre_second,
     )
     conv_part, conv_wide, kernel_part, depth_part, grad_attend, second_up_grad = convolution_back(
         sizes, "convolve_back", 6, 2, limit, grad_conv, after_attend, gains, conv_weights,
         depthwise_kernel, depth_row, rows_conv, conv_pre, mixed, stats,
         reduces=[(second_up_wide, [(hidden, False)])],
     )
-    (attend_part, attend_wide, table_part, grad_first, second_down_grad, value_grad, gate_grad,
+    (attend_part, attend_wide, table_part, grad_first, layer_output, second_down_grad, value_grad, gate_grad,
      out_grad) = attention_back(
         sizes, "attend_back", 7, 1, limit, grad_attend, after_first, gains, attend_weights,
-        table_wide, rows_attend, qkv, context, log_total,
+        table_wide, rows_attend, qkv, context, log_total, out_tokens,
         reduces=[
             (second_down_wide, [(hidden, True)]),
             (conv_wide, [(width, False), (width, False), (width, True)]),

time: 507 us -> 500 us (0.986)
  Pallas kernels: 503 us -> 495 us
    pallas_call x8, Pallas kernels: 498 us -> 491 us  [comm_call(): pl.pallas_call(kernel, name=name, out_shape=tuple(out_shapes), in_specs=i...]
where the time goes in v5:
time: 500 us; the launch traced here: 499 us
  Pallas kernels  495 us (99%)
    pallas_call x8, Pallas kernels, comm_call(): pl.pallas_call(kernel, name=name, out_shape=tuple(out_shapes), in_specs=i...  491 us

profile of v5, /device:TPU:0, one launch (start us, length us, event | category | flops | bytes accessed | tf_op | source)
XLA Modules:
  0.0 499.4 jit_solution(12042007772311558216)
XLA Ops:
  0.7 0.0 copy-start
  1.3 0.0 copy-done
  1.4 0.3 convolution_convert_fusion
  1.7 0.8 copy.46.refs_4_.refs_5_
  2.4 80.8 %first.1 = (f32[256,1024]{1,0:T(8,128)}, f32[256,1024]{1,0:T(8,128)}, f32[8,1024]{1,0:T(8,128)}, bf16[1024,1024]{1,0:T(8,128)(2,1)}, bf16[1024,1024]{1,0:T(8,128...) custom-call(s32[1]{0:T(128)S(6)} %copy.49.refs_0_.refs_7_, ...), custom_call_target="tpu_custom_call" | custom-call | flops 1000000000 | bytes 100000000 | tf_op jit(solution)/shard_map/first/pallas_call | solution.py:745
  83.3 52.5 %attend.1 = (f32[256,1024]{1,0:T(8,128)}, f32[16,1024]{1,0:T(8,128)}, bf16[1024,1024]{1,0:T(8,128)(2,1)}, bf16[1024,768]{1,0:T(8,128)(2,1)}, bf16[1024,256]{1,0:...) custom-call(s32[1]{0:T(128)S(6)} %copy.49.refs_0_.refs_7_, ...), custom_call_target="tpu_custom_call" | custom-call | flops 20000000000 | bytes 100000000 | tf_op jit(solution)/shard_map/attend/pallas_call | solution.py:745
  135.8 52.0 %convolve.1 = (f32[256,1024]{1,0:T(8,128)}, f32[16,1024]{1,0:T(8,128)}, bf16[1024,1024]{1,0:T(8,128)(2,1)}, bf16[1024,512]{1,0:T(8,128)(2,1)}, f32[1024,256]{1,0...) custom-call(s32[1]{0:T(128)S(6)} %copy.49.refs_0_.refs_7_, f32[256,1024]{1,0:T(8,128)} %get-tuple-element.113.refs_1_.refs_2_, ...), custom_call_target="tpu_custom_call" | custom-call | flops 15000000512 | bytes 100000000 | tf_op jit(solution)/shard_map/convolve/pallas_call | solution.py:745
  187.8 45.7 %second.1 = (f32[256,1024]{1,0:T(8,128)}, f32[8,1024]{1,0:T(8,128)}, bf16[4,256,256]{2,1,0:T(8,128)(2,1)}, f32[16,1024]{1,0:T(8,128)}, bf16[1024,1024]{1,0:T(8,128)(2,1)}, /*index=5*/bf16[1024,1024]{1,0:T(8,128)(2,1)}) custom-call(s32[1]{0:T(128)S(6)} %copy.49.refs_0_.refs_7_, f32[256,1024]{1,0:T(8,128)} %get-tuple-element.115.refs_1_, ...), custom_call_target="tpu_custom_call" | custom-call | flops 1000000000 | bytes 100000000 | tf_op jit(solution)/shard_map/second/pallas_call | solution.py:745
  233.5 43.5 %second_back.1 = (f32[8,1024]{1,0:T(8,128)}, bf16[1024,1024]{1,0:T(8,128)(2,1)}, bf16[1024,1024]{1,0:T(8,128)(2,1)}, f32[256,1024]{1,0:T(8,128)}) custom-call(f32[256,1024]{1,0:T(8,128)} %get-tuple-element.119.refs_0_, f32[256,1024]{1,0:T(8,128)} %get-tuple-element.115.refs_1_, f32[8,1024]{1,0:T(8,128)} %get-tuple-element.111.refs_2_.refs_3_, ...), custom_call_target="tpu_custom_call" | custom-call | flops 1000000000 | bytes 100000000 | tf_op jit(solution)/shard_map/second_back/pallas_call | solution.py:745
  277.0 51.1 %convolve_back.1 = (f32[8,1024]{1,0:T(8,128)}, bf16[1024,768]{1,0:T(8,128)(2,1)}, f32[32,256]{1,0:T(8,128)}, f32[8,256]{1,0:T(8,128)}, f32[256,1024]{1,0:T(8,128)}, /*index=5*/f32[128,1024]{1,0:T(8,128)}) custom-call(s32[1]{0:T(128)S(6)} %copy.49.refs_0_.refs_7_, f32[256,1024]{1,0:T(8,128)} %get-tuple-element.122.refs_1_, ...), custom_call_target="tpu_custom_call" | custom-call | flops 20000000000 | bytes 100000000 | tf_op jit(solution)/shard_map/convolve_back/pallas_call | solution.py:745
  328.2 72.9 %attend_back.1 = (f32[8,1024]{1,0:T(8,128)}, bf16[1024,1024]{1,0:T(8,128)(2,1)}, f32[80,128]{1,0:T(8,128)}, f32[256,1024]{1,0:T(8,128)}, bf16[256,1024]{1,0:T(8,...) custom-call(s32[1]{0:T(128)S(6)} %copy.49.refs_0_.refs_7_, ...), custom_call_target="tpu_custom_call" | custom-call | flops 49999998976 | bytes 100000000 | tf_op jit(solution)/shard_map/attend_back/pallas_call | solution.py:745
  401.1 92.3 %first_back.1 = (f32[1,256]{1,0:T(1,128)}, f32[1,256]{1,0:T(1,128)}, f32[1,256]{1,0:T(1,128)}, f32[1,256]{1,0:T(1,128)}, f32[1,256]{1,0:T(1,128)}, /*index=5*/f3...) custom-call(f32[256,1024]{1,0:T(8,128)} %get-tuple-element.137.refs_, ...), custom_call_target="tpu_custom_call" | custom-call | flops 1000000000 | bytes 100000000 | tf_op jit(solution)/shard_map/first_back/pallas_call | solution.py:745
  493.4 4.6 results.1
  498.0 1.5 copy.48
  (2 shorter events, 0.0 us)
Async XLA Ops:
  0.7 0.7 copy-start

commit v6 on v5

--- a/solution.py
+++ b/solution.py
@@ -985,10 +985,11 @@
             feed_forward_second(act.at[place], down_t, target)
             if slot is not None:
                 collect.send(slot)
-            if len(chunks) - 1 - place < next_job.steps:
-                next_job.advance(len(chunks) - 1 - place)
+            if len(chunks) - 1 - place == 2:
+                next_job.advance(0)
+        next_job.advance(1)
         collect.combine()
-        for step in range(len(chunks), next_job.steps):
+        for step in range(2, next_job.steps):
             next_job.advance(step)
     else:
         for chunk, slot in spread.arrivals():

time: 500 us -> 498 us (level)
  no operation moved by 1% of the time
where the time goes in v6:
time: 498 us
  Pallas kernels  494 us (99%)
    pallas_call x8, Pallas kernels, comm_call(): pl.pallas_call(kernel, name=name, out_shape=tuple(out_shapes), in_specs=i...  489 us

profile of v6, /device:TPU:0, one launch (start us, length us, event | category | flops | bytes accessed | tf_op | source)
XLA Modules:
  0.0 498.0 jit_solution(10824218630014062431)
XLA Ops:
  0.7 0.0 copy-start
  1.3 0.0 copy-done
  1.4 0.3 convolution_convert_fusion
  1.7 0.8 copy.46.refs_4_.refs_5_
  2.4 76.7 %first.1 = (f32[256,1024]{1,0:T(8,128)}, f32[256,1024]{1,0:T(8,128)}, f32[8,1024]{1,0:T(8,128)}, bf16[1024,1024]{1,0:T(8,128)(2,1)}, bf16[1024,1024]{1,0:T(8,128...) custom-call(s32[1]{0:T(128)S(6)} %copy.49.refs_0_.refs_7_, ...), custom_call_target="tpu_custom_call" | custom-call | flops 1000000000 | bytes 100000000 | tf_op jit(solution)/shard_map/first/pallas_call | solution.py:745
  79.2 53.5 %attend.1 = (f32[256,1024]{1,0:T(8,128)}, f32[16,1024]{1,0:T(8,128)}, bf16[1024,1024]{1,0:T(8,128)(2,1)}, bf16[1024,768]{1,0:T(8,128)(2,1)}, bf16[1024,256]{1,0:...) custom-call(s32[1]{0:T(128)S(6)} %copy.49.refs_0_.refs_7_, ...), custom_call_target="tpu_custom_call" | custom-call | flops 20000000000 | bytes 100000000 | tf_op jit(solution)/shard_map/attend/pallas_call | solution.py:745
  132.7 57.6 %convolve.1 = (f32[256,1024]{1,0:T(8,128)}, f32[16,1024]{1,0:T(8,128)}, bf16[1024,1024]{1,0:T(8,128)(2,1)}, bf16[1024,512]{1,0:T(8,128)(2,1)}, f32[1024,256]{1,0...) custom-call(s32[1]{0:T(128)S(6)} %copy.49.refs_0_.refs_7_, f32[256,1024]{1,0:T(8,128)} %get-tuple-element.113.refs_1_.refs_2_, ...), custom_call_target="tpu_custom_call" | custom-call | flops 15000000512 | bytes 100000000 | tf_op jit(solution)/shard_map/convolve/pallas_call | solution.py:745
  190.3 45.4 %second.1 = (f32[256,1024]{1,0:T(8,128)}, f32[8,1024]{1,0:T(8,128)}, bf16[4,256,256]{2,1,0:T(8,128)(2,1)}, f32[16,1024]{1,0:T(8,128)}, bf16[1024,1024]{1,0:T(8,128)(2,1)}, /*index=5*/bf16[1024,1024]{1,0:T(8,128)(2,1)}) custom-call(s32[1]{0:T(128)S(6)} %copy.49.refs_0_.refs_7_, f32[256,1024]{1,0:T(8,128)} %get-tuple-element.115.refs_1_, ...), custom_call_target="tpu_custom_call" | custom-call | flops 1000000000 | bytes 100000000 | tf_op jit(solution)/shard_map/second/pallas_call | solution.py:745
  235.8 43.2 %second_back.1 = (f32[8,1024]{1,0:T(8,128)}, bf16[1024,1024]{1,0:T(8,128)(2,1)}, bf16[1024,1024]{1,0:T(8,128)(2,1)}, f32[256,1024]{1,0:T(8,128)}) custom-call(f32[256,1024]{1,0:T(8,128)} %get-tuple-element.119.refs_0_, f32[256,1024]{1,0:T(8,128)} %get-tuple-element.115.refs_1_, f32[8,1024]{1,0:T(8,128)} %get-tuple-element.111.refs_2_.refs_3_, ...), custom_call_target="tpu_custom_call" | custom-call | flops 1000000000 | bytes 100000000 | tf_op jit(solution)/shard_map/second_back/pallas_call | solution.py:745
  279.0 50.2 %convolve_back.1 = (f32[8,1024]{1,0:T(8,128)}, bf16[1024,768]{1,0:T(8,128)(2,1)}, f32[32,256]{1,0:T(8,128)}, f32[8,256]{1,0:T(8,128)}, f32[256,1024]{1,0:T(8,128)}, /*index=5*/f32[128,1024]{1,0:T(8,128)}) custom-call(s32[1]{0:T(128)S(6)} %copy.49.refs_0_.refs_7_, f32[256,1024]{1,0:T(8,128)} %get-tuple-element.122.refs_1_, ...), custom_call_target="tpu_custom_call" | custom-call | flops 20000000000 | bytes 100000000 | tf_op jit(solution)/shard_map/convolve_back/pallas_call | solution.py:745
  329.2 69.7 %attend_back.1 = (f32[8,1024]{1,0:T(8,128)}, bf16[1024,1024]{1,0:T(8,128)(2,1)}, f32[80,128]{1,0:T(8,128)}, f32[256,1024]{1,0:T(8,128)}, bf16[256,1024]{1,0:T(8,...) custom-call(s32[1]{0:T(128)S(6)} %copy.49.refs_0_.refs_7_, ...), custom_call_target="tpu_custom_call" | custom-call | flops 49999998976 | bytes 100000000 | tf_op jit(solution)/shard_map/attend_back/pallas_call | solution.py:745
  398.9 93.1 %first_back.1 = (f32[1,256]{1,0:T(1,128)}, f32[1,256]{1,0:T(1,128)}, f32[1,256]{1,0:T(1,128)}, f32[1,256]{1,0:T(1,128)}, f32[1,256]{1,0:T(1,128)}, /*index=5*/f3...) custom-call(f32[256,1024]{1,0:T(8,128)} %get-tuple-element.137.refs_, ...), custom_call_target="tpu_custom_call" | custom-call | flops 1000000000 | bytes 100000000 | tf_op jit(solution)/shard_map/first_back/pallas_call | solution.py:745
  492.0 4.6 results.1
  496.6 1.5 copy.48
  (2 shorter events, 0.0 us)
Async XLA Ops:
  0.7 0.7 copy-start
